TPU v7x, 512 devices: a whole 4x4x16 slice. The times are simulated.
512 devices in a mesh: section: 2 (over x_hi), lat: 64 (over z, x_lo, core), tp: 4 (over y).
Axes of the slice: x: 4 (x_hi: 2, x_lo: 2; x = x_hi * 2 + x_lo), y: 4, z: 16, core: 2. Of those that a mesh axis runs over, the one named last changes fastest.
Arguments:
- initial_field: bfloat16 [2, 8, 192, 48, 192], P(None, 'tp', 'lat'), may hold values from -6 to 6
- first_gain: bfloat16 [2, 192], P('section'), may hold values from 0.25 to 1.75
- first_shift: bfloat16 [2, 192], P('section'), may hold values from -1.75 to 1.75
- qkv_weight: bfloat16 [2, 192, 576], P('section', None, 'tp'), may hold values from -0.4375 to 0.4375
- qkv_bias: bfloat16 [2, 576], P('section', 'tp'), may hold values from -1.75 to 1.75
- proj_weight: bfloat16 [2, 192, 192], P('section', None, 'tp'), may hold values from -0.4375 to 0.4375
- proj_bias: bfloat16 [2, 192], P('section', 'tp'), may hold values from -1.75 to 1.75
- second_gain: bfloat16 [2, 192], P('section'), may hold values from 0.25 to 1.75
- second_shift: bfloat16 [2, 192], P('section'), may hold values from -1.75 to 1.75
- expand_weight: bfloat16 [2, 192, 768], P('section', None, 'tp'), may hold values from -0.4375 to 0.4375
- expand_bias: bfloat16 [2, 768], P('section', 'tp'), may hold values from -1.75 to 1.75
- reduce_weight: bfloat16 [2, 768, 192], P('section', 'tp'), may hold values from -0.21875 to 0.21875
- reduce_bias: bfloat16 [2, 192], P('section', 'tp'), may hold values from -1.75 to 1.75
- earth_bias: float32 [2, 4, 64, 6, 1656], P('section', 'tp', 'lat'), may hold values from -4 to 340
Outputs:
- predicted_states: bfloat16 [2, 2, 8, 192, 48, 192], P('section', None, 'tp', 'lat')
All inputs are finite; a program needn't handle non-finite values.
Results may differ from a plain program's by a relative error of at most 0.018.
Values may be sent and summed in bfloat16 or wider, within the bound.
No kernel may reach another device: no remote copies, remote signals or barrier semaphores. Data moves between devices by JAX's collectives and lax.ppermute only.
A program may use at most 64 MiB of HBM per device.

v0:
```python
import jax
import jax.numpy as jnp
import numpy as np
from jax import lax
from jax.sharding import PartitionSpec as P

WZ = 2
WH = 6
WW = 12


epsilon = 1e-05


def swapped(block, axis, apart):
    count = lax.axis_size(axis)
    route = []
    for low in range(count):
        high = low | 1 << apart
        if high != low and high < count:
            route += [(low, high), (high, low)]
    return lax.ppermute(block, axis, route)


def passed_along(value, axis, steps):
    count = lax.axis_size(axis)
    first, last = (max(0, -steps), min(count, count - steps))
    return lax.ppermute(value, axis, [(source, source + steps) for source in range(first, last)])


def bias_entries():
    half_rows = WH // 2
    query_pos = np.arange(WZ * half_rows * WW)
    attended_location = np.arange(WZ * WH * WW)
    query_level = query_pos // (half_rows * WW)
    query_row = query_pos // WW % half_rows
    query_col = query_pos % WW
    key_level = attended_location // (WH * WW)
    key_row = attended_location // WW % WH
    key_column_index = attended_location % WW
    table_items = (
        ((query_level[:, None] * WZ + key_level[None, :]) * half_rows + query_row[:, None]) * WH
        + key_row[None, :]
    ) * (2 * WW - 1) + (query_col[:, None] - key_column_index[None, :] + WW - 1)
    return table_items.astype(np.int32)


def layer_norm(values, gain, offset):
    floats = values.astype(jnp.float32)
    middle_point = jnp.mean(floats, axis=-1, keepdims=True)
    spread = jnp.mean((floats - middle_point) ** 2, axis=-1, keepdims=True)
    return (floats - middle_point) * lax.rsqrt(spread + epsilon) * gain.astype(
        jnp.float32
    ) + offset.astype(jnp.float32)


def earth_block(grid, norms, weights, bias_block, band_half):
    first_gain, first_shift, second_gain, second_shift = norms
    (
        qkv_matrix,
        qkv_offset,
        proj_matrix,
        proj_offset,
        expand_matrix,
        expand_offset,
        reduce_matrix,
        shrink_translation,
    ) = weights
    levels, lat_rows, lon_cols, width = grid.shape
    heads = bias_block.shape[0]
    head_size = width // heads
    scale = 1.0 / float(np.sqrt(head_size))
    meridian_slabs = lon_cols // WW
    normed = layer_norm(grid, first_gain, first_shift).astype(jnp.bfloat16)
    flat = normed.reshape(-1, width)
    own_mixed = (
        jnp.dot(flat, qkv_matrix, preferred_element_type=jnp.float32)
        + qkv_offset.astype(jnp.float32)
    ).astype(jnp.bfloat16)
    neighbour_keyvalue = swapped(own_mixed[:, width:], "lat", 0)
    own_kv = own_mixed[:, width:].reshape(levels, lat_rows, lon_cols, 2 * width)
    neighbour_keyvalue = neighbour_keyvalue.reshape(levels, lat_rows, lon_cols, 2 * width)
    lower_first = jnp.concatenate([own_kv, neighbour_keyvalue], axis=1)
    upper_first = jnp.concatenate([neighbour_keyvalue, own_kv], axis=1)
    window_kv = jnp.where(band_half == 0, lower_first, upper_first)
    keyvals = window_kv.reshape(levels, 2 * lat_rows, meridian_slabs, WW, 2 * width).transpose(
        2, 0, 1, 3, 4
    )
    keyvals = keyvals.reshape(meridian_slabs, levels * 2 * lat_rows * WW, 2 * width)
    query_rows = (
        own_mixed[:, :width]
        .reshape(levels, lat_rows, meridian_slabs, WW, width)
        .transpose(2, 0, 1, 3, 4)
    )
    query_rows = query_rows.reshape(meridian_slabs, levels * lat_rows * WW, width)
    query_count = query_rows.shape[1]
    key_count = keyvals.shape[1]
    query_heads = query_rows.reshape(meridian_slabs, query_count, heads, head_size)
    key_heads = keyvals[..., :width].reshape(meridian_slabs, key_count, heads, head_size)
    value_heads = keyvals[..., width:].reshape(meridian_slabs, key_count, heads, head_size)
    scores = (
        jnp.einsum("wqhd,wkhd->whqk", query_heads, key_heads, preferred_element_type=jnp.float32)
        * scale
        + bias_block[None]
    )
    probs = jax.nn.softmax(scores, axis=-1).astype(jnp.bfloat16)
    attended = jnp.einsum(
        "whqk,wkhd->wqhd", probs, value_heads, preferred_element_type=jnp.float32
    ).astype(jnp.bfloat16)
    merged = (
        attended.reshape(meridian_slabs, levels, lat_rows, WW, width)
        .transpose(1, 2, 0, 3, 4)
        .reshape(-1, width)
    )
    branch = jnp.dot(merged, proj_matrix, preferred_element_type=jnp.float32) + proj_offset.astype(
        jnp.float32
    )
    middle = (grid.reshape(-1, width).astype(jnp.float32) + branch).astype(jnp.bfloat16)
    normed_two = layer_norm(middle, second_gain, second_shift).astype(jnp.bfloat16)
    hidden = jax.nn.gelu(
        jnp.dot(normed_two, expand_matrix, preferred_element_type=jnp.float32)
        + expand_offset.astype(jnp.float32),
        approximate=False,
    ).astype(jnp.bfloat16)
    result = (
        middle.astype(jnp.float32)
        + jnp.dot(hidden, reduce_matrix, preferred_element_type=jnp.float32)
        + shrink_translation.astype(jnp.float32)
    ).astype(jnp.bfloat16)
    return result.reshape(levels, lat_rows, lon_cols, width)


def on_device(
    initial_field,
    first_gain,
    first_shift,
    qkv_weight,
    qkv_bias,
    proj_weight,
    proj_bias,
    second_gain,
    second_shift,
    expand_weight,
    expand_bias,
    reduce_weight,
    reduce_bias,
    earth_bias,
):
    collected_values = (
        lax.all_gather(qkv_weight, "tp", axis=2, tiled=True),
        lax.all_gather(qkv_bias, "tp", axis=1, tiled=True),
        lax.all_gather(proj_weight, "tp", axis=2, tiled=True),
        lax.all_gather(proj_bias, "tp", axis=1, tiled=True),
        lax.all_gather(expand_weight, "tp", axis=2, tiled=True),
        lax.all_gather(expand_bias, "tp", axis=1, tiled=True),
        lax.all_gather(reduce_weight, "tp", axis=1, tiled=True),
        lax.all_gather(reduce_bias, "tp", axis=1, tiled=True),
    )
    weights = tuple((piece[0] for piece in collected_values))
    norms = (first_gain[0], first_shift[0], second_gain[0], second_shift[0])
    bias_table = earth_bias[0, 0, 0]
    table_items = jnp.asarray(bias_entries())
    portion_index = lax.axis_index("section")
    band_half = lax.axis_index("lat") % 2
    micro_count = initial_field.shape[0]
    bias_block = jnp.take(bias_table, table_items, axis=1)
    carried = jnp.zeros_like(initial_field[0])
    daily_lead_times = []
    quarter_lead_times = []
    for turn_index in range(micro_count + 1):
        own_field = initial_field[min(turn_index, micro_count - 1)]
        block_input = jnp.where(portion_index == 0, own_field, carried)
        block_output = earth_block(block_input, norms, weights, bias_block, band_half)
        if turn_index < micro_count:
            daily_lead_times.append(block_output)
            carried = passed_along(block_output, "section", 1)
        if turn_index > 0:
            quarter_lead_times.append(block_output)
    predicted_states = jnp.where(
        portion_index == 0, jnp.stack(daily_lead_times), jnp.stack(quarter_lead_times)
    )
    return predicted_states[None]


def solution(mesh):
    return jax.shard_map(
        on_device,
        mesh=mesh,
        in_specs=(
            P(None, "tp", "lat", None, None),
            P("section", None),
            P("section", None),
            P("section", None, "tp"),
            P("section", "tp"),
            P("section", None, "tp"),
            P("section", "tp"),
            P("section", None),
            P("section", None),
            P("section", None, "tp"),
            P("section", "tp"),
            P("section", "tp", None),
            P("section", "tp"),
            P("section", "tp", "lat", None, None),
        ),
        out_specs=P("section", None, "tp", "lat", None, None),
        check_vma=False,
    )
```

profile of v0, /device:TPU:7, one launch (start us, length us, event | category | flops | bytes accessed | tf_op | source)
XLA Modules:
  0.0 165.5 jit_solution(211439283647402022)
XLA Ops:
  1.0 1.1 fusion.184
  3.5 1.3 dynamic-slice
  10.3 8.8 %all-reduce.4 = (bf16[768]{0:T(1024)(128)(2,1)S(1)}, bf16[192]{0:T(256)(128)(2,1)S(1)}, bf16[576]{0:T(1024)(128)(2,1)S(1)}, bf16[192]{0:T(256)(128)(2,1)S(1)}) all-reduce(bf16[768]{0:T(1024)(128)(2,1)S(1)} %dynamic-update-slice.2, bf16[192]{0:T(256)(128)(2,1)S(1)} %dynamic-update-slice.1, ...), channel_id=1, replica_groups=mesh['section'=2,'lat'=64,'tp'=4] {'tp'}, use_global_device_ids=true, to_apply=%add.2 | all-reduce | flops 1728 | bytes 6912
  19.1 10.2 %all_gather.24 = bf16[1,192,576]{1,2,0:T(8,128)(2,1)S(1)} all-gather(bf16[1,192,144]{1,2,0:T(8,128)(2,1)} %param.18), channel_id=1, replica_groups=mesh['section'=2,'lat'=64,'tp'=4] {'tp'}, dimensions={2}, use_global_device_ids=true | all-gather | bytes 276480 | tf_op jit(solution)/shard_map/all_gather | solution.py:150
  30.9 6.9 %collective-permute-start = (bf16[288,384]{1,0:T(8,128)(2,1)S(1)}, bf16[288,384]{1,0:T(8,128)(2,1)}, u32[]{:S(2)}, u32[]{:S(2)}) collective-permute-start(bf16[288,384]{1,0:T(8,128)(2,1)S(1)} %slice.62), channel_id=1, source_target_pairs={{0,4},{4,0},{8,12},{12,8},{16,20},{20,16},{24,28},{28,24},{32,36},... | collective-permute-start | bytes 663560 | tf_op jit(solution)/shard_map/ppermute | solution.py:22
  38.7 19.9 %gather_fusion = f32[10368,6]{1,0:T(8,128)} fusion(f32[6,1656]{0,1:T(8,128)S(1)} %bitcast.127, s32[11264]{0:T(1024)S(1)} %pad_clamp_fusion), kind=kCustom, calls=%fused_computation | custom fusion | bytes 539136 | tf_op jit(solution)/shard_map/jit(_take)/gather | solution.py:166
  58.6 4.8 %copy.74 = f32[72,144,6]{1,0,2:T(8,128)S(1)} copy(f32[72,144,6]{2,1,0:T(8,128)} %bitcast.128) | data formatting | bytes 497664 | tf_op jit(solution)/shard_map/jit(_take)/gather | solution.py:166
  63.5 9.2 %all_gather.26 = bf16[1,192,192]{1,2,0:T(8,128)(2,1)S(1)} all-gather(bf16[1,192,48]{1,2,0:T(8,128)(2,1)S(1)} %copy-done.10), channel_id=1, replica_groups=mesh['section'=2,'lat'=64,'tp'=4] {'tp'}, dimensions={2}, use_global_device_ids=true | all-gather | bytes 92160 | tf_op jit(solution)/shard_map/all_gather | solution.py:152
  74.0 12.1 %all_gather.28 = bf16[1,192,768]{1,0,2:T(2,128)(2,1)S(1)} all-gather(bf16[1,192,192]{1,0,2:T(2,128)(2,1)S(1)} %copy.77), channel_id=1, replica_groups=mesh['section'=2,'lat'=64,'tp'=4] {'tp'}, dimensions={2}, use_global_device_ids=true | all-gather | bytes 368640 | tf_op jit(solution)/shard_map/all_gather | solution.py:154
  86.6 10.6 %all_gather.30 = bf16[1,768,192]{2,1,0:T(8,128)(2,1)} all-gather(bf16[1,192,192]{2,1,0:T(8,128)(2,1)} %param.26), channel_id=1, replica_groups=mesh['section'=2,'lat'=64,'tp'=4] {'tp'}, dimensions={1}, use_global_device_ids=true | all-gather | bytes 368640 | tf_op jit(solution)/shard_map/all_gather | solution.py:156
  100.6 3.8 %fusion.18 = bf16[4,72,6,32]{1,3,2,0:T(8,128)(2,1)} fusion(bf16[4,144,6,32]{1,3,2,0:T(8,128)(2,1)S(1)} %bitcast.155, f32[4,6,72]{2,1,0:T(8,128)S(1)} %fusion.354, f32[6,72,144]{2,1,0:T(8,128)S(1)} %bitcast.143, bf16[4,144,6,32]{1,3,2,0:T(8,128)(2,1)S(1)} %bitcast.151, bf16[4,72,6,32]{3,2,0,1:T(8,128)(2,1)S(1)} %reshape_reshape.9), kind=kOutput, calls=%fused_computation.46 | convolution fusion | flops 33151824 | bytes 919296 | tf_op jit(solution)/shard_map/whqk,wkhd->wqhd/dot_general | solution.py:107
  104.4 1.8 %copy.75 = bf16[4,72,6,32]{3,2,0,1:T(8,128)(2,1)S(1)} copy(bf16[4,72,6,32]{1,3,2,0:T(8,128)(2,1)} %fusion.18) | data formatting | bytes 221184 | tf_op jit(solution)/shard_map/convert_element_type | solution.py:109
  107.3 2.4 %fusion.17 = bf16[288,192]{1,0:T(8,128)(2,1)S(1)} fusion(f32[288,192]{1,0:T(8,128)S(1)} %get-tuple-element.20, f32[768]{0:T(1024)S(1)} %copy-done.11, bf16[1,768,192]{2,1,0:T(8,128)(2,1)S(1)} %copy-done.1, bf16[1,192,768]{2,1,0:T(8,128)(2,1)S(1)} %copy.78, f32[192]{0:T(256)S(1)} %copy-done.22, f32[192]{0:T(256)S(1)} %bitcast.171, f32[192]{0:T(256)S(1)} %bitcast.168, ...), kind=kOutput, calls=%fused_computation.45 | convolution fusion | flops 184909824 | bytes 929280 | tf_op jit(solution)/shard_map/dot_general | solution.py:127
  109.7 1.5 collective-permute-start.1
  111.2 5.9 %collective-permute-done.1 = bf16[2,3,48,192]{3,2,1,0:T(8,128)(2,1)S(1)} collective-permute-done((bf16[2,3,48,192]{3,2,1,0:T(8,128)(2,1)S(1)}, bf16[2,3,48,192]{3,2,1,0:T(8,128)(2,1)S(1)}, u32[]{:S(2)}, u32[]{:S(2)}) %collective-permute-start.1) | collective-permute-done | bytes 110624 | tf_op jit(solution)/shard_map/ppermute | solution.py:28
  118.1 10.0 %collective-permute-start.2 = (bf16[288,384]{1,0:T(8,128)(2,1)S(1)}, bf16[288,384]{1,0:T(8,128)(2,1)S(1)}, u32[]{:S(2)}, u32[]{:S(2)}) collective-permute-start(bf16[288,384]{1,0:T(8,128)(2,1)S(1)} %slice.66), channel_id=1, source_target_pairs={{0,4},{4,0},{8,12},{12,8},{16,20},{20,16},{24,28},{28,24},{32,36},... | collective-permute-start | bytes 663560 | tf_op jit(solution)/shard_map/ppermute | solution.py:22
  131.2 1.7 %fusion.358 = f32[4,6,72]{2,1,0:T(8,128)} fusion(f32[6,72,144]{2,1,0:T(8,128)S(1)} %bitcast.144, bf16[4,144,6,32]{1,3,2,0:T(8,128)(2,1)S(1)} %bitcast.152, bf16[4,72,6,32]{3,2,0,1:T(8,128)(2,1)S(1)} %reshape_reshape.10), kind=kOutput, calls=%fused_computation.393 | convolution fusion | flops 16920720 | bytes 587520 | tf_op jit(solution)/shard_map/sub | solution.py:106
  132.9 3.9 %fusion.19 = bf16[4,72,6,32]{1,3,2,0:T(8,128)(2,1)S(1)} fusion(bf16[4,144,6,32]{1,3,2,0:T(8,128)(2,1)S(1)} %bitcast.156, f32[4,6,72]{2,1,0:T(8,128)} %fusion.358, f32[6,72,144]{2,1,0:T(8,128)S(1)} %bitcast.145, bf16[4,144,6,32]{1,3,2,0:T(8,128)(2,1)S(1)} %bitcast.153, bf16[4,72,6,32]{3,2,0,1:T(8,128)(2,1)S(1)} %reshape_reshape.10), kind=kOutput, calls=%fused_computation.47 | convolution fusion | flops 33151824 | bytes 919296 | tf_op jit(solution)/shard_map/whqk,wkhd->wqhd/dot_general | solution.py:107
  138.8 2.4 %fusion.16 = bf16[288,192]{1,0:T(8,128)(2,1)S(1)} fusion(f32[768]{0:T(1024)S(1)} %copy-done.12, bf16[288,192]{1,0:T(8,128)(2,1)S(1)} %fusion.189, bf16[1,768,192]{2,1,0:T(8,128)(2,1)S(1)} %copy-done.1, bf16[1,192,768]{2,1,0:T(8,128)(2,1)S(1)} %copy.78, f32[192]{0:T(256)S(1)} %copy-done.23, f32[288]{0:T(512)S(1)} %add_rsqrt_fusion.4, ...), kind=kOutput, calls=%fused_computation.44 | convolution fusion | flops 185020416 | bytes 818688 | tf_op jit(solution)/shard_map/dot_general | solution.py:127
  141.2 1.3 collective-permute-start.3
  142.5 7.1 %collective-permute-done.3 = bf16[2,3,48,192]{3,2,1,0:T(8,128)(2,1)S(1)} collective-permute-done((bf16[2,3,48,192]{3,2,1,0:T(8,128)(2,1)S(1)}, bf16[2,3,48,192]{3,2,1,0:T(8,128)(2,1)S(1)}, u32[]{:S(2)}, u32[]{:S(2)}) %collective-permute-start.3) | collective-permute-done | bytes 110624 | tf_op jit(solution)/shard_map/ppermute | solution.py:28
  150.6 3.3 %collective-permute-start.4 = (bf16[288,384]{1,0:T(8,128)(2,1)S(1)}, bf16[288,384]{1,0:T(8,128)(2,1)S(1)}, u32[]{:S(2)}, u32[]{:S(2)}) collective-permute-start(bf16[288,384]{1,0:T(8,128)(2,1)S(1)} %slice.70), channel_id=1, source_target_pairs={{0,4},{4,0},{8,12},{12,8},{16,20},{20,16},{24,28},{28,24},{32,36},... | collective-permute-start | bytes 663560 | tf_op jit(solution)/shard_map/ppermute | solution.py:22
  157.1 3.1 %fusion.20 = bf16[4,72,6,32]{1,3,2,0:T(8,128)(2,1)S(1)} fusion(bf16[4,144,6,32]{1,3,2,0:T(8,128)(2,1)S(1)} %bitcast.154, f32[4,6,72]{2,1,0:T(8,128)S(1)} %fusion.361, f32[6,72,144]{2,1,0:T(8,128)S(1)} %bitcast.147, bf16[4,144,6,32]{1,3,2,0:T(8,128)(2,1)S(1)} %bitcast.149, bf16[4,72,6,32]{3,2,0,1:T(8,128)(2,1)S(1)} %reshape_reshape.11), kind=kOutput, calls=%fused_computation.48 | convolution fusion | flops 33151824 | bytes 919296 | tf_op jit(solution)/shard_map/whqk,wkhd->wqhd/dot_general | solution.py:107
  162.3 2.4 %fusion.15 = bf16[288,192]{1,0:T(8,128)(2,1)S(1)} fusion(f32[768]{0:T(1024)S(1)} %copy-done.13, bf16[288,192]{1,0:T(8,128)(2,1)S(1)} %fusion.190, bf16[1,768,192]{2,1,0:T(8,128)(2,1)S(1)} %copy-done.1, bf16[1,192,768]{2,1,0:T(8,128)(2,1)S(1)} %copy.78, f32[192]{0:T(256)S(1)} %copy-done.24, f32[288]{0:T(512)S(1)} %add_rsqrt_fusion.3, ...), kind=kOutput, calls=%fused_computation.43 | convolution fusion | flops 185020416 | bytes 818688 | tf_op jit(solution)/shard_map/dot_general | solution.py:127
  (157 shorter events, 27.0 us)
Async XLA Ops:
  30.4 7.9 %copy-start.9 = (f32[1,1,1,6,1656]{4,2,3,1,0:T(1,128)S(1)}, f32[1,1,1,6,1656]{4,2,3,1,0:T(1,128)}, u32[]{:S(2)}) copy-start(f32[1,1,1,6,1656]{4,2,3,1,0:T(1,128)} %param.28) | copy-start | bytes 119236
  30.7 7.9 %copy-start.8 = (s32[10368]{0:T(1024)S(1)}, s32[10368]{0:T(1024)}, u32[]{:S(2)}) copy-start(s32[10368]{0:T(1024)} %constant.152) | copy-start | bytes 124420
  30.9 66.4 %collective-permute-start = (bf16[288,384]{1,0:T(8,128)(2,1)S(1)}, bf16[288,384]{1,0:T(8,128)(2,1)}, u32[]{:S(2)}, u32[]{:S(2)}) collective-permute-start(bf16[288,384]{1,0:T(8,128)(2,1)S(1)} %slice.62), channel_id=1, source_target_pairs={{0,4},{4,0},{8,12},{12,8},{16,20},{20,16},{24,28},{28,24},{32,36},... | collective-permute-start | bytes 663560 | tf_op jit(solution)/shard_map/ppermute | solution.py:22
  58.6 4.9 %copy-start.10 = (bf16[1,192,48]{1,2,0:T(8,128)(2,1)S(1)}, bf16[1,192,48]{1,2,0:T(8,128)(2,1)}, u32[]{:S(2)}) copy-start(bf16[1,192,48]{1,2,0:T(8,128)(2,1)} %param.20) | copy-start | bytes 55300
  58.6 15.2 %copy-start.7 = (bf16[1,192,192]{2,1,0:T(8,128)(2,1)S(1)}, bf16[1,192,192]{2,1,0:T(8,128)(2,1)}, u32[]{:S(2)}) copy-start(bf16[1,192,192]{2,1,0:T(8,128)(2,1)} %param.24) | copy-start | bytes 221188
  63.4 33.8 %copy-start.14 = (bf16[1,192]{1,0:T(2,128)(2,1)S(1)}, bf16[1,192]{1,0:T(2,128)(2,1)}, u32[]{:S(2)}) copy-start(bf16[1,192]{1,0:T(2,128)(2,1)} %param.22) | copy-start | bytes 1156
  63.4 33.8 %copy-start.15 = (bf16[1,192]{1,0:T(2,128)(2,1)S(1)}, bf16[1,192]{1,0:T(2,128)(2,1)}, u32[]{:S(2)}) copy-start(bf16[1,192]{1,0:T(2,128)(2,1)} %param.23) | copy-start | bytes 1156
  63.5 33.8 %copy-start = (bf16[2,2,3,48,192]{4,3,2,1,0:T(8,128)(2,1)S(1)}, bf16[2,2,3,48,192]{4,3,2,1,0:T(8,128)(2,1)}, u32[]{:S(2)}) copy-start(bf16[2,2,3,48,192]{4,3,2,1,0:T(8,128)(2,1)} %param.15) | copy-start | bytes 663556
  97.2 10.0 %copy-start.16 = (f32[1,192]{1,0:T(1,128)}, f32[1,192]{1,0:T(1,128)S(1)}, u32[]{:S(2)}) copy-start(f32[1,192]{1,0:T(1,128)S(1)} %mul.170) | copy-start | bytes 2308
  97.3 10.0 %copy-start.19 = (f32[1,192]{1,0:T(1,128)}, f32[1,192]{1,0:T(1,128)S(1)}, u32[]{:S(2)}) copy-start(f32[1,192]{1,0:T(1,128)S(1)} %add.304) | copy-start | bytes 2308
  104.4 2.9 %copy-start.1 = (bf16[1,768,192]{2,1,0:T(8,128)(2,1)S(1)}, bf16[1,768,192]{2,1,0:T(8,128)(2,1)}, u32[]{:S(2)}) copy-start(bf16[1,768,192]{2,1,0:T(8,128)(2,1)} %all_gather.30) | copy-start | bytes 884740
  104.4 2.9 %copy-start.11 = (f32[768]{0:T(1024)S(1)}, f32[768]{0:T(1024)}, u32[]{:S(2)}) copy-start(f32[768]{0:T(1024)} %add.317) | copy-start | bytes 9220
  104.4 2.9 %copy-start.22 = (f32[192]{0:T(256)S(1)}, f32[192]{0:T(256)}, u32[]{:S(2)}) copy-start(f32[192]{0:T(256)} %add.318) | copy-start | bytes 2308
  109.7 7.9 %copy-start.3 = (bf16[288,192]{1,0:T(8,128)(2,1)}, bf16[288,192]{1,0:T(8,128)(2,1)S(1)}, u32[]{:S(2)}) copy-start(bf16[288,192]{1,0:T(8,128)(2,1)S(1)} %fusion.17) | copy-start | bytes 331780
  109.7 7.4 %collective-permute-start.1 = (bf16[2,3,48,192]{3,2,1,0:T(8,128)(2,1)S(1)}, bf16[2,3,48,192]{3,2,1,0:T(8,128)(2,1)S(1)}, u32[]{:S(2)}, u32[]{:S(2)}) collective-permute-start(bf16[2,3,48,192]{3,2,1,0:T(8,128)(2,1)S(1)} %bitcast.157), channel_id=1, source_target_pairs={{0,256},{1,257},{2,258},{3,259},{4,260},{5,261},{6,262},{7,263},{8... | collective-permute-start | bytes 331784 | tf_op jit(solution)/shard_map/ppermute | solution.py:28
  118.1 11.1 %collective-permute-start.2 = (bf16[288,384]{1,0:T(8,128)(2,1)S(1)}, bf16[288,384]{1,0:T(8,128)(2,1)S(1)}, u32[]{:S(2)}, u32[]{:S(2)}) collective-permute-start(bf16[288,384]{1,0:T(8,128)(2,1)S(1)} %slice.66), channel_id=1, source_target_pairs={{0,4},{4,0},{8,12},{12,8},{16,20},{20,16},{24,28},{28,24},{32,36},... | collective-permute-start | bytes 663560 | tf_op jit(solution)/shard_map/ppermute | solution.py:22
  141.2 8.5 %collective-permute-start.3 = (bf16[2,3,48,192]{3,2,1,0:T(8,128)(2,1)S(1)}, bf16[2,3,48,192]{3,2,1,0:T(8,128)(2,1)S(1)}, u32[]{:S(2)}, u32[]{:S(2)}) collective-permute-start(bf16[2,3,48,192]{3,2,1,0:T(8,128)(2,1)S(1)} %bitcast.159), channel_id=1, source_target_pairs={{0,256},{1,257},{2,258},{3,259},{4,260},{5,261},{6,262},{7,263},{8... | collective-permute-start | bytes 331784 | tf_op jit(solution)/shard_map/ppermute | solution.py:28
  150.6 4.2 %collective-permute-start.4 = (bf16[288,384]{1,0:T(8,128)(2,1)S(1)}, bf16[288,384]{1,0:T(8,128)(2,1)S(1)}, u32[]{:S(2)}, u32[]{:S(2)}) collective-permute-start(bf16[288,384]{1,0:T(8,128)(2,1)S(1)} %slice.70), channel_id=1, source_target_pairs={{0,4},{4,0},{8,12},{12,8},{16,20},{20,16},{24,28},{28,24},{32,36},... | collective-permute-start | bytes 663560 | tf_op jit(solution)/shard_map/ppermute | solution.py:22
  160.3 2.0 %copy-start.13 = (f32[768]{0:T(1024)S(1)}, f32[768]{0:T(1024)}, u32[]{:S(2)}) copy-start(f32[768]{0:T(1024)} %add.317) | copy-start | bytes 9220
  160.3 2.0 %copy-start.18 = (f32[1,192]{1,0:T(1,128)S(1)}, f32[1,192]{1,0:T(1,128)}, u32[]{:S(2)}) copy-start(f32[1,192]{1,0:T(1,128)} %copy-done.16) | copy-start | bytes 2308
  160.3 2.0 %copy-start.21 = (f32[1,192]{1,0:T(1,128)S(1)}, f32[1,192]{1,0:T(1,128)}, u32[]{:S(2)}) copy-start(f32[1,192]{1,0:T(1,128)} %copy-done.19) | copy-start | bytes 2308
  160.3 2.0 %copy-start.24 = (f32[192]{0:T(256)S(1)}, f32[192]{0:T(256)}, u32[]{:S(2)}) copy-start(f32[192]{0:T(256)} %add.318) | copy-start | bytes 2308
  162.3 2.4 %copy-start.4 = (bf16[288,192]{1,0:T(8,128)(2,1)S(1)}, bf16[288,192]{1,0:T(8,128)(2,1)}, u32[]{:S(2)}) copy-start(bf16[288,192]{1,0:T(8,128)(2,1)} %copy-done.3) | copy-start | bytes 331780
  162.3 2.4 %copy-start.6 = (bf16[288,192]{1,0:T(8,128)(2,1)S(1)}, bf16[288,192]{1,0:T(8,128)(2,1)}, u32[]{:S(2)}) copy-start(bf16[288,192]{1,0:T(8,128)(2,1)} %copy-done.5) | copy-start | bytes 331780
  (6 other events, 10.9 us)
where the time goes:
time: 166 us
  blocking collectives  50.9 us (31%)
  local copies, waits for them, and re-layouts  40.5 us (24%)
  matrix products  23.5 us (14%)
  starting transfers between devices  23 us (14%)
  waiting for transfers between devices  14 us (8%)
  other arithmetic  10.6 us (6%)
  between operations  2.92 us (2%)
    gather x2, local copies, waits for them, and re-layouts, on_device(): bias_block = jnp.take(bias_table, table_items, axis=1)  24.8 us
    ppermute x3, starting transfers between devices, swapped(): return lax.ppermute(block, axis, route)  20.3 us
    ppermute x2, waiting for transfers between devices, passed_along(): lax.ppermute(value, axis, [(source, source + steps) for source in range(f...  13.1 us
    all_gather x1, blocking collectives, on_device(): lax.all_gather(expand_weight, 'tp', axis=2, tiled=True)  12.1 us
    dot_general x3, matrix products, earth_block(): jnp.einsum('whqk,wkhd->wqhd', probs, value_heads, preferred_element_type=...  10.8 us
    all_gather x1, blocking collectives, on_device(): lax.all_gather(reduce_weight, 'tp', axis=1, tiled=True)  10.6 us
    all_gather x1, blocking collectives, on_device(): lax.all_gather(qkv_weight, 'tp', axis=2, tiled=True)  10.2 us
    all_gather x1, blocking collectives, on_device(): lax.all_gather(proj_weight, 'tp', axis=2, tiled=True)  9.17 us
  transfers between devices with their start and end apart: 5, of which 4 were waited for; matrix products, arithmetic and copies ran while one was open for 17% of the time, Pallas kernels for 0%

commit v1 on v0

v1 whole, which is shorter than its diff:
```python
import functools

import jax
import jax.numpy as jnp
import numpy as np
from jax import lax
from jax.experimental import pallas as pl
from jax.experimental.pallas import tpu as pltpu
from jax.sharding import PartitionSpec as P

WZ = 2
WH = 6
WW = 12
HALF = WH // 2
C = 192
HEADS = 6
DIM = C // HEADS
WIN = WZ * WH * WW
SPAN = 2 * WW - 1
MLP = 768
EPS = 1e-05
LOG2E = 1.4426950408889634
BF = jnp.bfloat16
F32 = jnp.float32
PACK_ROWS = 208
SLOT = 256

VMEM = pl.BlockSpec(memory_space=pltpu.VMEM)
PARAMS = pltpu.CompilerParams(vmem_limit_bytes=56 * 1024 * 1024)


def pick_rows():
    out = np.zeros((2, 2 * WIN, 1), np.int32)
    for core in range(2):
        for row in range(2 * WIN):
            w, rest = divmod(row, WIN)
            wl, zh = divmod(rest, WZ * WH)
            z, hh = divmod(zh, WH)
            half, h = divmod(hh, HALF)
            lon = (2 * core + w) * WW + wl
            out[core, row, 0] = half * 288 + (z * HALF + h) * 48 + lon
    return out


def place_rows():
    out = np.zeros((2, 288, 1), np.int32)
    for core in range(2):
        for row in range(288):
            zh, lon = divmod(row, 48)
            z, h = divmod(zh, HALF)
            w, wl = divmod(lon, WW)
            out[core, row, 0] = w * WIN + wl * WZ * WH + z * WH + HALF * core + h
    return out


def turn_columns():
    out = np.zeros((WZ * WH * SPAN, WZ * WH * SPAN), np.float32)
    for zk in range(WZ):
        for hk in range(WH):
            for j in range(SPAN):
                out[(zk * WH + hk) * SPAN + j, (SPAN - 1 - j) * WZ * WH + zk * WH + hk] = 1.0
    return out.astype(BF)


def pack_kernel(qkv, proj, expand, reduce, qkv_b, proj_b, expand_b, reduce_b, out):
    out[192:208, :] = jnp.zeros((16, 576), BF)
    out[0:192, 0:192] = expand[0]
    out[0:192, 192:336] = qkv[0]
    out[0:192, 336:384] = proj[0]
    out[0:192, 384:576] = reduce[0]
    out[192:193, 0:192] = expand_b[...]
    out[192:193, 192:336] = qkv_b[...]
    out[192:193, 336:384] = proj_b[...]
    out[192:193, 384:432] = reduce_b[...]


def one_hot(index, width):
    rows = index.shape[0]
    lanes = lax.broadcasted_iota(jnp.int32, (rows, width), 1)
    return jnp.where(lanes == index, 1.0, 0.0).astype(BF)


def norm(x, gain, shift):
    mean = jnp.sum(x, axis=-1, keepdims=True) * (1.0 / C)
    centred = x - mean
    var = jnp.sum(centred * centred, axis=-1, keepdims=True) * (1.0 / C)
    return centred * lax.rsqrt(var + EPS) * gain + shift


def dot(a, b):
    return jnp.dot(a, b, preferred_element_type=F32)


def assemble(pack, wqkv, wproj, wexp, wred, bq, bp, be, br):
    rows = slice(0, C)
    wqkv[...] = jnp.zeros_like(wqkv)
    bq[...] = jnp.zeros_like(bq)
    for j in range(4):
        wexp[:, C * j : C * (j + 1)] = pack[j, rows, 0:192]
        wproj[:, 48 * j : 48 * (j + 1)] = pack[j, rows, 336:384]
        wred[C * j : C * (j + 1), :] = pack[j, rows, 384:576]
        be[:, C * j : C * (j + 1)] = pack[j, 192:193, 0:192].astype(F32)
        bp[:, 48 * j : 48 * (j + 1)] = pack[j, 192:193, 336:384].astype(F32)
        br[:, 48 * j : 48 * (j + 1)] = pack[j, 192:193, 384:432].astype(F32)
        at = 144 * j
        while at < 144 * (j + 1):
            part, inner = divmod(at, C)
            size = min(C - inner, 144 * (j + 1) - at)
            source = slice(192 + at - 144 * j, 192 + at - 144 * j + size)
            target = slice(SLOT * part + inner, SLOT * part + inner + size)
            wqkv[:, target] = pack[j, rows, source]
            bq[:, target] = pack[j, 192:193, source].astype(F32)
            at += size


def expand_bias(table, turn, lines, bias):
    for z in range(WZ):
        for half in range(2):
            for r in range(HALF):
                zhr = z * WH + half * HALF + r
                for zk in range(WZ):
                    start = ((z * WZ + zk) * HALF + r) * WH * SPAN
                    lines[8 * zhr : 8 * zhr + HEADS, 138 * zk : 138 * (zk + 1)] = table[
                        half, :, start : start + WH * SPAN
                    ]
    whole = lines[...]
    high = whole.astype(BF)
    rest = whole - high.astype(F32)
    middle = rest.astype(BF)
    low = (rest - middle.astype(F32)).astype(BF)
    turned = (dot(high, turn[...]) + dot(middle, turn[...]) + dot(low, turn[...])) * LOG2E
    for wq in range(WW):
        start = WZ * WH * (WW - 1 - wq)
        piece = turned[:, start : start + WIN]
        for zhr in range(WZ * WH):
            row = wq * WZ * WH + zhr
            bias[:, row, :] = piece[8 * zhr : 8 * zhr + HEADS, :]


def window_block(x, gains, wqkv, wproj, wexp, wred, bq, bp, be, br, bias):
    first_gain, first_shift, second_gain, second_shift = gains
    floats = x.astype(F32)
    normed = norm(floats, first_gain, first_shift).astype(BF)
    mixed = (dot(normed, wqkv[...]) + bq[...]).astype(BF)
    q, k, v = mixed[:, 0:C], mixed[:, SLOT : SLOT + C], mixed[:, 2 * SLOT : 2 * SLOT + C]
    head_of = lax.broadcasted_iota(jnp.int32, (WIN, C), 1) // DIM
    scale = LOG2E / float(np.sqrt(DIM))
    total = None
    zero = jnp.zeros((WIN, C), BF)
    for h in range(HEADS):
        own = head_of == h
        scores = lax.dot_general(
            jnp.where(own, q, zero), k, (((1,), (1,)), ((), ())), preferred_element_type=F32
        )
        scores = scores * scale + bias[h]
        top = jnp.max(scores, axis=-1, keepdims=True)
        weights = jnp.exp2(scores - top)
        probs = (weights * (1.0 / jnp.sum(weights, axis=-1, keepdims=True))).astype(BF)
        part = dot(probs, jnp.where(own, v, zero))
        total = part if total is None else total + part
    middle = (floats + dot(total.astype(BF), wproj[...]) + bp[...]).astype(BF)
    middle_floats = middle.astype(F32)
    normed_two = norm(middle_floats, second_gain, second_shift).astype(BF)
    pre = dot(normed_two, wexp[...]) + be[...]
    hidden = (0.5 * pre * (1.0 + lax.erf(pre * float(np.sqrt(0.5))))).astype(BF)
    return (middle_floats + dot(hidden, wred[...]) + br[...]).astype(BF)


def prepare(pack, gain_refs, table, turn, lines, bias, mats):
    assemble(pack, *mats)
    lines[...] = jnp.zeros_like(lines)
    expand_bias(table, turn, lines, bias)
    return tuple(ref[...].astype(F32) for ref in gain_refs)


def first_kernel(field, index, pack, g1, s1, g2, s2, table, turn, out, lines, bias, *mats):
    @pl.when(lax.axis_index("section") == 0)
    def _():
        core = lax.rem(lax.axis_index("lat"), 2)
        gains = prepare(pack, (g1, s1, g2, s2), table, turn, lines, bias, mats)
        chosen = one_hot(index[core], 576)
        for t in range(2):
            source = jnp.concatenate([field[0, t], field[1, t]], axis=0)
            tokens = dot(chosen, source).astype(BF)
            for w in range(2):
                x = tokens[WIN * w : WIN * (w + 1)]
                out[t, WIN * w : WIN * (w + 1), :] = window_block(x, gains, *mats, bias)


def second_kernel(received, own, pack, g1, s1, g2, s2, table, turn, out, lines, bias, *mats):
    section = lax.axis_index("section")

    @pl.when(section == 0)
    def _():
        out[...] = own[...]

    @pl.when(section == 1)
    def _():
        gains = prepare(pack, (g1, s1, g2, s2), table, turn, lines, bias, mats)
        for t in range(2):
            for w in range(2):
                rows = slice(WIN * w, WIN * (w + 1))
                out[t, rows, :] = window_block(received[t, rows, :], gains, *mats, bias)


def place_kernel(windows, index, out):
    core = lax.rem(lax.axis_index("lat"), 2)
    chosen = one_hot(index[core], 576)
    for t in range(2):
        source = jnp.concatenate([windows[0, t], windows[1, t]], axis=0)
        out[t] = dot(chosen, source).astype(BF)


def call(kernel, out_shape, args, scratch=(), flops=0):
    return pl.pallas_call(
        kernel,
        out_shape=out_shape,
        in_specs=[VMEM] * len(args),
        out_specs=VMEM,
        scratch_shapes=list(scratch),
        compiler_params=PARAMS,
        cost_estimate=pl.CostEstimate(flops=flops, bytes_accessed=1 << 20, transcendentals=0),
    )(*args)


def on_device(
    initial_field,
    first_gain,
    first_shift,
    qkv_weight,
    qkv_bias,
    proj_weight,
    proj_bias,
    second_gain,
    second_shift,
    expand_weight,
    expand_bias_row,
    reduce_weight,
    reduce_bias,
    earth_bias,
):
    lat_count = lax.axis_size("lat")
    pairs = [[2 * i, 2 * i + 1] for i in range(lat_count // 2)]
    packed = call(
        pack_kernel,
        jax.ShapeDtypeStruct((PACK_ROWS, 576), BF),
        (
            qkv_weight,
            proj_weight,
            expand_weight,
            reduce_weight,
            qkv_bias,
            proj_bias,
            expand_bias_row,
            reduce_bias,
        ),
    )
    pack = lax.all_gather(packed, "tp")
    field = lax.all_gather(initial_field.reshape(2, 288, C), "lat", axis_index_groups=pairs)
    table = lax.all_gather(earth_bias.reshape(HEADS, -1), "lat", axis_index_groups=pairs)
    turn = jnp.asarray(turn_columns())
    gains = (first_gain, first_shift, second_gain, second_shift)
    scratch = [
        pltpu.VMEM((96, WZ * WH * SPAN), F32),
        pltpu.VMEM((HEADS, WIN, WIN), F32),
        pltpu.VMEM((C, 3 * SLOT), BF),
        pltpu.VMEM((C, C), BF),
        pltpu.VMEM((C, MLP), BF),
        pltpu.VMEM((MLP, C), BF),
        pltpu.VMEM((1, 3 * SLOT), F32),
        pltpu.VMEM((1, C), F32),
        pltpu.VMEM((1, MLP), F32),
        pltpu.VMEM((1, C), F32),
    ]
    shape = jax.ShapeDtypeStruct((2, 288, C), BF)
    flops = 2 * 576 * 192 * 192 * 14
    daily = call(
        first_kernel,
        shape,
        (field, jnp.asarray(pick_rows()), pack, *gains, table, turn),
        scratch,
        flops,
    )
    received = lax.ppermute(daily, "section", [(0, 1)])
    states = call(second_kernel, shape, (received, daily, pack, *gains, table, turn), scratch, flops)
    both = lax.all_gather(states, "lat", axis_index_groups=pairs)
    placed = call(place_kernel, shape, (both, jnp.asarray(place_rows())))
    return placed.reshape(1, 2, 2, 3, 48, C)


def solution(mesh):
    return jax.shard_map(
        on_device,
        mesh=mesh,
        in_specs=(
            P(None, "tp", "lat", None, None),
            P("section", None),
            P("section", None),
            P("section", None, "tp"),
            P("section", "tp"),
            P("section", None, "tp"),
            P("section", "tp"),
            P("section", None),
            P("section", None),
            P("section", None, "tp"),
            P("section", "tp"),
            P("section", "tp", None),
            P("section", "tp"),
            P("section", "tp", "lat", None, None),
        ),
        out_specs=P("section", None, "tp", "lat", None, None),
        check_vma=False,
    )
```

time: 166 us -> 72.9 us (0.44)
  the two profiles are of different devices: /device:TPU:7 before, /device:TPU:5 now
where the time goes in v1:
time: 72.9 us; the launch traced here: 72.2 us
  blocking collectives  31.4 us (43%)
  waiting for transfers between devices  18 us (25%)
  Pallas kernels  17.1 us (23%)
  local copies, waits for them, and re-layouts  4.48 us (6%)
  starting transfers between devices  1.28 us (2%)
    ppermute x1, waiting for transfers between devices, on_device(): received = lax.ppermute(daily, 'section', [(0, 1)])  18 us
    pallas_call x4, Pallas kernels, call(): pl.pallas_call(kernel, out_shape=out_shape, in_specs=[VMEM] * len(args),...  17.1 us
    all_gather x1, blocking collectives, on_device(): pack = lax.all_gather(packed, 'tp')  15.7 us
    all_gather x1, blocking collectives, on_device(): both = lax.all_gather(states, 'lat', axis_index_groups=pairs)  7.77 us
    all_gather x1, blocking collectives, on_device(): lax.all_gather(initial_field.reshape(2, 288, C), 'lat', axis_index_groups...  5.5 us
    unnamed x4, local copies, waits for them, and re-layouts  3.78 us
    all_gather x1, blocking collectives, on_device(): lax.all_gather(earth_bias.reshape(HEADS, -1), 'lat', axis_index_groups=pa...  2.39 us
  transfers between devices with their start and end apart: 1, of which 1 were waited for; matrix products, arithmetic and copies ran while one was open for 0% of the time, Pallas kernels for 0%

profile of v1, /device:TPU:5, one launch (start us, length us, event | category | flops | bytes accessed | tf_op | source)
XLA Modules:
  0.0 72.2 jit_solution(1113365170287778764)
XLA Ops:
  0.0 1.5 %copy.24.proj = bf16[1,192,48]{2,1,0:T(8,128)(2,1)} copy(bf16[1,192,48]{1,2,0:T(8,128)(2,1)} %param.22) | data formatting | bytes 36864 | tf_op args[5]
  1.5 2.4 %all-gather.1 = f32[2,1,1,6,1656]{4,2,3,1,0:T(1,128)S(1)} all-gather(f32[1,1,1,6,1656]{4,2,3,1,0:T(1,128)} %param.30), channel_id=3, replica_groups={{0,4},{8,12},{16,20},{24,28},{32,36},{40,44},{48,52},{56,60},{64,68},{7..., dimensions={0}, use_global_device_ids=true | all-gather | bytes 119232 | tf_op jit(solution)/shard_map/all_gather | solution.py:260
  3.9 0.7 copy.26.table
  4.5 1.6 %copy.23.qkv = bf16[1,192,144]{2,1,0:T(8,128)(2,1)} copy(bf16[1,192,144]{1,2,0:T(8,128)(2,1)} %param.20) | data formatting | bytes 110592 | tf_op args[3]
  6.2 5.5 %all_gather.18.field = bf16[2,2,288,192]{3,2,1,0:T(8,128)(2,1)} all-gather(bf16[1,2,288,192]{3,2,1,0:T(8,128)(2,1)} %bitcast.11), channel_id=1, replica_groups={{0,4},{8,12},{16,20},{24,28},{32,36},{40,44},{48,52},{56,60},{64,68},{7..., dimensions={0}, use_global_device_ids=true | all-gather | bytes 663552 | tf_op jit(solution)/shard_map/all_gather | solution.py:259
  11.7 1.9 %shard_map.163 = bf16[208,576]{1,0:T(8,128)(2,1)} custom-call(bf16[1,192,144]{2,1,0:T(8,128)(2,1)} %copy.23.qkv, bf16[1,192,48]{2,1,0:T(8,128)(2,1)} %copy.24.proj, bf16[1,192,192]{2,1,0:T(8,128)(2,1)} %expand.1, bf16[1,192,192]{2,1,0:T(8,128)(2,1)} %reduce.1, bf16[1,144]{1,0:T(2,128)(2,1)} %qkv_b.1, bf16[1,48]{1,0:T(2,128)(2,1)} %proj_b.1, ...), custom_call_target="tpu_custom_call" | custom-call | bytes 1048576 | tf_op jit(solution)/shard_map/pallas_call | solution.py:215
  13.5 15.7 %all-gather = bf16[832,576]{1,0:T(8,128)(2,1)} all-gather(bf16[208,576]{1,0:T(8,128)(2,1)} %shard_map.163), channel_id=2, replica_groups=mesh['section'=2,'lat'=64,'tp'=4] {'tp'}, dimensions={0}, use_global_device_ids=true | all-gather | bytes 1198080 | tf_op jit(solution)/shard_map/all_gather | solution.py:258
  29.2 2.4 %shard_map.164.own = bf16[2,288,192]{2,1,0:T(8,128)(2,1)} custom-call(bf16[2,2,288,192]{3,2,1,0:T(8,128)(2,1)} %all_gather.18.field, s32[2,288,1]{2,1,0:T(8,128)} %constant.7.clone.index, bf16[4,208,576]{2,1,0:T(8,128)(2,1)} %bitcast.7, bf16[1,192]{1,0:T(2,128)(2,1)} %g1.3, bf16[1,192]{1,0:T(2,128)(2,1)} %s1_.3, bf16[1,192]{1,0:T(2,128)(2,1)} %g2.3, ...), custom_call_target="tpu_custom_call" | custom-call | flops 594542592 | bytes 1048576 | tf_op jit(solution)/shard_map/pallas_call | solution.py:215
  31.6 1.3 %collective-permute-start = (bf16[2,288,192]{2,1,0:T(8,128)(2,1)}, bf16[2,288,192]{2,1,0:T(8,128)(2,1)S(1)}, u32[]{:S(2)}, u32[]{:S(2)}) collective-permute-start(bf16[2,288,192]{2,1,0:T(8,128)(2,1)} %shard_map.164.own), channel_id=1, source_target_pairs={{0,256},{1,257},{2,258},{3,259},{4,260},{5,261},{6,262},{7,263},{8... | collective-permute-start | bytes 663560 | tf_op jit(solution)/shard_map/ppermute | solution.py:284
  32.9 18.0 %collective-permute-done.received = bf16[2,288,192]{2,1,0:T(8,128)(2,1)S(1)} collective-permute-done((bf16[2,288,192]{2,1,0:T(8,128)(2,1)}, bf16[2,288,192]{2,1,0:T(8,128)(2,1)S(1)}, u32[]{:S(2)}, u32[]{:S(2)}) %collective-permute-start) | collective-permute-done | bytes 221216 | tf_op jit(solution)/shard_map/ppermute | solution.py:284
  50.9 0.0 copy-start
  50.9 0.7 copy-done
  51.6 10.5 %shard_map.165 = bf16[2,288,192]{2,1,0:T(8,128)(2,1)} custom-call(bf16[2,288,192]{2,1,0:T(8,128)(2,1)} %copy-done, bf16[2,288,192]{2,1,0:T(8,128)(2,1)} %shard_map.164.own, bf16[4,208,576]{2,1,0:T(8,128)(2,1)} %bitcast.8, bf16[1,192]{1,0:T(2,128)(2,1)} %g1.3, bf16[1,192]{1,0:T(2,128)(2,1)} %s1_.3, bf16[1,192]{1,0:T(2,128)(2,1)} %g2.3, bf16[1,192]{1,0:T(2,128)(2,1)} %s2_.3, ...), custom_call_target="tpu_custom_call" | custom-call | flops 594542592 | bytes 1048576 | tf_op jit(solution)/shard_map/pallas_call | solution.py:215
  62.1 7.8 %all-gather.2 = bf16[4,288,192]{2,1,0:T(8,128)(2,1)} all-gather(bf16[2,288,192]{2,1,0:T(8,128)(2,1)} %shard_map.165), channel_id=4, replica_groups={{0,4},{8,12},{16,20},{24,28},{32,36},{40,44},{48,52},{56,60},{64,68},{7..., dimensions={0}, use_global_device_ids=true | all-gather | bytes 663552 | tf_op jit(solution)/shard_map/all_gather | solution.py:286
  69.9 2.3 %shard_map.166 = bf16[2,288,192]{2,1,0:T(8,128)(2,1)} custom-call(bf16[2,2,288,192]{3,2,1,0:T(8,128)(2,1)} %bitcast.9, s32[2,288,1]{2,1,0:T(8,128)} %constant.8.clone.index), custom_call_target="tpu_custom_call" | custom-call | bytes 1048576 | tf_op jit(solution)/shard_map/pallas_call | solution.py:215
  (1 shorter events, 0.0 us)
Async XLA Ops:
  31.6 19.3 %collective-permute-start = (bf16[2,288,192]{2,1,0:T(8,128)(2,1)}, bf16[2,288,192]{2,1,0:T(8,128)(2,1)S(1)}, u32[]{:S(2)}, u32[]{:S(2)}) collective-permute-start(bf16[2,288,192]{2,1,0:T(8,128)(2,1)} %shard_map.164.own), channel_id=1, source_target_pairs={{0,256},{1,257},{2,258},{3,259},{4,260},{5,261},{6,262},{7,263},{8... | collective-permute-start | bytes 663560 | tf_op jit(solution)/shard_map/ppermute | solution.py:284
  50.9 0.7 copy-start

commit v2 on v1

v2 whole, which is shorter than its diff:
```python
import jax
import jax.numpy as jnp
import numpy as np
from jax import lax
from jax.experimental import pallas as pl
from jax.experimental.pallas import tpu as pltpu
from jax.sharding import PartitionSpec as P

WZ = 2
WH = 6
WW = 12
HALF = WH // 2
C = 192
HEADS = 6
DIM = C // HEADS
WIN = WZ * WH * WW
SPAN = 2 * WW - 1
KEYS = WZ * WH
LINE = KEYS * SPAN
MLP = 768
EPS = 1e-05
LOG2E = 1.4426950408889634
BF = jnp.bfloat16
F32 = jnp.float32
TOKENS = 576
SIDE = WH * SPAN

VMEM = pl.BlockSpec(memory_space=pltpu.VMEM)
PARAMS = pltpu.CompilerParams(vmem_limit_bytes=20 * 1024 * 1024)


def pick_rows():
    out = np.zeros((2, 2 * WIN, TOKENS), np.float32)
    for core in range(2):
        for row in range(2 * WIN):
            w, rest = divmod(row, WIN)
            wl, zh = divmod(rest, WZ * WH)
            z, hh = divmod(zh, WH)
            half, h = divmod(hh, HALF)
            lon = (2 * core + w) * WW + wl
            out[core, row, half * 288 + (z * HALF + h) * 48 + lon] = 1.0
    return out.astype(BF)


def split_rows():
    out = np.zeros((2 * WIN, 2 * WIN), np.float32)
    for row in range(2 * WIN):
        w, rest = divmod(row, WIN)
        wl, zh = divmod(rest, WZ * WH)
        z, hh = divmod(zh, WH)
        half, h = divmod(hh, HALF)
        out[((half * WZ + z) * HALF + h) * 24 + w * WW + wl, row] = 1.0
    return out.astype(BF)


def turn_columns():
    out = np.zeros((LINE, LINE), np.float32)
    for key in range(KEYS):
        for j in range(SPAN):
            out[key * SPAN + j, (SPAN - 1 - j) * KEYS + key] = 1.0
    return out.astype(BF)


def pack_kernel(
    qkv, proj, expand, reduce, qkv_b, proj_b, expand_b, reduce_b, field, table, weights, tokens, lines
):
    weights[288:304, :] = jnp.zeros((16, 384), BF)
    weights[0:144, 0:192] = qkv[0]
    weights[144:192, 0:192] = proj[0]
    weights[0:192, 192:384] = expand[0]
    weights[192:288, 0:192] = reduce[0, 0:96]
    weights[192:288, 192:384] = reduce[0, 96:192]
    weights[288:289, 0:144] = qkv_b[...]
    weights[288:289, 144:192] = proj_b[...]
    weights[288:289, 192:384] = expand_b[...]
    weights[289:290, 0:48] = reduce_b[...]
    tokens[0:TOKENS, 0:C] = field[...]
    lines[...] = jnp.zeros_like(lines)
    for zr in range(WZ * HALF):
        z, r = divmod(zr, HALF)
        for zk in range(WZ):
            start = ((z * WZ + zk) * HALF + r) * SIDE
            lines[zk, 8 * zr : 8 * zr + HEADS, :] = table[:, start : start + SIDE]
    for zk in range(WZ):
        whole = lines[zk]
        high = whole.astype(BF)
        rest = whole - high.astype(F32)
        middle = rest.astype(BF)
        low = (rest - middle.astype(F32)).astype(BF)
        for i, part in enumerate((high, middle, low)):
            at = TOKENS + 144 * zk + 48 * i
            tokens[at : at + 48, 0:SIDE] = part


def norm(x, gain, shift):
    mean = jnp.sum(x, axis=-1, keepdims=True) * (1.0 / C)
    centred = x - mean
    var = jnp.sum(centred * centred, axis=-1, keepdims=True) * (1.0 / C)
    return centred * lax.rsqrt(var + EPS) * gain + shift


def dot(a, b):
    return jnp.dot(a, b, preferred_element_type=F32)


def dot_t(a, b):
    return lax.dot_general(a, b, (((1,), (1,)), ((), ())), preferred_element_type=F32)


def assemble(pack, wqkv, wproj, wexp, wred, bqkv, brow):
    for j in range(4):
        wqkv[144 * j : 144 * (j + 1), :] = pack[j, 0:144, 0:192]
        wproj[48 * j : 48 * (j + 1), :] = pack[j, 144:192, 0:192]
        wexp[:, C * j : C * (j + 1)] = pack[j, 0:192, 192:384]
        wred[C * j : C * j + 96, :] = pack[j, 192:288, 0:192]
        wred[C * j + 96 : C * (j + 1), :] = pack[j, 192:288, 192:384]
        brow[0:1, C * j : C * (j + 1)] = pack[j, 288:289, 192:384].astype(F32)
        brow[1:2, 48 * j : 48 * (j + 1)] = pack[j, 288:289, 144:192].astype(F32)
        brow[2:3, 48 * j : 48 * (j + 1)] = pack[j, 289:290, 0:48].astype(F32)
        at = 144 * j
        while at < 144 * (j + 1):
            part, inner = divmod(at, C)
            size = min(C - inner, 144 * (j + 1) - at)
            source = at - 144 * j
            bqkv[part : part + 1, inner : inner + size] = pack[
                j, 288:289, source : source + size
            ].astype(F32)
            at += size


def expand_bias(field, turn, bias):
    for half in range(2):
        parts = None
        for zk in range(WZ):
            rows = slice(TOKENS + 144 * zk, TOKENS + 144 * (zk + 1))
            part = dot(field[half, rows, 0:SIDE], turn[SIDE * zk : SIDE * (zk + 1), :])
            parts = part if parts is None else parts + part
        turned = (parts[0:48] + parts[48:96] + parts[96:144]) * LOG2E
        for wq in range(WW):
            start = KEYS * (WW - 1 - wq)
            piece = turned[:, start : start + WIN]
            for zr in range(WZ * HALF):
                z, r = divmod(zr, HALF)
                row = wq * KEYS + z * WH + half * HALF + r
                bias[:, row, :] = piece[8 * zr : 8 * zr + HEADS, :]


def window_block(x, gains, wqkv, wproj, wexp, wred, bqkv, brow, bias):
    first_gain, first_shift, second_gain, second_shift = gains
    floats = x.astype(F32)
    normed = norm(floats, first_gain, first_shift).astype(BF)
    q, k, v = (
        (dot_t(normed, wqkv[C * i : C * (i + 1), :]) + bqkv[i : i + 1, :]).astype(BF)
        for i in range(3)
    )
    head_of = lax.broadcasted_iota(jnp.int32, (WIN, C), 1) // DIM
    scale = LOG2E / float(np.sqrt(DIM))
    total = None
    zero = jnp.zeros((WIN, C), BF)
    for h in range(HEADS):
        own = head_of == h
        scores = dot_t(jnp.where(own, q, zero), k) * scale + bias[h]
        top = jnp.max(scores, axis=-1, keepdims=True)
        weights = jnp.exp2(scores - top)
        probs = (weights * (1.0 / jnp.sum(weights, axis=-1, keepdims=True))).astype(BF)
        part = dot(probs, jnp.where(own, v, zero))
        total = part if total is None else total + part
    middle = (floats + dot_t(total.astype(BF), wproj[...]) + brow[1:2, 0:C]).astype(BF)
    middle_floats = middle.astype(F32)
    normed_two = norm(middle_floats, second_gain, second_shift).astype(BF)
    pre = dot(normed_two, wexp[...]) + brow[0:1, :]
    hidden = (0.5 * pre * (1.0 + lax.erf(pre * float(np.sqrt(0.5))))).astype(BF)
    return (middle_floats + dot(hidden, wred[...]) + brow[2:3, 0:C]).astype(BF)


def first_kernel(field, pick, pack, g1, s1, g2, s2, turn, out, bias, *mats):
    assemble(pack, *mats)
    expand_bias(field, turn, bias)

    @pl.when(lax.axis_index("section") == 0)
    def _():
        gains = tuple(ref[...].astype(F32) for ref in (g1, s1, g2, s2))
        chosen = pick[lax.rem(lax.axis_index("lat"), 2)]
        for t in range(2):
            rows = slice(288 * t, 288 * (t + 1))
            source = jnp.concatenate([field[0, rows, 0:C], field[1, rows, 0:C]], axis=0)
            tokens = dot(chosen, source).astype(BF)
            for w in range(2):
                x = tokens[WIN * w : WIN * (w + 1)]
                out[t, WIN * w : WIN * (w + 1), :] = window_block(x, gains, *mats, bias)


def second_kernel(received, own, split, g1, s1, g2, s2, bias, *rest):
    *mats, out, hold = rest
    section = lax.axis_index("section")

    @pl.when(section == 0)
    def _():
        hold[...] = own[...]

    @pl.when(section == 1)
    def _():
        gains = tuple(ref[...].astype(F32) for ref in (g1, s1, g2, s2))
        for t in range(2):
            for w in range(2):
                rows = slice(WIN * w, WIN * (w + 1))
                hold[t, rows, :] = window_block(received[t, rows, :], gains, *mats, bias)

    for t in range(2):
        ordered = dot(split[...], hold[t]).astype(BF)
        out[0, t] = ordered[0:WIN]
        out[1, t] = ordered[WIN : 2 * WIN]


def place_kernel(both, out, sems):
    core = lax.rem(lax.axis_index("lat"), 2)
    copies = [
        pltpu.make_async_copy(both.at[side, core], out.at[:, pl.ds(24 * side, 24), :], sems.at[side])
        for side in range(2)
    ]
    for copy in copies:
        copy.start()
    for copy in copies:
        copy.wait()


def call(kernel, out_shape, args, scratch=(), flops=0):
    many = isinstance(out_shape, tuple)
    return pl.pallas_call(
        kernel,
        out_shape=out_shape,
        in_specs=[VMEM] * len(args),
        out_specs=(VMEM,) * len(out_shape) if many else VMEM,
        scratch_shapes=list(scratch),
        compiler_params=PARAMS,
        cost_estimate=pl.CostEstimate(flops=flops, bytes_accessed=1 << 20, transcendentals=0),
    )(*args)


def on_device(
    initial_field,
    first_gain,
    first_shift,
    qkv_weight,
    qkv_bias,
    proj_weight,
    proj_bias,
    second_gain,
    second_shift,
    expand_weight,
    expand_bias_row,
    reduce_weight,
    reduce_bias,
    earth_bias,
):
    lat_count = lax.axis_size("lat")
    pairs = [[2 * i, 2 * i + 1] for i in range(lat_count // 2)]
    shape = jax.ShapeDtypeStruct
    weights, tokens = call(
        pack_kernel,
        (shape((304, 384), BF), shape((TOKENS + 288, 256), BF)),
        (
            jnp.swapaxes(qkv_weight, 1, 2),
            jnp.swapaxes(proj_weight, 1, 2),
            expand_weight,
            reduce_weight,
            qkv_bias,
            proj_bias,
            expand_bias_row,
            reduce_bias,
            initial_field.reshape(TOKENS, C),
            earth_bias.reshape(HEADS, -1),
        ),
        [pltpu.VMEM((WZ, 48, SIDE), F32)],
    )
    field = lax.all_gather(tokens, "lat", axis_index_groups=pairs)
    pack = lax.all_gather(weights, "tp")
    gains = (first_gain, first_shift, second_gain, second_shift)
    mats = (
        shape((3 * C, C), BF),
        shape((C, C), BF),
        shape((C, MLP), BF),
        shape((MLP, C), BF),
        shape((3, C), F32),
        shape((3, MLP), F32),
    )
    flops = 2 * 576 * 192 * 192 * 14
    daily, bias, *mats = call(
        first_kernel,
        (shape((2, 288, C), BF), shape((HEADS, WIN, WIN), F32), *mats),
        (field, jnp.asarray(pick_rows()), pack, *gains, jnp.asarray(turn_columns())),
        flops=flops,
    )
    received = lax.ppermute(daily, "section", [(0, 1)])
    states = call(
        second_kernel,
        shape((2, 2, WIN, C), BF),
        (received, daily, jnp.asarray(split_rows()), *gains, bias, *mats),
        [pltpu.VMEM((2, 288, C), BF)],
        flops,
    )
    both = lax.all_gather(states, "lat", axis_index_groups=pairs)
    placed = pl.pallas_call(
        place_kernel,
        out_shape=shape((12, 48, C), BF),
        in_specs=[pl.BlockSpec(memory_space=pl.ANY)],
        out_specs=pl.BlockSpec(memory_space=pl.ANY),
        scratch_shapes=[pltpu.SemaphoreType.DMA((2,))],
        compiler_params=PARAMS,
    )(both.reshape(2, 2, 12, 24, C))
    return placed.reshape(1, 2, 2, 3, 48, C)


def solution(mesh):
    return jax.shard_map(
        on_device,
        mesh=mesh,
        in_specs=(
            P(None, "tp", "lat", None, None),
            P("section", None),
            P("section", None),
            P("section", None, "tp"),
            P("section", "tp"),
            P("section", None, "tp"),
            P("section", "tp"),
            P("section", None),
            P("section", None),
            P("section", None, "tp"),
            P("section", "tp"),
            P("section", "tp", None),
            P("section", "tp"),
            P("section", "tp", "lat", None, None),
        ),
        out_specs=P("section", None, "tp", "lat", None, None),
        check_vma=False,
    )
```

time: 72.9 us -> 54.2 us (0.74)
  blocking collectives: 31.4 us -> 22.4 us
  Pallas kernels: 17.1 us -> 8.6 us
  waiting for transfers between devices: 18 us -> 15.1 us
  local copies, waits for them, and re-layouts: 4.48 us -> 6.3 us
    pallas_call x4 -> x3, Pallas kernels: 17.1 us -> 7.87 us  [call(): pl.pallas_call(kernel, out_shape=out_shape, in_specs=[VMEM] * len(args),...]
    all_gather x3 -> x2, blocking collectives: 23.6 us -> 15.9 us  [the longest x1 13.1 us: on_device(): pack = lax.all_gather(weights, 'tp')]
    ppermute x1, waiting for transfers between devices: 18 us -> 15.1 us  [on_device(): received = lax.ppermute(daily, 'section', [(0, 1)])]
    unnamed x4 -> x33, local copies, waits for them, and re-layouts: 3.78 us -> 6.3 us
    all_gather x1, blocking collectives: 7.77 us -> 6.52 us  [on_device(): both = lax.all_gather(states, 'lat', axis_index_groups=pairs)]
where the time goes in v2:
time: 54.2 us; the launch traced here: 53.8 us
  blocking collectives  22.4 us (41%)
  waiting for transfers between devices  15.1 us (28%)
  Pallas kernels  8.6 us (16%)
  local copies, waits for them, and re-layouts  6.3 us (12%)
  starting transfers between devices  1.29 us (2%)
    ppermute x1, waiting for transfers between devices, on_device(): received = lax.ppermute(daily, 'section', [(0, 1)])  15.1 us
    all_gather x1, blocking collectives, on_device(): pack = lax.all_gather(weights, 'tp')  13.1 us
    pallas_call x3, Pallas kernels, call(): pl.pallas_call(kernel, out_shape=out_shape, in_specs=[VMEM] * len(args),...  7.87 us
    all_gather x1, blocking collectives, on_device(): both = lax.all_gather(states, 'lat', axis_index_groups=pairs)  6.52 us
    unnamed x33, local copies, waits for them, and re-layouts  6.3 us
    all_gather x1, blocking collectives, on_device(): field = lax.all_gather(tokens, 'lat', axis_index_groups=pairs)  2.74 us
    ppermute x1, starting transfers between devices, on_device(): received = lax.ppermute(daily, 'section', [(0, 1)])  1.29 us
  transfers between devices with their start and end apart: 1, of which 1 were waited for; matrix products, arithmetic and copies ran while one was open for 0% of the time, Pallas kernels for 0%

profile of v2, /device:TPU:5, one launch (start us, length us, event | category | flops | bytes accessed | tf_op | source)
XLA Modules:
  0.0 53.8 jit_solution(14416428153664862972)
XLA Ops:
  0.0 0.8 %copy.20 = f32[1,1,1,6,1656]{4,3,2,1,0:T(8,128)S(1)} copy(f32[1,1,1,6,1656]{4,2,3,1,0:T(1,128)} %param.30) | data formatting | bytes 79488
  0.8 0.0 copy-start.12
  0.8 0.0 copy-start.14
  0.8 0.1 copy-done.4
  0.9 0.6 %copy-done.13 = bf16[1,192]{1,0:T(2,128)(2,1)S(1)} copy-done((bf16[1,192]{1,0:T(2,128)(2,1)S(1)}, bf16[1,192]{1,0:T(2,128)(2,1)}, u32[]{:S(2)}) %copy-start.13) | copy-done | bytes 408
  1.5 0.0 copy-done.12
  1.5 1.0 %copy-done.1 = bf16[2,2,3,48,192]{4,3,2,1,0:T(8,128)(2,1)S(1)} copy-done((bf16[2,2,3,48,192]{4,3,2,1,0:T(8,128)(2,1)S(1)}, bf16[2,2,3,48,192]{4,3,2,1,0:T(8,128)(2,1)}, u32[]{:S(2)}) %copy-start.1) | copy-done | bytes 221208
  2.5 0.9 %copy-done.5 = bf16[1,192,192]{2,1,0:T(8,128)(2,1)S(1)} copy-done((bf16[1,192,192]{2,1,0:T(8,128)(2,1)S(1)}, bf16[1,192,192]{2,1,0:T(8,128)(2,1)}, u32[]{:S(2)}) %copy-start.5) | copy-done | bytes 73752
  3.4 0.9 %copy-done.6 = bf16[1,192,144]{1,2,0:T(8,128)(2,1)S(1)} copy-done((bf16[1,192,144]{1,2,0:T(8,128)(2,1)S(1)}, bf16[1,192,144]{1,2,0:T(8,128)(2,1)}, u32[]{:S(2)}) %copy-start.6) | copy-done | bytes 55320
  4.3 0.7 %copy-done.7 = bf16[1,192,48]{1,2,0:T(8,128)(2,1)S(1)} copy-done((bf16[1,192,48]{1,2,0:T(8,128)(2,1)S(1)}, bf16[1,192,48]{1,2,0:T(8,128)(2,1)}, u32[]{:S(2)}) %copy-start.7) | copy-done | bytes 18456
  5.0 0.7 %copy-done.15 = bf16[1,48]{1,0:T(2,128)(2,1)S(1)} copy-done((bf16[1,48]{1,0:T(2,128)(2,1)S(1)}, bf16[1,48]{1,0:T(2,128)(2,1)}, u32[]{:S(2)}) %copy-start.15) | copy-done | bytes 120
  5.7 0.1 shard_map.163
  5.8 2.7 %all-gather = bf16[1728,256]{1,0:T(8,128)(2,1)S(1)} all-gather(bf16[864,256]{1,0:T(8,128)(2,1)S(1)} %get-tuple-element.15), channel_id=2, replica_groups={{0,4},{8,12},{16,20},{24,28},{32,36},{40,44},{48,52},{56,60},{64,68},{7..., dimensions={0}, use_global_device_ids=true | all-gather | bytes 1327104 | tf_op jit(solution)/shard_map/all_gather | solution.py:276
  8.6 13.1 %all-gather.1 = bf16[1216,384]{1,0:T(8,128)(2,1)S(1)} all-gather(bf16[304,384]{1,0:T(8,128)(2,1)S(1)} %get-tuple-element.16), channel_id=3, replica_groups=mesh['section'=2,'lat'=64,'tp'=4] {'tp'}, dimensions={0}, use_global_device_ids=true | all-gather | bytes 1167360 | tf_op jit(solution)/shard_map/all_gather | solution.py:277
  21.7 0.0 copy-done.3
  21.7 0.0 copy-done.9
  21.7 0.0 copy-done.10
  21.8 0.6 %copy-done.8 = bf16[1,192]{1,0:T(2,128)(2,1)S(1)} copy-done((bf16[1,192]{1,0:T(2,128)(2,1)S(1)}, bf16[1,192]{1,0:T(2,128)(2,1)}, u32[]{:S(2)}) %copy-start.8) | copy-done | bytes 408
  22.4 1.2 %shard_map.164 = (bf16[2,288,192]{2,1,0:T(8,128)(2,1)S(1)}, f32[6,144,144]{2,1,0:T(8,128)S(1)}, bf16[576,192]{1,0:T(8,128)(2,1)S(1)}, bf16[192,192]{1,0:T(8,128)...) custom-call(bf16[2,864,256]{2,1,0:T(8,128)(2,1)S(1)} %bitcast.11, ...), custom_call_target="tpu_custom_call" | custom-call | flops 594542592 | bytes 1048576 | tf_op jit(solution)/shard_map/pallas_call | solution.py:229
  23.6 1.3 %collective-permute-start = (bf16[2,288,192]{2,1,0:T(8,128)(2,1)S(1)}, bf16[2,288,192]{2,1,0:T(8,128)(2,1)S(1)}, u32[]{:S(2)}, u32[]{:S(2)}) collective-permute-start(bf16[2,288,192]{2,1,0:T(8,128)(2,1)S(1)} %get-tuple-element.17.own), channel_id=1, source_target_pairs={{0,256},{1,257},{2,258},{3,259},{4,260},{5,261},{6,262},{7,263},{8... | collective-permute-start | bytes 663560 | tf_op jit(solution)/shard_map/ppermute | solution.py:294
  24.9 15.1 %collective-permute-done.received = bf16[2,288,192]{2,1,0:T(8,128)(2,1)S(1)} collective-permute-done((bf16[2,288,192]{2,1,0:T(8,128)(2,1)S(1)}, bf16[2,288,192]{2,1,0:T(8,128)(2,1)S(1)}, u32[]{:S(2)}, u32[]{:S(2)}) %collective-permute-start) | collective-permute-done | bytes 221216 | tf_op jit(solution)/shard_map/ppermute | solution.py:294
  40.0 6.6 %shard_map.165 = bf16[2,2,144,192]{3,2,1,0:T(8,128)(2,1)S(1)} custom-call(bf16[2,288,192]{2,1,0:T(8,128)(2,1)S(1)} %collective-permute-done.received, bf16[2,288,192]{2,1,0:T(8,128)(2,1)S(1)} %get-tuple-element.17.own, bf16[288,288]{1,0:T(8,128)(2,1)S(1)} %copy-done.2, bf16[1,192]{1,0:T(2,128)(2,1)S(1)} %copy-done.8, bf16[1,192]{1,0:T(2,128)(2,1)S(1)} %copy-done.9, ...), custom_call_target="tpu_custom_call" | custom-call | flops 594542592 | bytes 1048576 | tf_op jit(solution)/shard_map/pallas_call | solution.py:229
  46.6 6.5 %all-gather.2 = bf16[4,2,144,192]{3,2,1,0:T(8,128)(2,1)S(1)} all-gather(bf16[2,2,144,192]{3,2,1,0:T(8,128)(2,1)S(1)} %shard_map.165), channel_id=4, replica_groups={{0,4},{8,12},{16,20},{24,28},{32,36},{40,44},{48,52},{56,60},{64,68},{7..., dimensions={0}, use_global_device_ids=true | all-gather | bytes 663552 | tf_op jit(solution)/shard_map/all_gather | solution.py:302
  53.1 0.7 %shard_map.166 = bf16[12,48,192]{2,1,0:T(8,128)(2,1)} custom-call(bf16[2,2,12,24,192]{4,3,2,1,0:T(8,128)(2,1)S(1)} %bitcast.12), custom_call_target="tpu_custom_call" | custom-call | tf_op jit(solution)/shard_map/pallas_call | solution.py:303
  (18 shorter events, 0.0 us)
Async XLA Ops:
  0.0 0.9 %copy-start.4 = (bf16[1,192,192]{2,1,0:T(8,128)(2,1)S(1)}, bf16[1,192,192]{2,1,0:T(8,128)(2,1)}, u32[]{:S(2)}) copy-start(bf16[1,192,192]{2,1,0:T(8,128)(2,1)} %expand.1) | copy-start | bytes 221188
  0.8 0.7 %copy-start.13 = (bf16[1,192]{1,0:T(2,128)(2,1)S(1)}, bf16[1,192]{1,0:T(2,128)(2,1)}, u32[]{:S(2)}) copy-start(bf16[1,192]{1,0:T(2,128)(2,1)} %expand_b.1) | copy-start | bytes 1156
  0.8 0.7 %copy-start.12 = (bf16[1,144]{1,0:T(2,128)(2,1)S(1)}, bf16[1,144]{1,0:T(2,128)(2,1)}, u32[]{:S(2)}) copy-start(bf16[1,144]{1,0:T(2,128)(2,1)} %qkv_b.1) | copy-start | bytes 868
  0.8 0.7 %copy-start.14 = (bf16[1,48]{1,0:T(2,128)(2,1)S(1)}, bf16[1,48]{1,0:T(2,128)(2,1)}, u32[]{:S(2)}) copy-start(bf16[1,48]{1,0:T(2,128)(2,1)} %proj_b.1) | copy-start | bytes 292
  1.5 1.0 %copy-start.1 = (bf16[2,2,3,48,192]{4,3,2,1,0:T(8,128)(2,1)S(1)}, bf16[2,2,3,48,192]{4,3,2,1,0:T(8,128)(2,1)}, u32[]{:S(2)}) copy-start(bf16[2,2,3,48,192]{4,3,2,1,0:T(8,128)(2,1)} %param.17) | copy-start | bytes 663556
  2.5 0.9 %copy-start.5 = (bf16[1,192,192]{2,1,0:T(8,128)(2,1)S(1)}, bf16[1,192,192]{2,1,0:T(8,128)(2,1)}, u32[]{:S(2)}) copy-start(bf16[1,192,192]{2,1,0:T(8,128)(2,1)} %reduce.1) | copy-start | bytes 221188
  3.4 0.9 %copy-start.6 = (bf16[1,192,144]{1,2,0:T(8,128)(2,1)S(1)}, bf16[1,192,144]{1,2,0:T(8,128)(2,1)}, u32[]{:S(2)}) copy-start(bf16[1,192,144]{1,2,0:T(8,128)(2,1)} %param.20) | copy-start | bytes 165892
  4.3 0.7 %copy-start.7 = (bf16[1,192,48]{1,2,0:T(8,128)(2,1)S(1)}, bf16[1,192,48]{1,2,0:T(8,128)(2,1)}, u32[]{:S(2)}) copy-start(bf16[1,192,48]{1,2,0:T(8,128)(2,1)} %param.22) | copy-start | bytes 55300
  5.0 0.7 %copy-start.15 = (bf16[1,48]{1,0:T(2,128)(2,1)S(1)}, bf16[1,48]{1,0:T(2,128)(2,1)}, u32[]{:S(2)}) copy-start(bf16[1,48]{1,0:T(2,128)(2,1)} %reduce_b.1) | copy-start | bytes 292
  8.6 13.2 %copy-start = (bf16[2,288,576]{2,1,0:T(8,128)(2,1)S(1)}, bf16[2,288,576]{2,1,0:T(8,128)(2,1)}, u32[]{:S(2)}) copy-start(bf16[2,288,576]{2,1,0:T(8,128)(2,1)} %constant.6.clone.pick) | copy-start | bytes 1990660
  8.6 13.2 %copy-start.3 = (bf16[276,276]{1,0:T(8,128)(2,1)S(1)}, bf16[276,276]{1,0:T(8,128)(2,1)}, u32[]{:S(2)}) copy-start(bf16[276,276]{1,0:T(8,128)(2,1)} %constant.7.clone.turn) | copy-start | bytes 457060
  8.6 13.2 %copy-start.9 = (bf16[1,192]{1,0:T(2,128)(2,1)S(1)}, bf16[1,192]{1,0:T(2,128)(2,1)}, u32[]{:S(2)}) copy-start(bf16[1,192]{1,0:T(2,128)(2,1)} %s1_.3) | copy-start | bytes 1156
  8.6 13.2 %copy-start.10 = (bf16[1,192]{1,0:T(2,128)(2,1)S(1)}, bf16[1,192]{1,0:T(2,128)(2,1)}, u32[]{:S(2)}) copy-start(bf16[1,192]{1,0:T(2,128)(2,1)} %g2.3) | copy-start | bytes 1156
  8.6 13.2 %copy-start.11 = (bf16[1,192]{1,0:T(2,128)(2,1)S(1)}, bf16[1,192]{1,0:T(2,128)(2,1)}, u32[]{:S(2)}) copy-start(bf16[1,192]{1,0:T(2,128)(2,1)} %s2_.3) | copy-start | bytes 1156
  21.7 0.7 %copy-start.8 = (bf16[1,192]{1,0:T(2,128)(2,1)S(1)}, bf16[1,192]{1,0:T(2,128)(2,1)}, u32[]{:S(2)}) copy-start(bf16[1,192]{1,0:T(2,128)(2,1)} %g1.3) | copy-start | bytes 1156
  22.4 17.6 %copy-start.2 = (bf16[288,288]{1,0:T(8,128)(2,1)S(1)}, bf16[288,288]{1,0:T(8,128)(2,1)}, u32[]{:S(2)}) copy-start(bf16[288,288]{1,0:T(8,128)(2,1)} %constant.8.clone.split) | copy-start | bytes 497668
  23.6 16.4 %collective-permute-start = (bf16[2,288,192]{2,1,0:T(8,128)(2,1)S(1)}, bf16[2,288,192]{2,1,0:T(8,128)(2,1)S(1)}, u32[]{:S(2)}, u32[]{:S(2)}) collective-permute-start(bf16[2,288,192]{2,1,0:T(8,128)(2,1)S(1)} %get-tuple-element.17.own), channel_id=1, source_target_pairs={{0,256},{1,257},{2,258},{3,259},{4,260},{5,261},{6,262},{7,263},{8... | collective-permute-start | bytes 663560 | tf_op jit(solution)/shard_map/ppermute | solution.py:294

commit v3 on v2

--- a/solution.py
+++ b/solution.py
@@ -61,26 +61,71 @@
     return out.astype(BF)
 
 
-def pack_kernel(
-    qkv, proj, expand, reduce, qkv_b, proj_b, expand_b, reduce_b, field, table, weights, tokens, lines
+def load_kernel(
+    qkv,
+    proj,
+    expand,
+    reduce,
+    qkv_b,
+    proj_b,
+    expand_b,
+    reduce_b,
+    field,
+    table,
+    pick,
+    turn,
+    split,
+    g1,
+    s1,
+    g2,
+    s2,
+    weights,
+    tokens,
+    pick_out,
+    turn_out,
+    split_out,
+    gains_out,
+    qkv_v,
+    proj_v,
+    expand_v,
+    reduce_v,
+    qkv_bv,
+    proj_bv,
+    expand_bv,
+    reduce_bv,
+    field_v,
+    table_v,
+    gains_v,
+    lines,
+    sems,
 ):
+    core = lax.rem(lax.axis_index("lat"), 2)
+    moves = [(table.at[h], table_v.at[pl.ds(h, 1), :]) for h in range(HEADS)]
+    moves += [
+        (qkv.at[0], qkv_v),
+        (proj.at[0], proj_v),
+        (expand.at[0], expand_v),
+        (reduce.at[0], reduce_v),
+        (qkv_b, qkv_bv),
+        (proj_b, proj_bv),
+        (expand_b, expand_bv),
+        (reduce_b, reduce_bv),
+        (field, field_v),
+    ]
+    moves += [(ref, gains_v.at[i]) for i, ref in enumerate((g1, s1, g2, s2))]
+    moves += [(pick.at[core], pick_out), (turn, turn_out), (split, split_out)]
+    copies = [pltpu.make_async_copy(a, b, sems.at[i]) for i, (a, b) in enumerate(moves)]
+    for copy in copies:
+        copy.start()
     weights[288:304, :] = jnp.zeros((16, 384), BF)
-    weights[0:144, 0:192] = qkv[0]
-    weights[144:192, 0:192] = proj[0]
-    weights[0:192, 192:384] = expand[0]
-    weights[192:288, 0:192] = reduce[0, 0:96]
-    weights[192:288, 192:384] = reduce[0, 96:192]
-    weights[288:289, 0:144] = qkv_b[...]
-    weights[288:289, 144:192] = proj_b[...]
-    weights[288:289, 192:384] = expand_b[...]
-    weights[289:290, 0:48] = reduce_b[...]
-    tokens[0:TOKENS, 0:C] = field[...]
     lines[...] = jnp.zeros_like(lines)
+    for copy in copies[:HEADS]:
+        copy.wait()
     for zr in range(WZ * HALF):
         z, r = divmod(zr, HALF)
         for zk in range(WZ):
             start = ((z * WZ + zk) * HALF + r) * SIDE
-            lines[zk, 8 * zr : 8 * zr + HEADS, :] = table[:, start : start + SIDE]
+            lines[zk, 8 * zr : 8 * zr + HEADS, :] = table_v[0:HEADS, start : start + SIDE]
     for zk in range(WZ):
         whole = lines[zk]
         high = whole.astype(BF)
@@ -90,6 +135,20 @@
         for i, part in enumerate((high, middle, low)):
             at = TOKENS + 144 * zk + 48 * i
             tokens[at : at + 48, 0:SIDE] = part
+    for copy in copies[HEADS:]:
+        copy.wait()
+    weights[0:144, 0:192] = qkv_v[...]
+    weights[144:192, 0:192] = proj_v[...]
+    weights[0:192, 192:384] = expand_v[...]
+    weights[192:288, 0:192] = reduce_v[0:96, :]
+    weights[192:288, 192:384] = reduce_v[96:192, :]
+    weights[288:289, 0:144] = qkv_bv[...]
+    weights[288:289, 144:192] = proj_bv[...]
+    weights[288:289, 192:384] = expand_bv[...]
+    weights[289:290, 0:48] = reduce_bv[...]
+    tokens[0:TOKENS, 0:C] = field_v[...]
+    for i in range(4):
+        gains_out[i : i + 1, :] = gains_v[i].astype(F32)
 
 
 def norm(x, gain, shift):
@@ -145,69 +204,76 @@
                 bias[:, row, :] = piece[8 * zr : 8 * zr + HEADS, :]
 
 
-def window_block(x, gains, wqkv, wproj, wexp, wred, bqkv, brow, bias):
-    first_gain, first_shift, second_gain, second_shift = gains
-    floats = x.astype(F32)
-    normed = norm(floats, first_gain, first_shift).astype(BF)
-    q, k, v = (
-        (dot_t(normed, wqkv[C * i : C * (i + 1), :]) + bqkv[i : i + 1, :]).astype(BF)
-        for i in range(3)
-    )
+def attend(q, k, v, bias):
     head_of = lax.broadcasted_iota(jnp.int32, (WIN, C), 1) // DIM
     scale = LOG2E / float(np.sqrt(DIM))
-    total = None
     zero = jnp.zeros((WIN, C), BF)
+    stacked = jnp.concatenate([jnp.where(head_of == h, q, zero) for h in range(HEADS)], axis=0)
+    scores = dot_t(stacked, k)
+    probs, inverse = [], []
     for h in range(HEADS):
-        own = head_of == h
-        scores = dot_t(jnp.where(own, q, zero), k) * scale + bias[h]
-        top = jnp.max(scores, axis=-1, keepdims=True)
-        weights = jnp.exp2(scores - top)
-        probs = (weights * (1.0 / jnp.sum(weights, axis=-1, keepdims=True))).astype(BF)
-        part = dot(probs, jnp.where(own, v, zero))
-        total = part if total is None else total + part
-    middle = (floats + dot_t(total.astype(BF), wproj[...]) + brow[1:2, 0:C]).astype(BF)
+        own = scores[WIN * h : WIN * (h + 1)] * scale + bias[h]
+        weights = jnp.exp2(own - jnp.max(own, axis=-1, keepdims=True))
+        inverse.append(1.0 / jnp.sum(weights, axis=-1, keepdims=True))
+        probs.append(weights.astype(BF))
+    values = dot(jnp.concatenate(probs, axis=0), v)
+    total = values[0:WIN] * inverse[0]
+    for h in range(1, HEADS):
+        part = values[WIN * h : WIN * (h + 1)] * inverse[h]
+        total = jnp.where(head_of == h, part, total)
+    return total.astype(BF)
+
+
+def block(x, gains, wqkv, wproj, wexp, wred, bqkv, brow, bias, queries, keys, values, attended):
+    floats = x.astype(F32)
+    normed = norm(floats, gains[0:1, :], gains[1:2, :]).astype(BF)
+    for i, ref in enumerate((queries, keys, values)):
+        ref[...] = (dot_t(normed, wqkv[C * i : C * (i + 1), :]) + bqkv[i : i + 1, :]).astype(BF)
+    for w in range(TOKENS // WIN):
+        rows = slice(WIN * w, WIN * (w + 1))
+        attended[rows, :] = attend(queries[rows, :], keys[rows, :], values[rows, :], bias)
+    middle = (floats + dot_t(attended[...], wproj[...]) + brow[1:2, 0:C]).astype(BF)
     middle_floats = middle.astype(F32)
-    normed_two = norm(middle_floats, second_gain, second_shift).astype(BF)
+    normed_two = norm(middle_floats, gains[2:3, :], gains[3:4, :]).astype(BF)
     pre = dot(normed_two, wexp[...]) + brow[0:1, :]
     hidden = (0.5 * pre * (1.0 + lax.erf(pre * float(np.sqrt(0.5))))).astype(BF)
     return (middle_floats + dot(hidden, wred[...]) + brow[2:3, 0:C]).astype(BF)
 
 
-def first_kernel(field, pick, pack, g1, s1, g2, s2, turn, out, bias, *mats):
+def first_kernel(field, pick, pack, gains, turn, out, bias, *rest):
+    *mats, tokens, queries, keys, values, attended = rest
+    section = lax.axis_index("section")
     assemble(pack, *mats)
     expand_bias(field, turn, bias)
 
-    @pl.when(lax.axis_index("section") == 0)
+    @pl.when(section == 0)
     def _():
-        gains = tuple(ref[...].astype(F32) for ref in (g1, s1, g2, s2))
-        chosen = pick[lax.rem(lax.axis_index("lat"), 2)]
         for t in range(2):
             rows = slice(288 * t, 288 * (t + 1))
             source = jnp.concatenate([field[0, rows, 0:C], field[1, rows, 0:C]], axis=0)
-            tokens = dot(chosen, source).astype(BF)
-            for w in range(2):
-                x = tokens[WIN * w : WIN * (w + 1)]
-                out[t, WIN * w : WIN * (w + 1), :] = window_block(x, gains, *mats, bias)
-
-
-def second_kernel(received, own, split, g1, s1, g2, s2, bias, *rest):
-    *mats, out, hold = rest
+            tokens[rows, :] = dot(pick[...], source).astype(BF)
+        result = block(tokens[...], gains, *mats, bias, queries, keys, values, attended)
+        out[:, 0:C] = result[0:288]
+        out[:, C : 2 * C] = result[288:576]
+
+
+def second_kernel(received, own, split, gains, bias, *rest):
+    *mats, out, hold, tokens, queries, keys, values, attended = rest
     section = lax.axis_index("section")
 
     @pl.when(section == 0)
     def _():
-        hold[...] = own[...]
+        hold[0:288, :] = own[:, 0:C]
+        hold[288:576, :] = own[:, C : 2 * C]
 
     @pl.when(section == 1)
     def _():
-        gains = tuple(ref[...].astype(F32) for ref in (g1, s1, g2, s2))
-        for t in range(2):
-            for w in range(2):
-                rows = slice(WIN * w, WIN * (w + 1))
-                hold[t, rows, :] = window_block(received[t, rows, :], gains, *mats, bias)
+        tokens[0:288, :] = received[:, 0:C]
+        tokens[288:576, :] = received[:, C : 2 * C]
+        hold[...] = block(tokens[...], gains, *mats, bias, queries, keys, values, attended)
 
     for t in range(2):
-        ordered = dot(split[...], hold[t]).astype(BF)
+        ordered = dot(split[...], hold[288 * t : 288 * (t + 1), :]).astype(BF)
         out[0, t] = ordered[0:WIN]
         out[1, t] = ordered[WIN : 2 * WIN]
 
@@ -256,26 +322,57 @@
     lat_count = lax.axis_size("lat")
     pairs = [[2 * i, 2 * i + 1] for i in range(lat_count // 2)]
     shape = jax.ShapeDtypeStruct
-    weights, tokens = call(
-        pack_kernel,
-        (shape((304, 384), BF), shape((TOKENS + 288, 256), BF)),
-        (
-            jnp.swapaxes(qkv_weight, 1, 2),
-            jnp.swapaxes(proj_weight, 1, 2),
-            expand_weight,
-            reduce_weight,
-            qkv_bias,
-            proj_bias,
-            expand_bias_row,
-            reduce_bias,
-            initial_field.reshape(TOKENS, C),
-            earth_bias.reshape(HEADS, -1),
+    hbm = pl.BlockSpec(memory_space=pltpu.HBM)
+    operands = (
+        jnp.swapaxes(qkv_weight, 1, 2),
+        jnp.swapaxes(proj_weight, 1, 2),
+        expand_weight,
+        reduce_weight,
+        qkv_bias,
+        proj_bias,
+        expand_bias_row,
+        reduce_bias,
+        initial_field.reshape(TOKENS, C),
+        earth_bias.reshape(HEADS, 1, -1),
+        jnp.asarray(pick_rows()),
+        jnp.asarray(turn_columns()),
+        jnp.asarray(split_rows()),
+        first_gain,
+        first_shift,
+        second_gain,
+        second_shift,
+    )
+    weights, tokens, pick, turn, split, gains = pl.pallas_call(
+        load_kernel,
+        out_shape=(
+            shape((304, 384), BF),
+            shape((TOKENS + 288, 256), BF),
+            shape((288, TOKENS), BF),
+            shape((LINE, LINE), BF),
+            shape((288, 288), BF),
+            shape((4, C), F32),
         ),
-        [pltpu.VMEM((WZ, 48, SIDE), F32)],
-    )
+        in_specs=[hbm] * len(operands),
+        out_specs=(VMEM,) * 6,
+        scratch_shapes=[
+            pltpu.VMEM((144, C), BF),
+            pltpu.VMEM((48, C), BF),
+            pltpu.VMEM((C, C), BF),
+            pltpu.VMEM((C, C), BF),
+            pltpu.VMEM((1, 144), BF),
+            pltpu.VMEM((1, 48), BF),
+            pltpu.VMEM((1, C), BF),
+            pltpu.VMEM((1, 48), BF),
+            pltpu.VMEM((TOKENS, C), BF),
+            pltpu.VMEM((8, 1656), F32),
+            pltpu.VMEM((4, 1, C), BF),
+            pltpu.VMEM((WZ, 48, SIDE), F32),
+            pltpu.SemaphoreType.DMA((22,)),
+        ],
+        compiler_params=PARAMS,
+    )(*(pltpu.with_memory_space_constraint(x, pltpu.HBM) for x in operands))
     field = lax.all_gather(tokens, "lat", axis_index_groups=pairs)
     pack = lax.all_gather(weights, "tp")
-    gains = (first_gain, first_shift, second_gain, second_shift)
     mats = (
         shape((3 * C, C), BF),
         shape((C, C), BF),
@@ -284,19 +381,21 @@
         shape((3, C), F32),
         shape((3, MLP), F32),
     )
+    stages = [pltpu.VMEM((TOKENS, C), BF)] * 5
     flops = 2 * 576 * 192 * 192 * 14
     daily, bias, *mats = call(
         first_kernel,
-        (shape((2, 288, C), BF), shape((HEADS, WIN, WIN), F32), *mats),
-        (field, jnp.asarray(pick_rows()), pack, *gains, jnp.asarray(turn_columns())),
-        flops=flops,
+        (shape((288, 2 * C), BF), shape((HEADS, WIN, WIN), F32), *mats),
+        (field, pick, pack, gains, turn),
+        stages,
+        flops,
     )
     received = lax.ppermute(daily, "section", [(0, 1)])
     states = call(
         second_kernel,
         shape((2, 2, WIN, C), BF),
-        (received, daily, jnp.asarray(split_rows()), *gains, bias, *mats),
-        [pltpu.VMEM((2, 288, C), BF)],
+        (received, daily, split, gains, bias, *mats),
+        [pltpu.VMEM((TOKENS, C), BF)] + stages,
         flops,
     )
     both = lax.all_gather(states, "lat", axis_index_groups=pairs)

time: 54.2 us -> 42.3 us (0.78)
  local copies, waits for them, and re-layouts: 6.3 us -> 0 us
  waiting for transfers between devices: 15.1 us -> 11.3 us
  Pallas kernels: 8.6 us -> 7.58 us
    unnamed x33 -> x0, local copies, waits for them, and re-layouts: 6.3 us -> none
    ppermute x1, waiting for transfers between devices: 15.1 us -> 11.3 us  [on_device(): received = lax.ppermute(daily, 'section', [(0, 1)])]
    pallas_call x3 -> x2, Pallas kernels: 7.87 us -> 5.05 us  [call(): pl.pallas_call(kernel, out_shape=out_shape, in_specs=[VMEM] * len(args),...]
    pallas_call x0 -> x1, Pallas kernels: none -> 1.81 us  [on_device(): pl.pallas_call(load_kernel, out_shape=(shape((304, 384), BF), shape((TOKE...]
where the time goes in v3:
time: 42.3 us; the launch traced here: 42.1 us
  blocking collectives  21.9 us (52%)
  waiting for transfers between devices  11.3 us (27%)
  Pallas kernels  7.58 us (18%)
  starting transfers between devices  1.29 us (3%)
    all_gather x1, blocking collectives, on_device(): pack = lax.all_gather(weights, 'tp')  13 us
    ppermute x1, waiting for transfers between devices, on_device(): received = lax.ppermute(daily, 'section', [(0, 1)])  11.3 us
    all_gather x1, blocking collectives, on_device(): both = lax.all_gather(states, 'lat', axis_index_groups=pairs)  6.17 us
    pallas_call x2, Pallas kernels, call(): pl.pallas_call(kernel, out_shape=out_shape, in_specs=[VMEM] * len(args),...  5.05 us
    all_gather x1, blocking collectives, on_device(): field = lax.all_gather(tokens, 'lat', axis_index_groups=pairs)  2.74 us
    pallas_call x1, Pallas kernels, on_device(): pl.pallas_call(load_kernel, out_shape=(shape((304, 384), BF), shape((TOKE...  1.81 us
    ppermute x1, starting transfers between devices, on_device(): received = lax.ppermute(daily, 'section', [(0, 1)])  1.29 us
  transfers between devices with their start and end apart: 1, of which 1 were waited for; matrix products, arithmetic and copies ran while one was open for 0% of the time, Pallas kernels for 0%

profile of v3, /device:TPU:5, one launch (start us, length us, event | category | flops | bytes accessed | tf_op | source)
XLA Modules:
  0.0 42.1 jit_solution(13458496779811449334)
XLA Ops:
  0.0 1.8 %shard_map.163 = (bf16[304,384]{1,0:T(8,128)(2,1)S(1)}, bf16[864,256]{1,0:T(8,128)(2,1)S(1)}, bf16[288,576]{1,0:T(8,128)(2,1)S(1)}, bf16[276,276]{1,0:T(8,128)(2...) custom-call(bf16[1,144,192]{2,1,0:T(8,128)(2,1)} %bitcast.12, bf16[1,48,192]{2,1,0:T(8,128)(2,1)} %bitcast.14, ...), custom_call_target="tpu_custom_call" | custom-call | tf_op jit(solution)/shard_map/pallas_call | solution.py:345
  1.8 2.7 %all-gather = bf16[1728,256]{1,0:T(8,128)(2,1)S(1)} all-gather(bf16[864,256]{1,0:T(8,128)(2,1)S(1)} %get-tuple-element.19), channel_id=2, replica_groups={{0,4},{8,12},{16,20},{24,28},{32,36},{40,44},{48,52},{56,60},{64,68},{7..., dimensions={0}, use_global_device_ids=true | all-gather | bytes 1327104 | tf_op jit(solution)/shard_map/all_gather | solution.py:374
  4.6 13.0 %all-gather.1 = bf16[1216,384]{1,0:T(8,128)(2,1)S(1)} all-gather(bf16[304,384]{1,0:T(8,128)(2,1)S(1)} %get-tuple-element.21), channel_id=3, replica_groups=mesh['section'=2,'lat'=64,'tp'=4] {'tp'}, dimensions={0}, use_global_device_ids=true | all-gather | bytes 1167360 | tf_op jit(solution)/shard_map/all_gather | solution.py:375
  17.6 1.2 %shard_map.164 = (bf16[288,384]{1,0:T(8,128)(2,1)S(1)}, f32[6,144,144]{2,1,0:T(8,128)S(1)}, bf16[576,192]{1,0:T(8,128)(2,1)S(1)}, bf16[192,192]{1,0:T(8,128)(2,1...) custom-call(bf16[2,864,256]{2,1,0:T(8,128)(2,1)S(1)} %bitcast.9, ...), custom_call_target="tpu_custom_call" | custom-call | flops 594542592 | bytes 1048576 | tf_op jit(solution)/shard_map/pallas_call | solution.py:295
  18.7 1.3 %collective-permute-start = (bf16[288,384]{1,0:T(8,128)(2,1)S(1)}, bf16[288,384]{1,0:T(8,128)(2,1)S(1)}, u32[]{:S(2)}, u32[]{:S(2)}) collective-permute-start(bf16[288,384]{1,0:T(8,128)(2,1)S(1)} %get-tuple-element.24.own), channel_id=1, source_target_pairs={{0,256},{1,257},{2,258},{3,259},{4,260},{5,261},{6,262},{7,263},{8... | collective-permute-start | bytes 663560 | tf_op jit(solution)/shard_map/ppermute | solution.py:393
  20.0 11.3 %collective-permute-done.received = bf16[288,384]{1,0:T(8,128)(2,1)S(1)} collective-permute-done((bf16[288,384]{1,0:T(8,128)(2,1)S(1)}, bf16[288,384]{1,0:T(8,128)(2,1)S(1)}, u32[]{:S(2)}, u32[]{:S(2)}) %collective-permute-start) | collective-permute-done | bytes 221216 | tf_op jit(solution)/shard_map/ppermute | solution.py:393
  31.3 3.9 %shard_map.165 = bf16[2,2,144,192]{3,2,1,0:T(8,128)(2,1)S(1)} custom-call(bf16[288,384]{1,0:T(8,128)(2,1)S(1)} %collective-permute-done.received, bf16[288,384]{1,0:T(8,128)(2,1)S(1)} %get-tuple-element.24.own, bf16[288,288]{1,0:T(8,128)(2,1)S(1)} %get-tuple-element.25.split, f32[4,192]{1,0:T(4,128)S(1)} %get-tuple-element.22.gains, ...), custom_call_target="tpu_custom_call" | custom-call | flops 594542592 | bytes 1048576 | tf_op jit(solution)/shard_map/pallas_call | solution.py:295
  35.2 6.2 %all-gather.2 = bf16[4,2,144,192]{3,2,1,0:T(8,128)(2,1)S(1)} all-gather(bf16[2,2,144,192]{3,2,1,0:T(8,128)(2,1)S(1)} %shard_map.165), channel_id=4, replica_groups={{0,4},{8,12},{16,20},{24,28},{32,36},{40,44},{48,52},{56,60},{64,68},{7..., dimensions={0}, use_global_device_ids=true | all-gather | bytes 663552 | tf_op jit(solution)/shard_map/all_gather | solution.py:401
  41.4 0.7 %shard_map.166 = bf16[12,48,192]{2,1,0:T(8,128)(2,1)} custom-call(bf16[2,2,12,24,192]{4,3,2,1,0:T(8,128)(2,1)S(1)} %bitcast.10), custom_call_target="tpu_custom_call" | custom-call | tf_op jit(solution)/shard_map/pallas_call | solution.py:402
Async XLA Ops:
  18.7 12.6 %collective-permute-start = (bf16[288,384]{1,0:T(8,128)(2,1)S(1)}, bf16[288,384]{1,0:T(8,128)(2,1)S(1)}, u32[]{:S(2)}, u32[]{:S(2)}) collective-permute-start(bf16[288,384]{1,0:T(8,128)(2,1)S(1)} %get-tuple-element.24.own), channel_id=1, source_target_pairs={{0,256},{1,257},{2,258},{3,259},{4,260},{5,261},{6,262},{7,263},{8... | collective-permute-start | bytes 663560 | tf_op jit(solution)/shard_map/ppermute | solution.py:393

commit v4 on v3

--- a/solution.py
+++ b/solution.py
@@ -29,35 +29,41 @@
 PARAMS = pltpu.CompilerParams(vmem_limit_bytes=20 * 1024 * 1024)
 
 
+def places(core):
+    row = 0
+    for w in range(2):
+        for wl in range(WW):
+            for z in range(WZ):
+                for other in range(2):
+                    for h in range(HALF):
+                        yield row, other, z, h, w * WW + wl
+                        row += 1
+
+
 def pick_rows():
     out = np.zeros((2, 2 * WIN, TOKENS), np.float32)
     for core in range(2):
-        for row in range(2 * WIN):
-            w, rest = divmod(row, WIN)
-            wl, zh = divmod(rest, WZ * WH)
-            z, hh = divmod(zh, WH)
-            half, h = divmod(hh, HALF)
-            lon = (2 * core + w) * WW + wl
-            out[core, row, half * 288 + (z * HALF + h) * 48 + lon] = 1.0
+        for row, other, z, h, lon in places(core):
+            out[core, row, other * 288 + (z * HALF + h) * 48 + 24 * core + lon] = 1.0
     return out.astype(BF)
 
 
 def split_rows():
-    out = np.zeros((2 * WIN, 2 * WIN), np.float32)
-    for row in range(2 * WIN):
-        w, rest = divmod(row, WIN)
-        wl, zh = divmod(rest, WZ * WH)
-        z, hh = divmod(zh, WH)
-        half, h = divmod(hh, HALF)
-        out[((half * WZ + z) * HALF + h) * 24 + w * WW + wl, row] = 1.0
+    out = np.zeros((2, 2 * WIN, 2 * WIN), np.float32)
+    for core in range(2):
+        for row, other, z, h, lon in places(core):
+            out[core, (((core ^ other) * WZ + z) * HALF + h) * 24 + lon, row] = 1.0
     return out.astype(BF)
 
 
 def turn_columns():
-    out = np.zeros((LINE, LINE), np.float32)
-    for key in range(KEYS):
-        for j in range(SPAN):
-            out[key * SPAN + j, (SPAN - 1 - j) * KEYS + key] = 1.0
+    out = np.zeros((2, LINE, LINE), np.float32)
+    for core in range(2):
+        for zk in range(WZ):
+            for hk in range(WH):
+                key = zk * WH + HALF * (core ^ (hk // HALF)) + hk % HALF
+                for j in range(SPAN):
+                    out[core, (zk * WH + hk) * SPAN + j, (SPAN - 1 - j) * KEYS + key] = 1.0
     return out.astype(BF)
 
 
@@ -113,7 +119,7 @@
         (field, field_v),
     ]
     moves += [(ref, gains_v.at[i]) for i, ref in enumerate((g1, s1, g2, s2))]
-    moves += [(pick.at[core], pick_out), (turn, turn_out), (split, split_out)]
+    moves += [(pick.at[core], pick_out), (turn.at[core], turn_out), (split.at[core], split_out)]
     copies = [pltpu.make_async_copy(a, b, sems.at[i]) for i, (a, b) in enumerate(moves)]
     for copy in copies:
         copy.start()
@@ -187,12 +193,12 @@
             at += size
 
 
-def expand_bias(field, turn, bias):
-    for half in range(2):
+def expand_bias(fields, turn, bias):
+    for half, field in enumerate(fields):
         parts = None
         for zk in range(WZ):
             rows = slice(TOKENS + 144 * zk, TOKENS + 144 * (zk + 1))
-            part = dot(field[half, rows, 0:SIDE], turn[SIDE * zk : SIDE * (zk + 1), :])
+            part = dot(field[rows, 0:SIDE], turn[SIDE * zk : SIDE * (zk + 1), :])
             parts = part if parts is None else parts + part
         turned = (parts[0:48] + parts[48:96] + parts[96:144]) * LOG2E
         for wq in range(WW):
@@ -224,58 +230,82 @@
     return total.astype(BF)
 
 
-def block(x, gains, wqkv, wproj, wexp, wred, bqkv, brow, bias, queries, keys, values, attended):
+def block(x, gains, wqkv, wproj, wexp, wred, bqkv, brow, bias):
     floats = x.astype(F32)
     normed = norm(floats, gains[0:1, :], gains[1:2, :]).astype(BF)
-    for i, ref in enumerate((queries, keys, values)):
-        ref[...] = (dot_t(normed, wqkv[C * i : C * (i + 1), :]) + bqkv[i : i + 1, :]).astype(BF)
-    for w in range(TOKENS // WIN):
-        rows = slice(WIN * w, WIN * (w + 1))
-        attended[rows, :] = attend(queries[rows, :], keys[rows, :], values[rows, :], bias)
-    middle = (floats + dot_t(attended[...], wproj[...]) + brow[1:2, 0:C]).astype(BF)
+    q, k, v = (
+        (dot_t(normed, wqkv[C * i : C * (i + 1), :]) + bqkv[i : i + 1, :]).astype(BF)
+        for i in range(3)
+    )
+    windows = (slice(WIN * w, WIN * (w + 1)) for w in range(2))
+    attended = jnp.concatenate([attend(q[rows], k[rows], v[rows], bias) for rows in windows], axis=0)
+    middle = (floats + dot_t(attended, wproj[...]) + brow[1:2, 0:C]).astype(BF)
     middle_floats = middle.astype(F32)
     normed_two = norm(middle_floats, gains[2:3, :], gains[3:4, :]).astype(BF)
-    pre = dot(normed_two, wexp[...]) + brow[0:1, :]
-    hidden = (0.5 * pre * (1.0 + lax.erf(pre * float(np.sqrt(0.5))))).astype(BF)
-    return (middle_floats + dot(hidden, wred[...]) + brow[2:3, 0:C]).astype(BF)
-
-
-def first_kernel(field, pick, pack, gains, turn, out, bias, *rest):
-    *mats, tokens, queries, keys, values, attended = rest
+    total = middle_floats + brow[2:3, 0:C]
+    for at in range(0, MLP, 256):
+        pre = dot(normed_two, wexp[:, at : at + 256]) + brow[0:1, at : at + 256]
+        hidden = (0.5 * pre * (1.0 + lax.erf(pre * float(np.sqrt(0.5))))).astype(BF)
+        total = total + dot(hidden, wred[at : at + 256, :])
+    return total.astype(BF)
+
+
+def daily_block(t, fields, pick, out, *rest):
+    rows = slice(288 * t, 288 * (t + 1))
+    source = jnp.concatenate([field[rows, 0:C] for field in fields], axis=0)
+    result = block(dot(pick[...], source).astype(BF), *rest)
+    out[:, 0:C] = result[0:WIN]
+    out[:, C : 2 * C] = result[WIN : 2 * WIN]
+
+
+def prepare_kernel(own, other, pick, pack, gains, turn, out, bias, *mats):
+    assemble(pack, *mats)
+    expand_bias((own, other), turn, bias)
+
+    @pl.when(lax.axis_index("section") == 0)
+    def _():
+        daily_block(0, (own, other), pick, out, gains, *mats, bias)
+
+
+def daily_kernel(own, other, pick, gains, bias, *rest):
+    *mats, out = rest
+
+    @pl.when(lax.axis_index("section") == 0)
+    def _():
+        daily_block(1, (own, other), pick, out, gains, *mats, bias)
+
+
+def chained_block(received, own, split, gains, bias, mats, hold):
     section = lax.axis_index("section")
-    assemble(pack, *mats)
-    expand_bias(field, turn, bias)
 
     @pl.when(section == 0)
     def _():
-        for t in range(2):
-            rows = slice(288 * t, 288 * (t + 1))
-            source = jnp.concatenate([field[0, rows, 0:C], field[1, rows, 0:C]], axis=0)
-            tokens[rows, :] = dot(pick[...], source).astype(BF)
-        result = block(tokens[...], gains, *mats, bias, queries, keys, values, attended)
-        out[:, 0:C] = result[0:288]
-        out[:, C : 2 * C] = result[288:576]
-
-
-def second_kernel(received, own, split, gains, bias, *rest):
-    *mats, out, hold, tokens, queries, keys, values, attended = rest
-    section = lax.axis_index("section")
-
-    @pl.when(section == 0)
-    def _():
-        hold[0:288, :] = own[:, 0:C]
-        hold[288:576, :] = own[:, C : 2 * C]
+        hold[0:WIN, :] = own[:, 0:C]
+        hold[WIN : 2 * WIN, :] = own[:, C : 2 * C]
 
     @pl.when(section == 1)
     def _():
-        tokens[0:288, :] = received[:, 0:C]
-        tokens[288:576, :] = received[:, C : 2 * C]
-        hold[...] = block(tokens[...], gains, *mats, bias, queries, keys, values, attended)
-
-    for t in range(2):
-        ordered = dot(split[...], hold[288 * t : 288 * (t + 1), :]).astype(BF)
-        out[0, t] = ordered[0:WIN]
-        out[1, t] = ordered[WIN : 2 * WIN]
+        hold[0:WIN, :] = received[:, 0:C]
+        hold[WIN : 2 * WIN, :] = received[:, C : 2 * C]
+        hold[...] = block(hold[...], gains, *mats, bias)
+
+    return dot(split[...], hold[...]).astype(BF)
+
+
+def chained_kernel(received, own, split, gains, bias, *rest):
+    *mats, out, hold = rest
+    ordered = chained_block(received, own, split, gains, bias, mats, hold)
+    out[0] = ordered[0:WIN]
+    out[1] = ordered[WIN : 2 * WIN]
+
+
+def last_kernel(earlier, received, own, split, gains, bias, *rest):
+    *mats, out, hold = rest
+    out[0, 0] = earlier[0]
+    out[1, 0] = earlier[1]
+    ordered = chained_block(received, own, split, gains, bias, mats, hold)
+    out[0, 1] = ordered[0:WIN]
+    out[1, 1] = ordered[WIN : 2 * WIN]
 
 
 def place_kernel(both, out, sems):
@@ -371,7 +401,8 @@
         ],
         compiler_params=PARAMS,
     )(*(pltpu.with_memory_space_constraint(x, pltpu.HBM) for x in operands))
-    field = lax.all_gather(tokens, "lat", axis_index_groups=pairs)
+    swap = [(i, i ^ 1) for i in range(lat_count)]
+    other = lax.ppermute(tokens, "lat", swap)
     pack = lax.all_gather(weights, "tp")
     mats = (
         shape((3 * C, C), BF),
@@ -381,21 +412,33 @@
         shape((3, C), F32),
         shape((3, MLP), F32),
     )
-    stages = [pltpu.VMEM((TOKENS, C), BF)] * 5
-    flops = 2 * 576 * 192 * 192 * 14
-    daily, bias, *mats = call(
-        first_kernel,
-        (shape((288, 2 * C), BF), shape((HEADS, WIN, WIN), F32), *mats),
-        (field, pick, pack, gains, turn),
-        stages,
+    flops = 2 * 288 * 192 * 192 * 14
+    dense = shape((WIN, 2 * C), BF)
+    ahead = [(0, 1)]
+    daily_0, bias, *mats = call(
+        prepare_kernel,
+        (dense, shape((HEADS, WIN, WIN), F32), *mats),
+        (tokens, other, pick, pack, gains, turn),
+        flops=flops,
+    )
+    received_0 = lax.ppermute(daily_0, "section", ahead)
+    daily_1 = call(
+        daily_kernel, dense, (tokens, other, pick, gains, bias, *mats), flops=flops
+    )
+    received_1 = lax.ppermute(daily_1, "section", ahead)
+    hold = [pltpu.VMEM((2 * WIN, C), BF)]
+    earlier = call(
+        chained_kernel,
+        shape((2, WIN, C), BF),
+        (received_0, daily_0, split, gains, bias, *mats),
+        hold,
         flops,
     )
-    received = lax.ppermute(daily, "section", [(0, 1)])
     states = call(
-        second_kernel,
+        last_kernel,
         shape((2, 2, WIN, C), BF),
-        (received, daily, split, gains, bias, *mats),
-        [pltpu.VMEM((TOKENS, C), BF)] + stages,
+        (earlier, received_1, daily_1, split, gains, bias, *mats),
+        hold,
         flops,
     )
     both = lax.all_gather(states, "lat", axis_index_groups=pairs)

time: 42.3 us -> 41.5 us (0.981)
  starting transfers between devices: 1.29 us -> 5.17 us
  blocking collectives: 21.9 us -> 18.2 us
  waiting for transfers between devices: 11.3 us -> 9.7 us
  Pallas kernels: 7.58 us -> 8.14 us
    ppermute x1 -> x3, starting transfers between devices: 1.29 us -> 5.17 us  [the longest x1 2.58 us: on_device(): other = lax.ppermute(tokens, 'lat', swap)]
    all_gather x1 -> x0, blocking collectives: 2.74 us -> none  [on_device(): field = lax.all_gather(tokens, 'lat', axis_index_groups=pairs)]
    ppermute x1 -> x3, waiting for transfers between devices: 11.3 us -> 9.7 us  [the longest x1 8.23 us: on_device(): received_0 = lax.ppermute(daily_0, 'section', ahead)]
    all_gather x1, blocking collectives: 6.17 us -> 4.83 us  [on_device(): both = lax.all_gather(states, 'lat', axis_index_groups=pairs)]
    pallas_call x2 -> x4, Pallas kernels: 5.05 us -> 5.61 us  [call(): pl.pallas_call(kernel, out_shape=out_shape, in_specs=[VMEM] * len(args),...]
  transfers between devices with their start and end apart: 1 -> 3, of which waited for: 1 -> 2; matrix products, arithmetic and copies ran while one was open for 0% -> 0% of each run, Pallas kernels for 0% -> 5%
where the time goes in v4:
time: 41.5 us; the launch traced here: 41.3 us
  blocking collectives  18.2 us (44%)
  waiting for transfers between devices  9.7 us (23%)
  Pallas kernels  8.14 us (20%)
  starting transfers between devices  5.17 us (12%)
    all_gather x1, blocking collectives, on_device(): pack = lax.all_gather(weights, 'tp')  13.4 us
    ppermute x1, waiting for transfers between devices, on_device(): received_0 = lax.ppermute(daily_0, 'section', ahead)  8.23 us
    pallas_call x4, Pallas kernels, call(): pl.pallas_call(kernel, out_shape=out_shape, in_specs=[VMEM] * len(args),...  5.61 us
    all_gather x1, blocking collectives, on_device(): both = lax.all_gather(states, 'lat', axis_index_groups=pairs)  4.83 us
    ppermute x1, starting transfers between devices, on_device(): other = lax.ppermute(tokens, 'lat', swap)  2.58 us
    pallas_call x1, Pallas kernels, on_device(): pl.pallas_call(load_kernel, out_shape=(shape((304, 384), BF), shape((TOKE...  1.81 us
    ppermute x1, waiting for transfers between devices, on_device(): received_1 = lax.ppermute(daily_1, 'section', ahead)  1.48 us
    ppermute x1, starting transfers between devices, on_device(): received_1 = lax.ppermute(daily_1, 'section', ahead)  1.29 us
  transfers between devices with their start and end apart: 3, of which 2 were waited for; matrix products, arithmetic and copies ran while one was open for 0% of the time, Pallas kernels for 5%

profile of v4, /device:TPU:5, one launch (start us, length us, event | category | flops | bytes accessed | tf_op | source)
XLA Modules:
  0.0 41.3 jit_solution(15201635722651102523)
XLA Ops:
  0.0 1.8 %shard_map.163 = (bf16[304,384]{1,0:T(8,128)(2,1)S(1)}, bf16[864,256]{1,0:T(8,128)(2,1)S(1)}, bf16[288,576]{1,0:T(8,128)(2,1)S(1)}, bf16[276,276]{1,0:T(8,128)(2...) custom-call(bf16[1,144,192]{2,1,0:T(8,128)(2,1)} %bitcast.10, bf16[1,48,192]{2,1,0:T(8,128)(2,1)} %bitcast.12, ...), custom_call_target="tpu_custom_call" | custom-call | tf_op jit(solution)/shard_map/pallas_call | solution.py:375
  1.8 2.6 %collective-permute-start = (bf16[864,256]{1,0:T(8,128)(2,1)S(1)}, bf16[864,256]{1,0:T(8,128)(2,1)S(1)}, u32[]{:S(2)}, u32[]{:S(2)}) collective-permute-start(bf16[864,256]{1,0:T(8,128)(2,1)S(1)} %get-tuple-element.19.own), channel_id=1, source_target_pairs={{0,4},{4,0},{8,12},{12,8},{16,20},{20,16},{24,28},{28,24},{32,36},... | collective-permute-start | bytes 1327112 | tf_op jit(solution)/shard_map/ppermute | solution.py:405
  4.4 13.4 %all-gather = bf16[1216,384]{1,0:T(8,128)(2,1)S(1)} all-gather(bf16[304,384]{1,0:T(8,128)(2,1)S(1)} %get-tuple-element.21), channel_id=2, replica_groups=mesh['section'=2,'lat'=64,'tp'=4] {'tp'}, dimensions={0}, use_global_device_ids=true | all-gather | bytes 1167360 | tf_op jit(solution)/shard_map/all_gather | solution.py:406
  17.8 0.0 collective-permute-done.other
  17.8 1.2 %shard_map.164 = (bf16[144,384]{1,0:T(8,128)(2,1)S(1)}, f32[6,144,144]{2,1,0:T(8,128)S(1)}, bf16[576,192]{1,0:T(8,128)(2,1)S(1)}, bf16[192,192]{1,0:T(8,128)(2,1...) custom-call(bf16[864,256]{1,0:T(8,128)(2,1)S(1)} %get-tuple-element., ...), custom_call_target="tpu_custom_call" | custom-call | flops 297271296 | bytes 1048576 | tf_op jit(solution)/shard_map/pallas_call | solution.py:325
  19.0 1.3 %collective-permute-start.1 = (bf16[144,384]{1,0:T(8,128)(2,1)S(1)}, bf16[144,384]{1,0:T(8,128)(2,1)S(1)}, u32[]{:S(2)}, u32[]{:S(2)}) collective-permute-start(bf16[144,384]{1,0:T(8,128)(2,1)S(1)} %get-tuple-element.24.own), channel_id=1, source_target_pairs={{0,256},{1,257},{2,258},{3,259},{4,260},{5,261},{6,262},{7,263},{8... | collective-permute-start | bytes 331784 | tf_op jit(solution)/shard_map/ppermute | solution.py:424
  20.3 1.3 %collective-permute-start.2 = (bf16[144,384]{1,0:T(8,128)(2,1)S(1)}, bf16[144,384]{1,0:T(8,128)(2,1)S(1)}, u32[]{:S(2)}, u32[]{:S(2)}) collective-permute-start(bf16[144,384]{1,0:T(8,128)(2,1)S(1)} %shard_map.166.own), channel_id=1, source_target_pairs={{0,256},{1,257},{2,258},{3,259},{4,260},{5,261},{6,262},{7,263},{8... | collective-permute-start | bytes 331784 | tf_op jit(solution)/shard_map/ppermute | solution.py:428
  21.6 8.2 %collective-permute-done.1.received = bf16[144,384]{1,0:T(8,128)(2,1)S(1)} collective-permute-done((bf16[144,384]{1,0:T(8,128)(2,1)S(1)}, bf16[144,384]{1,0:T(8,128)(2,1)S(1)}, u32[]{:S(2)}, u32[]{:S(2)}) %collective-permute-start.1) | collective-permute-done | bytes 110624 | tf_op jit(solution)/shard_map/ppermute | solution.py:424
  29.9 2.2 %shard_map.165.earlier = bf16[2,144,192]{2,1,0:T(8,128)(2,1)S(1)} custom-call(bf16[144,384]{1,0:T(8,128)(2,1)S(1)} %collective-permute-done.1.received, bf16[144,384]{1,0:T(8,128)(2,1)S(1)} %get-tuple-element.24.own, bf16[288,288]{1,0:T(8,128)(2,1)S(1)} %get-tuple-element.25.split, f32[4,192]{1,0:T(4,128)S(1)} %get-tuple-element.22.gains, ...), custom_call_target="tpu_custom_call" | custom-call | flops 297271296 | bytes 1048576 | tf_op jit(solution)/shard_map/pallas_call | solution.py:325
  32.1 1.5 %collective-permute-done.2.received = bf16[144,384]{1,0:T(8,128)(2,1)S(1)} collective-permute-done((bf16[144,384]{1,0:T(8,128)(2,1)S(1)}, bf16[144,384]{1,0:T(8,128)(2,1)S(1)}, u32[]{:S(2)}, u32[]{:S(2)}) %collective-permute-start.2) | collective-permute-done | bytes 110624 | tf_op jit(solution)/shard_map/ppermute | solution.py:428
  33.5 2.2 %shard_map.167 = bf16[2,2,144,192]{3,2,1,0:T(8,128)(2,1)S(1)} custom-call(bf16[2,144,192]{2,1,0:T(8,128)(2,1)S(1)} %shard_map.165.earlier, bf16[144,384]{1,0:T(8,128)(2,1)S(1)} %collective-permute-done.2.received, bf16[144,384]{1,0:T(8,128)(2,1)S(1)} %shard_map.166.own, bf16[288,288]{1,0:T(8,128)(2,1)S(1)} %get-tuple-element.25.split, ...), custom_call_target="tpu_custom_call" | custom-call | flops 297271296 | bytes 1048576 | tf_op jit(solution)/shard_map/pallas_call | solution.py:325
  35.8 4.8 %all-gather.1 = bf16[4,2,144,192]{3,2,1,0:T(8,128)(2,1)S(1)} all-gather(bf16[2,2,144,192]{3,2,1,0:T(8,128)(2,1)S(1)} %shard_map.167), channel_id=3, replica_groups={{0,4},{8,12},{16,20},{24,28},{32,36},{40,44},{48,52},{56,60},{64,68},{7..., dimensions={0}, use_global_device_ids=true | all-gather | bytes 663552 | tf_op jit(solution)/shard_map/all_gather | solution.py:444
  40.6 0.7 %shard_map.168 = bf16[12,48,192]{2,1,0:T(8,128)(2,1)} custom-call(bf16[2,2,12,24,192]{4,3,2,1,0:T(8,128)(2,1)S(1)} %bitcast.8), custom_call_target="tpu_custom_call" | custom-call | tf_op jit(solution)/shard_map/pallas_call | solution.py:445
  (1 shorter events, 0.0 us)
Async XLA Ops:
  1.8 16.0 %collective-permute-start = (bf16[864,256]{1,0:T(8,128)(2,1)S(1)}, bf16[864,256]{1,0:T(8,128)(2,1)S(1)}, u32[]{:S(2)}, u32[]{:S(2)}) collective-permute-start(bf16[864,256]{1,0:T(8,128)(2,1)S(1)} %get-tuple-element.19.own), channel_id=1, source_target_pairs={{0,4},{4,0},{8,12},{12,8},{16,20},{20,16},{24,28},{28,24},{32,36},... | collective-permute-start | bytes 1327112 | tf_op jit(solution)/shard_map/ppermute | solution.py:405
  19.0 10.9 %collective-permute-start.1 = (bf16[144,384]{1,0:T(8,128)(2,1)S(1)}, bf16[144,384]{1,0:T(8,128)(2,1)S(1)}, u32[]{:S(2)}, u32[]{:S(2)}) collective-permute-start(bf16[144,384]{1,0:T(8,128)(2,1)S(1)} %get-tuple-element.24.own), channel_id=1, source_target_pairs={{0,256},{1,257},{2,258},{3,259},{4,260},{5,261},{6,262},{7,263},{8... | collective-permute-start | bytes 331784 | tf_op jit(solution)/shard_map/ppermute | solution.py:424
  20.3 13.2 %collective-permute-start.2 = (bf16[144,384]{1,0:T(8,128)(2,1)S(1)}, bf16[144,384]{1,0:T(8,128)(2,1)S(1)}, u32[]{:S(2)}, u32[]{:S(2)}) collective-permute-start(bf16[144,384]{1,0:T(8,128)(2,1)S(1)} %shard_map.166.own), channel_id=1, source_target_pairs={{0,256},{1,257},{2,258},{3,259},{4,260},{5,261},{6,262},{7,263},{8... | collective-permute-start | bytes 331784 | tf_op jit(solution)/shard_map/ppermute | solution.py:428

commit v5 on v4

--- a/solution.py
+++ b/solution.py
@@ -22,37 +22,27 @@
 LOG2E = 1.4426950408889634
 BF = jnp.bfloat16
 F32 = jnp.float32
-TOKENS = 576
 SIDE = WH * SPAN
 
 VMEM = pl.BlockSpec(memory_space=pltpu.VMEM)
 PARAMS = pltpu.CompilerParams(vmem_limit_bytes=20 * 1024 * 1024)
 
 
-def places(core):
+def places():
     row = 0
     for w in range(2):
         for wl in range(WW):
-            for z in range(WZ):
-                for other in range(2):
+            for other in range(2):
+                for z in range(WZ):
                     for h in range(HALF):
                         yield row, other, z, h, w * WW + wl
                         row += 1
 
 
 def pick_rows():
-    out = np.zeros((2, 2 * WIN, TOKENS), np.float32)
-    for core in range(2):
-        for row, other, z, h, lon in places(core):
-            out[core, row, other * 288 + (z * HALF + h) * 48 + 24 * core + lon] = 1.0
-    return out.astype(BF)
-
-
-def split_rows():
-    out = np.zeros((2, 2 * WIN, 2 * WIN), np.float32)
-    for core in range(2):
-        for row, other, z, h, lon in places(core):
-            out[core, (((core ^ other) * WZ + z) * HALF + h) * 24 + lon, row] = 1.0
+    out = np.zeros((2 * WIN, 2 * WIN), np.float32)
+    for row, other, z, h, lon in places():
+        out[row, ((other * WZ + z) * HALF + h) * 24 + lon] = 1.0
     return out.astype(BF)
 
 
@@ -61,7 +51,7 @@
     for core in range(2):
         for zk in range(WZ):
             for hk in range(WH):
-                key = zk * WH + HALF * (core ^ (hk // HALF)) + hk % HALF
+                key = ((core ^ (hk // HALF)) * WZ + zk) * HALF + hk % HALF
                 for j in range(SPAN):
                     out[core, (zk * WH + hk) * SPAN + j, (SPAN - 1 - j) * KEYS + key] = 1.0
     return out.astype(BF)
@@ -78,18 +68,13 @@
     reduce_b,
     field,
     table,
-    pick,
-    turn,
-    split,
     g1,
     s1,
     g2,
     s2,
     weights,
-    tokens,
-    pick_out,
-    turn_out,
-    split_out,
+    kept,
+    sent,
     gains_out,
     qkv_v,
     proj_v,
@@ -99,7 +84,8 @@
     proj_bv,
     expand_bv,
     reduce_bv,
-    field_v,
+    kept_v,
+    sent_v,
     table_v,
     gains_v,
     lines,
@@ -116,31 +102,36 @@
         (proj_b, proj_bv),
         (expand_b, expand_bv),
         (reduce_b, reduce_bv),
-        (field, field_v),
+        (field.at[:, pl.ds(pl.multiple_of(24 * core, 8), 24), :], kept_v),
+        (field.at[:, pl.ds(pl.multiple_of(24 - 24 * core, 8), 24), :], sent_v),
     ]
     moves += [(ref, gains_v.at[i]) for i, ref in enumerate((g1, s1, g2, s2))]
-    moves += [(pick.at[core], pick_out), (turn.at[core], turn_out), (split.at[core], split_out)]
     copies = [pltpu.make_async_copy(a, b, sems.at[i]) for i, (a, b) in enumerate(moves)]
     for copy in copies:
         copy.start()
     weights[288:304, :] = jnp.zeros((16, 384), BF)
     lines[...] = jnp.zeros_like(lines)
+    blank = jnp.zeros((HEADS, 256 - SIDE), F32)
     for copy in copies[:HEADS]:
         copy.wait()
     for zr in range(WZ * HALF):
         z, r = divmod(zr, HALF)
         for zk in range(WZ):
             start = ((z * WZ + zk) * HALF + r) * SIDE
-            lines[zk, 8 * zr : 8 * zr + HEADS, :] = table_v[0:HEADS, start : start + SIDE]
+            target = pl.ds(zr, HEADS, stride=8)
+            lines[2 * zk, target, :] = table_v[0:HEADS, start : start + 128]
+            tail = table_v[0:HEADS, start + 128 : start + SIDE]
+            lines[2 * zk + 1, target, :] = jnp.concatenate([tail, blank], axis=1)
     for zk in range(WZ):
-        whole = lines[zk]
+        whole = jnp.concatenate([lines[2 * zk], lines[2 * zk + 1]], axis=1)
         high = whole.astype(BF)
         rest = whole - high.astype(F32)
         middle = rest.astype(BF)
         low = (rest - middle.astype(F32)).astype(BF)
         for i, part in enumerate((high, middle, low)):
-            at = TOKENS + 144 * zk + 48 * i
-            tokens[at : at + 48, 0:SIDE] = part
+            rows = slice(288 + 144 * zk + 48 * i, 288 + 144 * zk + 48 * (i + 1))
+            kept[rows, :] = part
+            sent[rows, :] = part
     for copy in copies[HEADS:]:
         copy.wait()
     weights[0:144, 0:192] = qkv_v[...]
@@ -152,7 +143,8 @@
     weights[288:289, 144:192] = proj_bv[...]
     weights[288:289, 192:384] = expand_bv[...]
     weights[289:290, 0:48] = reduce_bv[...]
-    tokens[0:TOKENS, 0:C] = field_v[...]
+    kept[0:288, 0:C] = kept_v[...].reshape(288, C)
+    sent[0:288, 0:C] = sent_v[...].reshape(288, C)
     for i in range(4):
         gains_out[i : i + 1, :] = gains_v[i].astype(F32)
 
@@ -197,17 +189,16 @@
     for half, field in enumerate(fields):
         parts = None
         for zk in range(WZ):
-            rows = slice(TOKENS + 144 * zk, TOKENS + 144 * (zk + 1))
+            rows = slice(288 + 144 * zk, 288 + 144 * (zk + 1))
             part = dot(field[rows, 0:SIDE], turn[SIDE * zk : SIDE * (zk + 1), :])
             parts = part if parts is None else parts + part
         turned = (parts[0:48] + parts[48:96] + parts[96:144]) * LOG2E
         for wq in range(WW):
             start = KEYS * (WW - 1 - wq)
             piece = turned[:, start : start + WIN]
-            for zr in range(WZ * HALF):
-                z, r = divmod(zr, HALF)
-                row = wq * KEYS + z * WH + half * HALF + r
-                bias[:, row, :] = piece[8 * zr : 8 * zr + HEADS, :]
+            row = wq * KEYS + half * WZ * HALF
+            for h in range(HEADS):
+                bias[h, row : row + WZ * HALF, :] = piece[8 * h : 8 * h + WZ * HALF, :]
 
 
 def attend(q, k, v, bias):
@@ -251,7 +242,7 @@
 
 
 def daily_block(t, fields, pick, out, *rest):
-    rows = slice(288 * t, 288 * (t + 1))
+    rows = slice(WIN * t, WIN * (t + 1))
     source = jnp.concatenate([field[rows, 0:C] for field in fields], axis=0)
     result = block(dot(pick[...], source).astype(BF), *rest)
     out[:, 0:C] = result[0:WIN]
@@ -259,12 +250,19 @@
 
 
 def prepare_kernel(own, other, pick, pack, gains, turn, out, bias, *mats):
-    assemble(pack, *mats)
-    expand_bias((own, other), turn, bias)
-
-    @pl.when(lax.axis_index("section") == 0)
+    section = lax.axis_index("section")
+    turn = turn.at[lax.rem(lax.axis_index("lat"), 2)]
+
+    @pl.when(section == 0)
     def _():
+        assemble(pack, *mats)
+        expand_bias((own, other), turn, bias)
         daily_block(0, (own, other), pick, out, gains, *mats, bias)
+
+    @pl.when(section == 1)
+    def _():
+        assemble(pack, *mats)
+        expand_bias((own, other), turn, bias)
 
 
 def daily_kernel(own, other, pick, gains, bias, *rest):
@@ -289,23 +287,23 @@
         hold[WIN : 2 * WIN, :] = received[:, C : 2 * C]
         hold[...] = block(hold[...], gains, *mats, bias)
 
-    return dot(split[...], hold[...]).astype(BF)
+    ordered = dot(split[...], hold[...]).astype(BF)
+    return ordered[0:WIN], ordered[WIN : 2 * WIN]
 
 
 def chained_kernel(received, own, split, gains, bias, *rest):
     *mats, out, hold = rest
-    ordered = chained_block(received, own, split, gains, bias, mats, hold)
-    out[0] = ordered[0:WIN]
-    out[1] = ordered[WIN : 2 * WIN]
+    out[0], out[1] = chained_block(received, own, split, gains, bias, mats, hold)
 
 
 def last_kernel(earlier, received, own, split, gains, bias, *rest):
     *mats, out, hold = rest
-    out[0, 0] = earlier[0]
-    out[1, 0] = earlier[1]
-    ordered = chained_block(received, own, split, gains, bias, mats, hold)
-    out[0, 1] = ordered[0:WIN]
-    out[1, 1] = ordered[WIN : 2 * WIN]
+    core = lax.rem(lax.axis_index("lat"), 2)
+    halves = chained_block(received, own, split, gains, bias, mats, hold)
+    for other in range(2):
+        half = core if other == 0 else 1 - core
+        out[half, 0] = earlier[other]
+        out[half, 1] = halves[other]
 
 
 def place_kernel(both, out, sems):
@@ -362,28 +360,26 @@
         proj_bias,
         expand_bias_row,
         reduce_bias,
-        initial_field.reshape(TOKENS, C),
+        initial_field.reshape(12, 48, C),
         earth_bias.reshape(HEADS, 1, -1),
-        jnp.asarray(pick_rows()),
-        jnp.asarray(turn_columns()),
-        jnp.asarray(split_rows()),
         first_gain,
         first_shift,
         second_gain,
         second_shift,
     )
-    weights, tokens, pick, turn, split, gains = pl.pallas_call(
+    pick = jnp.asarray(pick_rows())
+    split = jnp.asarray(pick_rows().T)
+    turn = jnp.asarray(turn_columns())
+    weights, kept, sent, gains = pl.pallas_call(
         load_kernel,
         out_shape=(
             shape((304, 384), BF),
-            shape((TOKENS + 288, 256), BF),
-            shape((288, TOKENS), BF),
-            shape((LINE, LINE), BF),
-            shape((288, 288), BF),
+            shape((576, 256), BF),
+            shape((576, 256), BF),
             shape((4, C), F32),
         ),
         in_specs=[hbm] * len(operands),
-        out_specs=(VMEM,) * 6,
+        out_specs=(VMEM,) * 4,
         scratch_shapes=[
             pltpu.VMEM((144, C), BF),
             pltpu.VMEM((48, C), BF),
@@ -393,16 +389,17 @@
             pltpu.VMEM((1, 48), BF),
             pltpu.VMEM((1, C), BF),
             pltpu.VMEM((1, 48), BF),
-            pltpu.VMEM((TOKENS, C), BF),
+            pltpu.VMEM((12, 24, C), BF),
+            pltpu.VMEM((12, 24, C), BF),
             pltpu.VMEM((8, 1656), F32),
             pltpu.VMEM((4, 1, C), BF),
-            pltpu.VMEM((WZ, 48, SIDE), F32),
-            pltpu.SemaphoreType.DMA((22,)),
+            pltpu.VMEM((4, 48, 128), F32),
+            pltpu.SemaphoreType.DMA((20,)),
         ],
         compiler_params=PARAMS,
     )(*(pltpu.with_memory_space_constraint(x, pltpu.HBM) for x in operands))
     swap = [(i, i ^ 1) for i in range(lat_count)]
-    other = lax.ppermute(tokens, "lat", swap)
+    other = lax.ppermute(sent, "lat", swap)
     pack = lax.all_gather(weights, "tp")
     mats = (
         shape((3 * C, C), BF),
@@ -418,12 +415,12 @@
     daily_0, bias, *mats = call(
         prepare_kernel,
         (dense, shape((HEADS, WIN, WIN), F32), *mats),
-        (tokens, other, pick, pack, gains, turn),
+        (kept, other, pick, pack, gains, turn),
         flops=flops,
     )
     received_0 = lax.ppermute(daily_0, "section", ahead)
     daily_1 = call(
-        daily_kernel, dense, (tokens, other, pick, gains, bias, *mats), flops=flops
+        daily_kernel, dense, (kept, other, pick, gains, bias, *mats), flops=flops
     )
     received_1 = lax.ppermute(daily_1, "section", ahead)
     hold = [pltpu.VMEM((2 * WIN, C), BF)]

time: 41.5 us -> 41.2 us (level)
  Pallas kernels: 8.14 us -> 7.38 us
    pallas_call x4, Pallas kernels: 5.61 us -> 5.09 us  [call(): pl.pallas_call(kernel, out_shape=out_shape, in_specs=[VMEM] * len(args),...]
where the time goes in v5:
time: 41.2 us; the launch traced here: 41 us
  blocking collectives  18.4 us (45%)
  waiting for transfers between devices  9.88 us (24%)
  Pallas kernels  7.38 us (18%)
  starting transfers between devices  5.3 us (13%)
    all_gather x1, blocking collectives, on_device(): pack = lax.all_gather(weights, 'tp')  13.5 us
    ppermute x1, waiting for transfers between devices, on_device(): received_0 = lax.ppermute(daily_0, 'section', ahead)  8.46 us
    pallas_call x4, Pallas kernels, call(): pl.pallas_call(kernel, out_shape=out_shape, in_specs=[VMEM] * len(args),...  5.09 us
    all_gather x1, blocking collectives, on_device(): both = lax.all_gather(states, 'lat', axis_index_groups=pairs)  4.82 us
    ppermute x1, starting transfers between devices, on_device(): other = lax.ppermute(sent, 'lat', swap)  2.58 us
    pallas_call x1, Pallas kernels, on_device(): pl.pallas_call(load_kernel, out_shape=(shape((304, 384), BF), shape((576,...  1.56 us
    ppermute x1, starting transfers between devices, on_device(): received_1 = lax.ppermute(daily_1, 'section', ahead)  1.42 us
    ppermute x1, waiting for transfers between devices, on_device(): received_1 = lax.ppermute(daily_1, 'section', ahead)  1.41 us
  transfers between devices with their start and end apart: 3, of which 2 were waited for; matrix products, arithmetic and copies ran while one was open for 0% of the time, Pallas kernels for 5%

profile of v5, /device:TPU:5, one launch (start us, length us, event | category | flops | bytes accessed | tf_op | source)
XLA Modules:
  0.0 41.0 jit_solution(14769345065066166260)
XLA Ops:
  0.0 1.6 %shard_map.163 = (bf16[304,384]{1,0:T(8,128)(2,1)S(1)}, bf16[576,256]{1,0:T(8,128)(2,1)S(1)}, bf16[576,256]{1,0:T(8,128)(2,1)S(1)}, f32[4,192]{1,0:T(4,128)S(1)}) custom-call(bf16[1,144,192]{2,1,0:T(8,128)(2,1)} %bitcast.10, bf16[1,48,192]{2,1,0:T(8,128)(2,1)} %bitcast.12, bf16[1,192,192]{2,1,0:T(8,128)(2,1)} %expand.1, bf16[1,192,192]{2,1,0:T(8,128)(2,1)} %reduce.1, ...), custom_call_target="tpu_custom_call" | custom-call | tf_op jit(solution)/shard_map/pallas_call | solution.py:373
  1.6 2.6 %collective-permute-start = (bf16[576,256]{1,0:T(8,128)(2,1)S(1)}, bf16[576,256]{1,0:T(8,128)(2,1)S(1)}, u32[]{:S(2)}, u32[]{:S(2)}) collective-permute-start(bf16[576,256]{1,0:T(8,128)(2,1)S(1)} %get-tuple-element.18), channel_id=1, source_target_pairs={{0,4},{4,0},{8,12},{12,8},{16,20},{20,16},{24,28},{28,24},{32,36},... | collective-permute-start | bytes 884744 | tf_op jit(solution)/shard_map/ppermute | solution.py:402
  4.2 0.0 copy-start.1
  4.2 0.0 copy-start.2
  4.2 13.5 %all-gather = bf16[1216,384]{1,0:T(8,128)(2,1)S(1)} all-gather(bf16[304,384]{1,0:T(8,128)(2,1)S(1)} %get-tuple-element.19), channel_id=2, replica_groups=mesh['section'=2,'lat'=64,'tp'=4] {'tp'}, dimensions={0}, use_global_device_ids=true | all-gather | bytes 1167360 | tf_op jit(solution)/shard_map/all_gather | solution.py:403
  17.7 0.0 collective-permute-done.other
  17.7 0.0 copy-done.1
  17.7 0.0 copy-done.2
  17.7 0.7 %shard_map.164 = (bf16[144,384]{1,0:T(8,128)(2,1)S(1)}, f32[6,144,144]{2,1,0:T(8,128)S(1)}, bf16[576,192]{1,0:T(8,128)(2,1)S(1)}, bf16[192,192]{1,0:T(8,128)(2,1...) custom-call(bf16[576,256]{1,0:T(8,128)(2,1)S(1)} %get-tuple-element., ...), custom_call_target="tpu_custom_call" | custom-call | flops 297271296 | bytes 1048576 | tf_op jit(solution)/shard_map/pallas_call | solution.py:323
  18.4 1.3 %collective-permute-start.1 = (bf16[144,384]{1,0:T(8,128)(2,1)S(1)}, bf16[144,384]{1,0:T(8,128)(2,1)S(1)}, u32[]{:S(2)}, u32[]{:S(2)}) collective-permute-start(bf16[144,384]{1,0:T(8,128)(2,1)S(1)} %get-tuple-element.21.own), channel_id=1, source_target_pairs={{0,256},{1,257},{2,258},{3,259},{4,260},{5,261},{6,262},{7,263},{8... | collective-permute-start | bytes 331784 | tf_op jit(solution)/shard_map/ppermute | solution.py:421
  19.7 0.0 copy-start
  19.8 1.4 %collective-permute-start.2 = (bf16[144,384]{1,0:T(8,128)(2,1)S(1)}, bf16[144,384]{1,0:T(8,128)(2,1)S(1)}, u32[]{:S(2)}, u32[]{:S(2)}) collective-permute-start(bf16[144,384]{1,0:T(8,128)(2,1)S(1)} %shard_map.166.own), channel_id=1, source_target_pairs={{0,256},{1,257},{2,258},{3,259},{4,260},{5,261},{6,262},{7,263},{8... | collective-permute-start | bytes 331784 | tf_op jit(solution)/shard_map/ppermute | solution.py:425
  21.2 8.5 %collective-permute-done.1.received = bf16[144,384]{1,0:T(8,128)(2,1)S(1)} collective-permute-done((bf16[144,384]{1,0:T(8,128)(2,1)S(1)}, bf16[144,384]{1,0:T(8,128)(2,1)S(1)}, u32[]{:S(2)}, u32[]{:S(2)}) %collective-permute-start.1) | collective-permute-done | bytes 110624 | tf_op jit(solution)/shard_map/ppermute | solution.py:421
  29.6 0.0 copy-done
  29.6 2.2 %shard_map.165.earlier = bf16[2,144,192]{2,1,0:T(8,128)(2,1)S(1)} custom-call(bf16[144,384]{1,0:T(8,128)(2,1)S(1)} %collective-permute-done.1.received, bf16[144,384]{1,0:T(8,128)(2,1)S(1)} %get-tuple-element.21.own, bf16[288,288]{1,0:T(8,128)(2,1)S(1)} %copy-done, f32[4,192]{1,0:T(4,128)S(1)} %get-tuple-element.20.gains, ...), custom_call_target="tpu_custom_call" | custom-call | flops 297271296 | bytes 1048576 | tf_op jit(solution)/shard_map/pallas_call | solution.py:323
  31.9 1.4 %collective-permute-done.2.received = bf16[144,384]{1,0:T(8,128)(2,1)S(1)} collective-permute-done((bf16[144,384]{1,0:T(8,128)(2,1)S(1)}, bf16[144,384]{1,0:T(8,128)(2,1)S(1)}, u32[]{:S(2)}, u32[]{:S(2)}) %collective-permute-start.2) | collective-permute-done | bytes 110624 | tf_op jit(solution)/shard_map/ppermute | solution.py:425
  33.3 2.2 %shard_map.167 = bf16[2,2,144,192]{3,2,1,0:T(8,128)(2,1)S(1)} custom-call(bf16[2,144,192]{2,1,0:T(8,128)(2,1)S(1)} %shard_map.165.earlier, bf16[144,384]{1,0:T(8,128)(2,1)S(1)} %collective-permute-done.2.received, bf16[144,384]{1,0:T(8,128)(2,1)S(1)} %shard_map.166.own, bf16[288,288]{1,0:T(8,128)(2,1)S(1)} %copy-done, f32[4,192]{1,0:T(4,128)S(1)} %get-tuple-element.20.gains, ...), custom_call_target="tpu_custom_call" | custom-call | flops 297271296 | bytes 1048576 | tf_op jit(solution)/shard_map/pallas_call | solution.py:323
  35.5 4.8 %all-gather.1 = bf16[4,2,144,192]{3,2,1,0:T(8,128)(2,1)S(1)} all-gather(bf16[2,2,144,192]{3,2,1,0:T(8,128)(2,1)S(1)} %shard_map.167), channel_id=3, replica_groups={{0,4},{8,12},{16,20},{24,28},{32,36},{40,44},{48,52},{56,60},{64,68},{7..., dimensions={0}, use_global_device_ids=true | all-gather | bytes 663552 | tf_op jit(solution)/shard_map/all_gather | solution.py:441
  40.3 0.7 %shard_map.168 = bf16[12,48,192]{2,1,0:T(8,128)(2,1)} custom-call(bf16[2,2,12,24,192]{4,3,2,1,0:T(8,128)(2,1)S(1)} %bitcast.8), custom_call_target="tpu_custom_call" | custom-call | tf_op jit(solution)/shard_map/pallas_call | solution.py:442
  (1 shorter events, 0.0 us)
Async XLA Ops:
  1.6 16.2 %collective-permute-start = (bf16[576,256]{1,0:T(8,128)(2,1)S(1)}, bf16[576,256]{1,0:T(8,128)(2,1)S(1)}, u32[]{:S(2)}, u32[]{:S(2)}) collective-permute-start(bf16[576,256]{1,0:T(8,128)(2,1)S(1)} %get-tuple-element.18), channel_id=1, source_target_pairs={{0,4},{4,0},{8,12},{12,8},{16,20},{20,16},{24,28},{28,24},{32,36},... | collective-permute-start | bytes 884744 | tf_op jit(solution)/shard_map/ppermute | solution.py:402
  4.2 13.6 %copy-start.1 = (bf16[288,288]{1,0:T(8,128)(2,1)S(1)}, bf16[288,288]{1,0:T(8,128)(2,1)}, u32[]{:S(2)}) copy-start(bf16[288,288]{1,0:T(8,128)(2,1)} %constant.6.clone.pick) | copy-start | bytes 497668
  4.2 13.6 %copy-start.2 = (bf16[2,276,276]{2,1,0:T(8,128)(2,1)S(1)}, bf16[2,276,276]{2,1,0:T(8,128)(2,1)}, u32[]{:S(2)}) copy-start(bf16[2,276,276]{2,1,0:T(8,128)(2,1)} %constant.8.clone.turn) | copy-start | bytes 914116
  18.4 11.2 %collective-permute-start.1 = (bf16[144,384]{1,0:T(8,128)(2,1)S(1)}, bf16[144,384]{1,0:T(8,128)(2,1)S(1)}, u32[]{:S(2)}, u32[]{:S(2)}) collective-permute-start(bf16[144,384]{1,0:T(8,128)(2,1)S(1)} %get-tuple-element.21.own), channel_id=1, source_target_pairs={{0,256},{1,257},{2,258},{3,259},{4,260},{5,261},{6,262},{7,263},{8... | collective-permute-start | bytes 331784 | tf_op jit(solution)/shard_map/ppermute | solution.py:421
  19.7 9.9 %copy-start = (bf16[288,288]{1,0:T(8,128)(2,1)S(1)}, bf16[288,288]{1,0:T(8,128)(2,1)}, u32[]{:S(2)}) copy-start(bf16[288,288]{1,0:T(8,128)(2,1)} %constant.7.clone.split) | copy-start | bytes 497668
  19.8 13.5 %collective-permute-start.2 = (bf16[144,384]{1,0:T(8,128)(2,1)S(1)}, bf16[144,384]{1,0:T(8,128)(2,1)S(1)}, u32[]{:S(2)}, u32[]{:S(2)}) collective-permute-start(bf16[144,384]{1,0:T(8,128)(2,1)S(1)} %shard_map.166.own), channel_id=1, source_target_pairs={{0,256},{1,257},{2,258},{3,259},{4,260},{5,261},{6,262},{7,263},{8... | collective-permute-start | bytes 331784 | tf_op jit(solution)/shard_map/ppermute | solution.py:425

commit v6 on v5

--- a/solution.py
+++ b/solution.py
@@ -228,7 +228,7 @@
         (dot_t(normed, wqkv[C * i : C * (i + 1), :]) + bqkv[i : i + 1, :]).astype(BF)
         for i in range(3)
     )
-    windows = (slice(WIN * w, WIN * (w + 1)) for w in range(2))
+    windows = (slice(at, at + WIN) for at in range(0, x.shape[0], WIN))
     attended = jnp.concatenate([attend(q[rows], k[rows], v[rows], bias) for rows in windows], axis=0)
     middle = (floats + dot_t(attended, wproj[...]) + brow[1:2, 0:C]).astype(BF)
     middle_floats = middle.astype(F32)
@@ -241,69 +241,43 @@
     return total.astype(BF)
 
 
-def daily_block(t, fields, pick, out, *rest):
-    rows = slice(WIN * t, WIN * (t + 1))
-    source = jnp.concatenate([field[rows, 0:C] for field in fields], axis=0)
-    result = block(dot(pick[...], source).astype(BF), *rest)
-    out[:, 0:C] = result[0:WIN]
-    out[:, C : 2 * C] = result[WIN : 2 * WIN]
-
-
-def prepare_kernel(own, other, pick, pack, gains, turn, out, bias, *mats):
+def daily_kernel(own, other, pick, pack, gains, turn, out, bias, *mats):
+    assemble(pack, *mats)
+    expand_bias((own, other), turn.at[lax.rem(lax.axis_index("lat"), 2)], bias)
+
+    @pl.when(lax.axis_index("section") == 0)
+    def _():
+        tokens = []
+        for t in range(2):
+            rows = slice(WIN * t, WIN * (t + 1))
+            source = jnp.concatenate([own[rows, 0:C], other[rows, 0:C]], axis=0)
+            tokens.append(dot(pick[...], source).astype(BF))
+        result = block(jnp.concatenate(tokens, axis=0), gains, *mats, bias)
+        out[:, 0:C] = result[0 : 2 * WIN]
+        out[:, C : 2 * C] = result[2 * WIN : 4 * WIN]
+
+
+def chained_kernel(received, own, split, gains, bias, *rest):
+    *mats, out, hold = rest
     section = lax.axis_index("section")
-    turn = turn.at[lax.rem(lax.axis_index("lat"), 2)]
+    core = lax.rem(lax.axis_index("lat"), 2)
 
     @pl.when(section == 0)
     def _():
-        assemble(pack, *mats)
-        expand_bias((own, other), turn, bias)
-        daily_block(0, (own, other), pick, out, gains, *mats, bias)
+        hold[0, ...] = own[:, 0:C]
+        hold[1, ...] = own[:, C : 2 * C]
 
     @pl.when(section == 1)
     def _():
-        assemble(pack, *mats)
-        expand_bias((own, other), turn, bias)
-
-
-def daily_kernel(own, other, pick, gains, bias, *rest):
-    *mats, out = rest
-
-    @pl.when(lax.axis_index("section") == 0)
-    def _():
-        daily_block(1, (own, other), pick, out, gains, *mats, bias)
-
-
-def chained_block(received, own, split, gains, bias, mats, hold):
-    section = lax.axis_index("section")
-
-    @pl.when(section == 0)
-    def _():
-        hold[0:WIN, :] = own[:, 0:C]
-        hold[WIN : 2 * WIN, :] = own[:, C : 2 * C]
-
-    @pl.when(section == 1)
-    def _():
-        hold[0:WIN, :] = received[:, 0:C]
-        hold[WIN : 2 * WIN, :] = received[:, C : 2 * C]
-        hold[...] = block(hold[...], gains, *mats, bias)
-
-    ordered = dot(split[...], hold[...]).astype(BF)
-    return ordered[0:WIN], ordered[WIN : 2 * WIN]
-
-
-def chained_kernel(received, own, split, gains, bias, *rest):
-    *mats, out, hold = rest
-    out[0], out[1] = chained_block(received, own, split, gains, bias, mats, hold)
-
-
-def last_kernel(earlier, received, own, split, gains, bias, *rest):
-    *mats, out, hold = rest
-    core = lax.rem(lax.axis_index("lat"), 2)
-    halves = chained_block(received, own, split, gains, bias, mats, hold)
-    for other in range(2):
-        half = core if other == 0 else 1 - core
-        out[half, 0] = earlier[other]
-        out[half, 1] = halves[other]
+        x = jnp.concatenate([received[:, 0:C], received[:, C : 2 * C]], axis=0)
+        result = block(x, gains, *mats, bias)
+        hold[0, ...] = result[0 : 2 * WIN]
+        hold[1, ...] = result[2 * WIN : 4 * WIN]
+
+    for t in range(2):
+        ordered = dot(split[...], hold[t]).astype(BF)
+        out[core, t] = ordered[0:WIN]
+        out[1 - core, t] = ordered[WIN : 2 * WIN]
 
 
 def place_kernel(both, out, sems):
@@ -409,33 +383,19 @@
         shape((3, C), F32),
         shape((3, MLP), F32),
     )
-    flops = 2 * 288 * 192 * 192 * 14
-    dense = shape((WIN, 2 * C), BF)
-    ahead = [(0, 1)]
-    daily_0, bias, *mats = call(
-        prepare_kernel,
-        (dense, shape((HEADS, WIN, WIN), F32), *mats),
+    flops = 2 * 576 * 192 * 192 * 14
+    daily, bias, *mats = call(
+        daily_kernel,
+        (shape((2 * WIN, 2 * C), BF), shape((HEADS, WIN, WIN), F32), *mats),
         (kept, other, pick, pack, gains, turn),
         flops=flops,
     )
-    received_0 = lax.ppermute(daily_0, "section", ahead)
-    daily_1 = call(
-        daily_kernel, dense, (kept, other, pick, gains, bias, *mats), flops=flops
-    )
-    received_1 = lax.ppermute(daily_1, "section", ahead)
-    hold = [pltpu.VMEM((2 * WIN, C), BF)]
-    earlier = call(
+    received = lax.ppermute(daily, "section", [(0, 1)])
+    states = call(
         chained_kernel,
-        shape((2, WIN, C), BF),
-        (received_0, daily_0, split, gains, bias, *mats),
-        hold,
-        flops,
-    )
-    states = call(
-        last_kernel,
         shape((2, 2, WIN, C), BF),
-        (earlier, received_1, daily_1, split, gains, bias, *mats),
-        hold,
+        (received, daily, split, gains, bias, *mats),
+        [pltpu.VMEM((2, 2 * WIN, C), BF)],
         flops,
     )
     both = lax.all_gather(states, "lat", axis_index_groups=pairs)

time: 41.2 us -> 40.7 us (0.988)
  waiting for transfers between devices: 9.88 us -> 11.9 us
  starting transfers between devices: 5.3 us -> 3.88 us
  Pallas kernels: 7.38 us -> 6.51 us
    ppermute x2 -> x1, waiting for transfers between devices: 9.87 us -> 11.9 us  [on_device(): received = lax.ppermute(daily, 'section', [(0, 1)])]
    ppermute x2 -> x1, starting transfers between devices: 2.72 us -> 1.29 us  [on_device(): received = lax.ppermute(daily, 'section', [(0, 1)])]
    pallas_call x4 -> x2, Pallas kernels: 5.09 us -> 4.23 us  [call(): pl.pallas_call(kernel, out_shape=out_shape, in_specs=[VMEM] * len(args),...]
  transfers between devices with their start and end apart: 3 -> 2, of which waited for: 2 -> 1; matrix products, arithmetic and copies ran while one was open for 0% -> 0% of each run, Pallas kernels for 5% -> 0%
where the time goes in v6:
time: 40.7 us; the launch traced here: 40.5 us
  blocking collectives  18.1 us (44%)
  waiting for transfers between devices  11.9 us (29%)
  Pallas kernels  6.51 us (16%)
  starting transfers between devices  3.88 us (10%)
    all_gather x1, blocking collectives, on_device(): pack = lax.all_gather(weights, 'tp')  13.5 us
    ppermute x1, waiting for transfers between devices, on_device(): received = lax.ppermute(daily, 'section', [(0, 1)])  11.9 us
    all_gather x1, blocking collectives, on_device(): both = lax.all_gather(states, 'lat', axis_index_groups=pairs)  4.57 us
    pallas_call x2, Pallas kernels, call(): pl.pallas_call(kernel, out_shape=out_shape, in_specs=[VMEM] * len(args),...  4.23 us
    ppermute x1, starting transfers between devices, on_device(): other = lax.ppermute(sent, 'lat', swap)  2.58 us
    pallas_call x1, Pallas kernels, on_device(): pl.pallas_call(load_kernel, out_shape=(shape((304, 384), BF), shape((576,...  1.56 us
    ppermute x1, starting transfers between devices, on_device(): received = lax.ppermute(daily, 'section', [(0, 1)])  1.29 us
  transfers between devices with their start and end apart: 2, of which 1 were waited for; matrix products, arithmetic and copies ran while one was open for 0% of the time, Pallas kernels for 0%

profile of v6, /device:TPU:5, one launch (start us, length us, event | category | flops | bytes accessed | tf_op | source)
XLA Modules:
  0.0 40.5 jit_solution(11648805161808348406)
XLA Ops:
  0.0 1.6 %shard_map.163 = (bf16[304,384]{1,0:T(8,128)(2,1)S(1)}, bf16[576,256]{1,0:T(8,128)(2,1)S(1)}, bf16[576,256]{1,0:T(8,128)(2,1)S(1)}, f32[4,192]{1,0:T(4,128)S(1)}) custom-call(bf16[1,144,192]{2,1,0:T(8,128)(2,1)} %bitcast.10, bf16[1,48,192]{2,1,0:T(8,128)(2,1)} %bitcast.12, bf16[1,192,192]{2,1,0:T(8,128)(2,1)} %expand.1, bf16[1,192,192]{2,1,0:T(8,128)(2,1)} %reduce.1, ...), custom_call_target="tpu_custom_call" | custom-call | tf_op jit(solution)/shard_map/pallas_call | solution.py:347
  1.6 2.6 %collective-permute-start = (bf16[576,256]{1,0:T(8,128)(2,1)S(1)}, bf16[576,256]{1,0:T(8,128)(2,1)S(1)}, u32[]{:S(2)}, u32[]{:S(2)}) collective-permute-start(bf16[576,256]{1,0:T(8,128)(2,1)S(1)} %get-tuple-element.18), channel_id=1, source_target_pairs={{0,4},{4,0},{8,12},{12,8},{16,20},{20,16},{24,28},{28,24},{32,36},... | collective-permute-start | bytes 884744 | tf_op jit(solution)/shard_map/ppermute | solution.py:376
  4.2 0.0 copy-start.1
  4.2 0.0 copy-start.2
  4.2 13.5 %all-gather = bf16[1216,384]{1,0:T(8,128)(2,1)S(1)} all-gather(bf16[304,384]{1,0:T(8,128)(2,1)S(1)} %get-tuple-element.19), channel_id=2, replica_groups=mesh['section'=2,'lat'=64,'tp'=4] {'tp'}, dimensions={0}, use_global_device_ids=true | all-gather | bytes 1167360 | tf_op jit(solution)/shard_map/all_gather | solution.py:377
  17.7 0.0 collective-permute-done.other
  17.7 0.0 copy-done.1
  17.7 0.0 copy-done.2
  17.7 0.0 copy-start
  17.7 0.7 %shard_map.164 = (bf16[288,384]{1,0:T(8,128)(2,1)S(1)}, f32[6,144,144]{2,1,0:T(8,128)S(1)}, bf16[576,192]{1,0:T(8,128)(2,1)S(1)}, bf16[192,192]{1,0:T(8,128)(2,1...) custom-call(bf16[576,256]{1,0:T(8,128)(2,1)S(1)} %get-tuple-element., ...), custom_call_target="tpu_custom_call" | custom-call | flops 594542592 | bytes 1048576 | tf_op jit(solution)/shard_map/pallas_call | solution.py:297
  18.4 1.3 %collective-permute-start.1 = (bf16[288,384]{1,0:T(8,128)(2,1)S(1)}, bf16[288,384]{1,0:T(8,128)(2,1)S(1)}, u32[]{:S(2)}, u32[]{:S(2)}) collective-permute-start(bf16[288,384]{1,0:T(8,128)(2,1)S(1)} %get-tuple-element.21.own), channel_id=1, source_target_pairs={{0,256},{1,257},{2,258},{3,259},{4,260},{5,261},{6,262},{7,263},{8... | collective-permute-start | bytes 663560 | tf_op jit(solution)/shard_map/ppermute | solution.py:393
  19.7 11.9 %collective-permute-done.1.received = bf16[288,384]{1,0:T(8,128)(2,1)S(1)} collective-permute-done((bf16[288,384]{1,0:T(8,128)(2,1)S(1)}, bf16[288,384]{1,0:T(8,128)(2,1)S(1)}, u32[]{:S(2)}, u32[]{:S(2)}) %collective-permute-start.1) | collective-permute-done | bytes 221216 | tf_op jit(solution)/shard_map/ppermute | solution.py:393
  31.7 0.0 copy-done
  31.7 3.6 %shard_map.165 = bf16[2,2,144,192]{3,2,1,0:T(8,128)(2,1)S(1)} custom-call(bf16[288,384]{1,0:T(8,128)(2,1)S(1)} %collective-permute-done.1.received, bf16[288,384]{1,0:T(8,128)(2,1)S(1)} %get-tuple-element.21.own, bf16[288,288]{1,0:T(8,128)(2,1)S(1)} %copy-done, f32[4,192]{1,0:T(4,128)S(1)} %get-tuple-element.20.gains, ...), custom_call_target="tpu_custom_call" | custom-call | flops 594542592 | bytes 1048576 | tf_op jit(solution)/shard_map/pallas_call | solution.py:297
  35.2 4.6 %all-gather.1 = bf16[4,2,144,192]{3,2,1,0:T(8,128)(2,1)S(1)} all-gather(bf16[2,2,144,192]{3,2,1,0:T(8,128)(2,1)S(1)} %shard_map.165), channel_id=3, replica_groups={{0,4},{8,12},{16,20},{24,28},{32,36},{40,44},{48,52},{56,60},{64,68},{7..., dimensions={0}, use_global_device_ids=true | all-gather | bytes 663552 | tf_op jit(solution)/shard_map/all_gather | solution.py:401
  39.8 0.7 %shard_map.166 = bf16[12,48,192]{2,1,0:T(8,128)(2,1)} custom-call(bf16[2,2,12,24,192]{4,3,2,1,0:T(8,128)(2,1)S(1)} %bitcast.7), custom_call_target="tpu_custom_call" | custom-call | tf_op jit(solution)/shard_map/pallas_call | solution.py:402
Async XLA Ops:
  1.6 16.2 %collective-permute-start = (bf16[576,256]{1,0:T(8,128)(2,1)S(1)}, bf16[576,256]{1,0:T(8,128)(2,1)S(1)}, u32[]{:S(2)}, u32[]{:S(2)}) collective-permute-start(bf16[576,256]{1,0:T(8,128)(2,1)S(1)} %get-tuple-element.18), channel_id=1, source_target_pairs={{0,4},{4,0},{8,12},{12,8},{16,20},{20,16},{24,28},{28,24},{32,36},... | collective-permute-start | bytes 884744 | tf_op jit(solution)/shard_map/ppermute | solution.py:376
  4.2 13.6 %copy-start.1 = (bf16[2,276,276]{2,1,0:T(8,128)(2,1)S(1)}, bf16[2,276,276]{2,1,0:T(8,128)(2,1)}, u32[]{:S(2)}) copy-start(bf16[2,276,276]{2,1,0:T(8,128)(2,1)} %constant.8.clone.turn) | copy-start | bytes 914116
  4.2 13.6 %copy-start.2 = (bf16[288,288]{1,0:T(8,128)(2,1)S(1)}, bf16[288,288]{1,0:T(8,128)(2,1)}, u32[]{:S(2)}) copy-start(bf16[288,288]{1,0:T(8,128)(2,1)} %constant.6.clone.pick) | copy-start | bytes 497668
  17.7 13.9 %copy-start = (bf16[288,288]{1,0:T(8,128)(2,1)S(1)}, bf16[288,288]{1,0:T(8,128)(2,1)}, u32[]{:S(2)}) copy-start(bf16[288,288]{1,0:T(8,128)(2,1)} %constant.7.clone.split) | copy-start | bytes 497668
  18.4 13.2 %collective-permute-start.1 = (bf16[288,384]{1,0:T(8,128)(2,1)S(1)}, bf16[288,384]{1,0:T(8,128)(2,1)S(1)}, u32[]{:S(2)}, u32[]{:S(2)}) collective-permute-start(bf16[288,384]{1,0:T(8,128)(2,1)S(1)} %get-tuple-element.21.own), channel_id=1, source_target_pairs={{0,256},{1,257},{2,258},{3,259},{4,260},{5,261},{6,262},{7,263},{8... | collective-permute-start | bytes 663560 | tf_op jit(solution)/shard_map/ppermute | solution.py:393

commit v7 on v6

--- a/solution.py
+++ b/solution.py
@@ -94,16 +94,16 @@
     core = lax.rem(lax.axis_index("lat"), 2)
     moves = [(table.at[h], table_v.at[pl.ds(h, 1), :]) for h in range(HEADS)]
     moves += [
+        (field.at[:, pl.ds(pl.multiple_of(24 * core, 8), 24), :], kept_v),
+        (field.at[:, pl.ds(pl.multiple_of(24 - 24 * core, 8), 24), :], sent_v),
+        (expand.at[0], expand_v),
+        (reduce.at[0], reduce_v),
         (qkv.at[0], qkv_v),
         (proj.at[0], proj_v),
-        (expand.at[0], expand_v),
-        (reduce.at[0], reduce_v),
         (qkv_b, qkv_bv),
         (proj_b, proj_bv),
         (expand_b, expand_bv),
         (reduce_b, reduce_bv),
-        (field.at[:, pl.ds(pl.multiple_of(24 * core, 8), 24), :], kept_v),
-        (field.at[:, pl.ds(pl.multiple_of(24 - 24 * core, 8), 24), :], sent_v),
     ]
     moves += [(ref, gains_v.at[i]) for i, ref in enumerate((g1, s1, g2, s2))]
     copies = [pltpu.make_async_copy(a, b, sems.at[i]) for i, (a, b) in enumerate(moves)]
@@ -132,19 +132,26 @@
             rows = slice(288 + 144 * zk + 48 * i, 288 + 144 * zk + 48 * (i + 1))
             kept[rows, :] = part
             sent[rows, :] = part
-    for copy in copies[HEADS:]:
-        copy.wait()
-    weights[0:144, 0:192] = qkv_v[...]
-    weights[144:192, 0:192] = proj_v[...]
+    arrived = iter(copies[HEADS:])
+    next(arrived).wait()
+    kept[0:288, 0:C] = kept_v[...].reshape(288, C)
+    next(arrived).wait()
+    sent[0:288, 0:C] = sent_v[...].reshape(288, C)
+    next(arrived).wait()
     weights[0:192, 192:384] = expand_v[...]
+    next(arrived).wait()
     weights[192:288, 0:192] = reduce_v[0:96, :]
     weights[192:288, 192:384] = reduce_v[96:192, :]
+    next(arrived).wait()
+    weights[0:144, 0:192] = qkv_v[...]
+    next(arrived).wait()
+    weights[144:192, 0:192] = proj_v[...]
+    for copy in arrived:
+        copy.wait()
     weights[288:289, 0:144] = qkv_bv[...]
     weights[288:289, 144:192] = proj_bv[...]
     weights[288:289, 192:384] = expand_bv[...]
     weights[289:290, 0:48] = reduce_bv[...]
-    kept[0:288, 0:C] = kept_v[...].reshape(288, C)
-    sent[0:288, 0:C] = sent_v[...].reshape(288, C)
     for i in range(4):
         gains_out[i : i + 1, :] = gains_v[i].astype(F32)
 
@@ -241,7 +248,7 @@
     return total.astype(BF)
 
 
-def daily_kernel(own, other, pick, pack, gains, turn, out, bias, *mats):
+def daily_kernel(own, other, pick, pack, gains, turn, out_0, out_1, bias, *mats):
     assemble(pack, *mats)
     expand_bias((own, other), turn.at[lax.rem(lax.axis_index("lat"), 2)], bias)
 
@@ -253,31 +260,40 @@
             source = jnp.concatenate([own[rows, 0:C], other[rows, 0:C]], axis=0)
             tokens.append(dot(pick[...], source).astype(BF))
         result = block(jnp.concatenate(tokens, axis=0), gains, *mats, bias)
-        out[:, 0:C] = result[0 : 2 * WIN]
-        out[:, C : 2 * C] = result[2 * WIN : 4 * WIN]
-
-
-def chained_kernel(received, own, split, gains, bias, *rest):
-    *mats, out, hold = rest
+        for w, (out, side) in enumerate(((out_0, 0), (out_0, C), (out_1, 0), (out_1, C))):
+            out[:, side : side + C] = result[WIN * w : WIN * (w + 1)]
+
+
+def chained_block(received, own, split, gains, bias, mats, hold):
     section = lax.axis_index("section")
-    core = lax.rem(lax.axis_index("lat"), 2)
 
     @pl.when(section == 0)
     def _():
-        hold[0, ...] = own[:, 0:C]
-        hold[1, ...] = own[:, C : 2 * C]
+        hold[0:WIN, :] = own[:, 0:C]
+        hold[WIN : 2 * WIN, :] = own[:, C : 2 * C]
 
     @pl.when(section == 1)
     def _():
         x = jnp.concatenate([received[:, 0:C], received[:, C : 2 * C]], axis=0)
-        result = block(x, gains, *mats, bias)
-        hold[0, ...] = result[0 : 2 * WIN]
-        hold[1, ...] = result[2 * WIN : 4 * WIN]
-
-    for t in range(2):
-        ordered = dot(split[...], hold[t]).astype(BF)
-        out[core, t] = ordered[0:WIN]
-        out[1 - core, t] = ordered[WIN : 2 * WIN]
+        hold[...] = block(x, gains, *mats, bias)
+
+    ordered = dot(split[...], hold[...]).astype(BF)
+    return ordered[0:WIN], ordered[WIN : 2 * WIN]
+
+
+def chained_kernel(received, own, split, gains, bias, *rest):
+    *mats, out, hold = rest
+    out[0], out[1] = chained_block(received, own, split, gains, bias, mats, hold)
+
+
+def last_kernel(earlier, received, own, split, gains, bias, *rest):
+    *mats, out, hold = rest
+    core = lax.rem(lax.axis_index("lat"), 2)
+    out[core, 0] = earlier[0]
+    out[1 - core, 0] = earlier[1]
+    mine, theirs = chained_block(received, own, split, gains, bias, mats, hold)
+    out[core, 1] = mine
+    out[1 - core, 1] = theirs
 
 
 def place_kernel(both, out, sems):
@@ -384,19 +400,30 @@
         shape((3, MLP), F32),
     )
     flops = 2 * 576 * 192 * 192 * 14
-    daily, bias, *mats = call(
+    dense = shape((WIN, 2 * C), BF)
+    daily_0, daily_1, bias, *mats = call(
         daily_kernel,
-        (shape((2 * WIN, 2 * C), BF), shape((HEADS, WIN, WIN), F32), *mats),
+        (dense, dense, shape((HEADS, WIN, WIN), F32), *mats),
         (kept, other, pick, pack, gains, turn),
         flops=flops,
     )
-    received = lax.ppermute(daily, "section", [(0, 1)])
+    received_0 = lax.ppermute(daily_0, "section", [(0, 1)])
+    received_1 = lax.ppermute(daily_1, "section", [(0, 1)])
+    hold = [pltpu.VMEM((2 * WIN, C), BF)]
+    shared = (split, gains, bias, *mats)
+    earlier = call(
+        chained_kernel,
+        shape((2, WIN, C), BF),
+        (received_0, daily_0, *shared),
+        hold,
+        flops // 2,
+    )
     states = call(
-        chained_kernel,
+        last_kernel,
         shape((2, 2, WIN, C), BF),
-        (received, daily, split, gains, bias, *mats),
-        [pltpu.VMEM((2, 2 * WIN, C), BF)],
-        flops,
+        (earlier, received_1, daily_1, *shared),
+        hold,
+        flops // 2,
     )
     both = lax.all_gather(states, "lat", axis_index_groups=pairs)
     placed = pl.pallas_call(

time: 40.7 us -> 40.6 us (level)
  waiting for transfers between devices: 11.9 us -> 9.12 us
  starting transfers between devices: 3.88 us -> 5.17 us
  Pallas kernels: 6.51 us -> 7.4 us
  blocking collectives: 18.1 us -> 18.6 us
    ppermute x1 -> x2, waiting for transfers between devices: 11.9 us -> 9.12 us  [the longest x1 9.12 us: on_device(): received_0 = lax.ppermute(daily_0, 'section', [(0, 1)])]
    ppermute x1 -> x2, starting transfers between devices: 1.29 us -> 2.58 us  [the longest x1 1.29 us: on_device(): received_0 = lax.ppermute(daily_0, 'section', [(0, 1)])]
    pallas_call x2 -> x3, Pallas kernels: 4.23 us -> 5.09 us  [call(): pl.pallas_call(kernel, out_shape=out_shape, in_specs=[VMEM] * len(args),...]
    all_gather x1, blocking collectives: 4.57 us -> 5.04 us  [on_device(): both = lax.all_gather(states, 'lat', axis_index_groups=pairs)]
  transfers between devices with their start and end apart: 2 -> 3, of which waited for: 1 -> 1; matrix products, arithmetic and copies ran while one was open for 0% -> 0% of each run, Pallas kernels for 0% -> 5%
where the time goes in v7:
time: 40.6 us; the launch traced here: 40.4 us
  blocking collectives  18.6 us (46%)
  waiting for transfers between devices  9.12 us (22%)
  Pallas kernels  7.4 us (18%)
  starting transfers between devices  5.17 us (13%)
    all_gather x1, blocking collectives, on_device(): pack = lax.all_gather(weights, 'tp')  13.5 us
    ppermute x1, waiting for transfers between devices, on_device(): received_0 = lax.ppermute(daily_0, 'section', [(0, 1)])  9.12 us
    pallas_call x3, Pallas kernels, call(): pl.pallas_call(kernel, out_shape=out_shape, in_specs=[VMEM] * len(args),...  5.09 us
    all_gather x1, blocking collectives, on_device(): both = lax.all_gather(states, 'lat', axis_index_groups=pairs)  5.04 us
    ppermute x1, starting transfers between devices, on_device(): other = lax.ppermute(sent, 'lat', swap)  2.58 us
    pallas_call x1, Pallas kernels, on_device(): pl.pallas_call(load_kernel, out_shape=(shape((304, 384), BF), shape((576,...  1.59 us
    ppermute x1, starting transfers between devices, on_device(): received_0 = lax.ppermute(daily_0, 'section', [(0, 1)])  1.29 us
    ppermute x1, starting transfers between devices, on_device(): received_1 = lax.ppermute(daily_1, 'section', [(0, 1)])  1.29 us
  transfers between devices with their start and end apart: 3, of which 1 were waited for; matrix products, arithmetic and copies ran while one was open for 0% of the time, Pallas kernels for 5%

profile of v7, /device:TPU:5, one launch (start us, length us, event | category | flops | bytes accessed | tf_op | source)
XLA Modules:
  0.0 40.4 jit_solution(3028587739313853559)
XLA Ops:
  0.0 1.6 %shard_map.163 = (bf16[304,384]{1,0:T(8,128)(2,1)S(1)}, bf16[576,256]{1,0:T(8,128)(2,1)S(1)}, bf16[576,256]{1,0:T(8,128)(2,1)S(1)}, f32[4,192]{1,0:T(4,128)S(1)}) custom-call(bf16[1,144,192]{2,1,0:T(8,128)(2,1)} %bitcast.10, bf16[1,48,192]{2,1,0:T(8,128)(2,1)} %bitcast.12, bf16[1,192,192]{2,1,0:T(8,128)(2,1)} %expand.1, bf16[1,192,192]{2,1,0:T(8,128)(2,1)} %reduce.1, ...), custom_call_target="tpu_custom_call" | custom-call | tf_op jit(solution)/shard_map/pallas_call | solution.py:363
  1.6 2.6 %collective-permute-start = (bf16[576,256]{1,0:T(8,128)(2,1)S(1)}, bf16[576,256]{1,0:T(8,128)(2,1)S(1)}, u32[]{:S(2)}, u32[]{:S(2)}) collective-permute-start(bf16[576,256]{1,0:T(8,128)(2,1)S(1)} %get-tuple-element.19), channel_id=1, source_target_pairs={{0,4},{4,0},{8,12},{12,8},{16,20},{20,16},{24,28},{28,24},{32,36},... | collective-permute-start | bytes 884744 | tf_op jit(solution)/shard_map/ppermute | solution.py:392
  4.2 0.0 copy-start.1
  4.2 0.0 copy-start.2
  4.2 13.5 %all-gather = bf16[1216,384]{1,0:T(8,128)(2,1)S(1)} all-gather(bf16[304,384]{1,0:T(8,128)(2,1)S(1)} %get-tuple-element.20), channel_id=2, replica_groups=mesh['section'=2,'lat'=64,'tp'=4] {'tp'}, dimensions={0}, use_global_device_ids=true | all-gather | bytes 1167360 | tf_op jit(solution)/shard_map/all_gather | solution.py:393
  17.8 0.0 collective-permute-done.other
  17.8 0.0 copy-done.1
  17.8 0.0 copy-done.2
  17.8 0.0 copy-start
  17.8 0.7 %shard_map.164 = (bf16[144,384]{1,0:T(8,128)(2,1)S(1)}, bf16[144,384]{1,0:T(8,128)(2,1)S(1)}, f32[6,144,144]{2,1,0:T(8,128)S(1)}, bf16[576,192]{1,0:T(8,128)(2,1...) custom-call(bf16[576,256]{1,0:T(8,128)(2,1)S(1)} %get-tuple-element., ...), custom_call_target="tpu_custom_call" | custom-call | flops 594542592 | bytes 1048576 | tf_op jit(solution)/shard_map/pallas_call | solution.py:313
  18.4 1.3 %collective-permute-start.1 = (bf16[144,384]{1,0:T(8,128)(2,1)S(1)}, bf16[144,384]{1,0:T(8,128)(2,1)S(1)}, u32[]{:S(2)}, u32[]{:S(2)}) collective-permute-start(bf16[144,384]{1,0:T(8,128)(2,1)S(1)} %get-tuple-element.22.own), channel_id=1, source_target_pairs={{0,256},{1,257},{2,258},{3,259},{4,260},{5,261},{6,262},{7,263},{8... | collective-permute-start | bytes 331784 | tf_op jit(solution)/shard_map/ppermute | solution.py:410
  19.7 1.3 %collective-permute-start.2 = (bf16[144,384]{1,0:T(8,128)(2,1)S(1)}, bf16[144,384]{1,0:T(8,128)(2,1)S(1)}, u32[]{:S(2)}, u32[]{:S(2)}) collective-permute-start(bf16[144,384]{1,0:T(8,128)(2,1)S(1)} %get-tuple-element.30.own), channel_id=1, source_target_pairs={{0,256},{1,257},{2,258},{3,259},{4,260},{5,261},{6,262},{7,263},{8... | collective-permute-start | bytes 331784 | tf_op jit(solution)/shard_map/ppermute | solution.py:411
  21.0 9.1 %collective-permute-done.1.received = bf16[144,384]{1,0:T(8,128)(2,1)S(1)} collective-permute-done((bf16[144,384]{1,0:T(8,128)(2,1)S(1)}, bf16[144,384]{1,0:T(8,128)(2,1)S(1)}, u32[]{:S(2)}, u32[]{:S(2)}) %collective-permute-start.1) | collective-permute-done | bytes 110624 | tf_op jit(solution)/shard_map/ppermute | solution.py:410
  30.2 0.0 copy-done
  30.2 2.2 %shard_map.165.earlier = bf16[2,144,192]{2,1,0:T(8,128)(2,1)S(1)} custom-call(bf16[144,384]{1,0:T(8,128)(2,1)S(1)} %collective-permute-done.1.received, bf16[144,384]{1,0:T(8,128)(2,1)S(1)} %get-tuple-element.22.own, bf16[288,288]{1,0:T(8,128)(2,1)S(1)} %copy-done, f32[4,192]{1,0:T(4,128)S(1)} %get-tuple-element.21.gains, ...), custom_call_target="tpu_custom_call" | custom-call | flops 297271296 | bytes 1048576 | tf_op jit(solution)/shard_map/pallas_call | solution.py:313
  32.4 0.0 collective-permute-done.2.received
  32.4 2.2 %shard_map.166 = bf16[2,2,144,192]{3,2,1,0:T(8,128)(2,1)S(1)} custom-call(bf16[2,144,192]{2,1,0:T(8,128)(2,1)S(1)} %shard_map.165.earlier, bf16[144,384]{1,0:T(8,128)(2,1)S(1)} %collective-permute-done.2.received, bf16[144,384]{1,0:T(8,128)(2,1)S(1)} %get-tuple-element.30.own, bf16[288,288]{1,0:T(8,128)(2,1)S(1)} %copy-done, ...), custom_call_target="tpu_custom_call" | custom-call | flops 297271296 | bytes 1048576 | tf_op jit(solution)/shard_map/pallas_call | solution.py:313
  34.6 5.0 %all-gather.1 = bf16[4,2,144,192]{3,2,1,0:T(8,128)(2,1)S(1)} all-gather(bf16[2,2,144,192]{3,2,1,0:T(8,128)(2,1)S(1)} %shard_map.166), channel_id=3, replica_groups={{0,4},{8,12},{16,20},{24,28},{32,36},{40,44},{48,52},{56,60},{64,68},{7..., dimensions={0}, use_global_device_ids=true | all-gather | bytes 663552 | tf_op jit(solution)/shard_map/all_gather | solution.py:428
  39.7 0.7 %shard_map.167 = bf16[12,48,192]{2,1,0:T(8,128)(2,1)} custom-call(bf16[2,2,12,24,192]{4,3,2,1,0:T(8,128)(2,1)S(1)} %bitcast.7), custom_call_target="tpu_custom_call" | custom-call | tf_op jit(solution)/shard_map/pallas_call | solution.py:429
Async XLA Ops:
  1.6 16.2 %collective-permute-start = (bf16[576,256]{1,0:T(8,128)(2,1)S(1)}, bf16[576,256]{1,0:T(8,128)(2,1)S(1)}, u32[]{:S(2)}, u32[]{:S(2)}) collective-permute-start(bf16[576,256]{1,0:T(8,128)(2,1)S(1)} %get-tuple-element.19), channel_id=1, source_target_pairs={{0,4},{4,0},{8,12},{12,8},{16,20},{20,16},{24,28},{28,24},{32,36},... | collective-permute-start | bytes 884744 | tf_op jit(solution)/shard_map/ppermute | solution.py:392
  4.2 13.6 %copy-start.1 = (bf16[2,276,276]{2,1,0:T(8,128)(2,1)S(1)}, bf16[2,276,276]{2,1,0:T(8,128)(2,1)}, u32[]{:S(2)}) copy-start(bf16[2,276,276]{2,1,0:T(8,128)(2,1)} %constant.8.clone.turn) | copy-start | bytes 914116
  4.2 13.6 %copy-start.2 = (bf16[288,288]{1,0:T(8,128)(2,1)S(1)}, bf16[288,288]{1,0:T(8,128)(2,1)}, u32[]{:S(2)}) copy-start(bf16[288,288]{1,0:T(8,128)(2,1)} %constant.6.clone.pick) | copy-start | bytes 497668
  17.8 12.4 %copy-start = (bf16[288,288]{1,0:T(8,128)(2,1)S(1)}, bf16[288,288]{1,0:T(8,128)(2,1)}, u32[]{:S(2)}) copy-start(bf16[288,288]{1,0:T(8,128)(2,1)} %constant.7.clone.split) | copy-start | bytes 497668
  18.4 11.7 %collective-permute-start.1 = (bf16[144,384]{1,0:T(8,128)(2,1)S(1)}, bf16[144,384]{1,0:T(8,128)(2,1)S(1)}, u32[]{:S(2)}, u32[]{:S(2)}) collective-permute-start(bf16[144,384]{1,0:T(8,128)(2,1)S(1)} %get-tuple-element.22.own), channel_id=1, source_target_pairs={{0,256},{1,257},{2,258},{3,259},{4,260},{5,261},{6,262},{7,263},{8... | collective-permute-start | bytes 331784 | tf_op jit(solution)/shard_map/ppermute | solution.py:410
  19.7 12.6 %collective-permute-start.2 = (bf16[144,384]{1,0:T(8,128)(2,1)S(1)}, bf16[144,384]{1,0:T(8,128)(2,1)S(1)}, u32[]{:S(2)}, u32[]{:S(2)}) collective-permute-start(bf16[144,384]{1,0:T(8,128)(2,1)S(1)} %get-tuple-element.30.own), channel_id=1, source_target_pairs={{0,256},{1,257},{2,258},{3,259},{4,260},{5,261},{6,262},{7,263},{8... | collective-permute-start | bytes 331784 | tf_op jit(solution)/shard_map/ppermute | solution.py:411

commit v8 on v7

--- a/solution.py
+++ b/solution.py
@@ -390,7 +390,8 @@
     )(*(pltpu.with_memory_space_constraint(x, pltpu.HBM) for x in operands))
     swap = [(i, i ^ 1) for i in range(lat_count)]
     other = lax.ppermute(sent, "lat", swap)
-    pack = lax.all_gather(weights, "tp")
+    shares = lax.all_gather(weights.reshape(2, 152, 2 * C), "tp", axis=0, tiled=True)
+    pack = shares.reshape(4, 304, 2 * C)
     mats = (
         shape((3 * C, C), BF),
         shape((C, C), BF),

time: 40.6 us -> 40.6 us (level)
  no operation moved by 1% of the time
where the time goes in v8:
time: 40.6 us; the launch traced here: 40.4 us
  blocking collectives  18.6 us (46%)
  waiting for transfers between devices  9.12 us (22%)
  Pallas kernels  7.4 us (18%)
  starting transfers between devices  5.17 us (13%)
    all_gather x1, blocking collectives, on_device(): lax.all_gather(weights.reshape(2, 152, 2 * C), 'tp', axis=0, tiled=True)  13.5 us
    ppermute x1, waiting for transfers between devices, on_device(): received_0 = lax.ppermute(daily_0, 'section', [(0, 1)])  9.12 us
    pallas_call x3, Pallas kernels, call(): pl.pallas_call(kernel, out_shape=out_shape, in_specs=[VMEM] * len(args),...  5.09 us
    all_gather x1, blocking collectives, on_device(): both = lax.all_gather(states, 'lat', axis_index_groups=pairs)  5.04 us
    ppermute x1, starting transfers between devices, on_device(): other = lax.ppermute(sent, 'lat', swap)  2.58 us
    pallas_call x1, Pallas kernels, on_device(): pl.pallas_call(load_kernel, out_shape=(shape((304, 384), BF), shape((576,...  1.59 us
    ppermute x1, starting transfers between devices, on_device(): received_0 = lax.ppermute(daily_0, 'section', [(0, 1)])  1.29 us
    ppermute x1, starting transfers between devices, on_device(): received_1 = lax.ppermute(daily_1, 'section', [(0, 1)])  1.29 us
  transfers between devices with their start and end apart: 3, of which 1 were waited for; matrix products, arithmetic and copies ran while one was open for 0% of the time, Pallas kernels for 5%

profile of v8, /device:TPU:5, one launch (start us, length us, event | category | flops | bytes accessed | tf_op | source)
XLA Modules:
  0.0 40.4 jit_solution(11707562449682206912)
XLA Ops:
  0.0 1.6 %shard_map.163 = (bf16[304,384]{1,0:T(8,128)(2,1)S(1)}, bf16[576,256]{1,0:T(8,128)(2,1)S(1)}, bf16[576,256]{1,0:T(8,128)(2,1)S(1)}, f32[4,192]{1,0:T(4,128)S(1)}) custom-call(bf16[1,144,192]{2,1,0:T(8,128)(2,1)} %bitcast.12, bf16[1,48,192]{2,1,0:T(8,128)(2,1)} %bitcast.14, bf16[1,192,192]{2,1,0:T(8,128)(2,1)} %expand.1, bf16[1,192,192]{2,1,0:T(8,128)(2,1)} %reduce.1, ...), custom_call_target="tpu_custom_call" | custom-call | tf_op jit(solution)/shard_map/pallas_call | solution.py:363
  1.6 2.6 %collective-permute-start = (bf16[576,256]{1,0:T(8,128)(2,1)S(1)}, bf16[576,256]{1,0:T(8,128)(2,1)S(1)}, u32[]{:S(2)}, u32[]{:S(2)}) collective-permute-start(bf16[576,256]{1,0:T(8,128)(2,1)S(1)} %get-tuple-element.19), channel_id=1, source_target_pairs={{0,4},{4,0},{8,12},{12,8},{16,20},{20,16},{24,28},{28,24},{32,36},... | collective-permute-start | bytes 884744 | tf_op jit(solution)/shard_map/ppermute | solution.py:392
  4.2 0.0 copy-start.1
  4.2 0.0 copy-start.2
  4.2 13.5 %all_gather.9 = bf16[8,152,384]{2,1,0:T(8,128)(2,1)S(1)} all-gather(bf16[2,152,384]{2,1,0:T(8,128)(2,1)S(1)} %bitcast.10), channel_id=1, replica_groups=mesh['section'=2,'lat'=64,'tp'=4] {'tp'}, dimensions={0}, use_global_device_ids=true | all-gather | bytes 1167360 | tf_op jit(solution)/shard_map/all_gather | solution.py:393
  17.8 0.0 collective-permute-done.other
  17.8 0.0 copy-done.1
  17.8 0.0 copy-done.2
  17.8 0.0 copy-start
  17.8 0.7 %shard_map.164 = (bf16[144,384]{1,0:T(8,128)(2,1)S(1)}, bf16[144,384]{1,0:T(8,128)(2,1)S(1)}, f32[6,144,144]{2,1,0:T(8,128)S(1)}, bf16[576,192]{1,0:T(8,128)(2,1...) custom-call(bf16[576,256]{1,0:T(8,128)(2,1)S(1)} %get-tuple-element., ...), custom_call_target="tpu_custom_call" | custom-call | flops 594542592 | bytes 1048576 | tf_op jit(solution)/shard_map/pallas_call | solution.py:313
  18.4 1.3 %collective-permute-start.1 = (bf16[144,384]{1,0:T(8,128)(2,1)S(1)}, bf16[144,384]{1,0:T(8,128)(2,1)S(1)}, u32[]{:S(2)}, u32[]{:S(2)}) collective-permute-start(bf16[144,384]{1,0:T(8,128)(2,1)S(1)} %get-tuple-element.22.own), channel_id=1, source_target_pairs={{0,256},{1,257},{2,258},{3,259},{4,260},{5,261},{6,262},{7,263},{8... | collective-permute-start | bytes 331784 | tf_op jit(solution)/shard_map/ppermute | solution.py:411
  19.7 1.3 %collective-permute-start.2 = (bf16[144,384]{1,0:T(8,128)(2,1)S(1)}, bf16[144,384]{1,0:T(8,128)(2,1)S(1)}, u32[]{:S(2)}, u32[]{:S(2)}) collective-permute-start(bf16[144,384]{1,0:T(8,128)(2,1)S(1)} %get-tuple-element.30.own), channel_id=1, source_target_pairs={{0,256},{1,257},{2,258},{3,259},{4,260},{5,261},{6,262},{7,263},{8... | collective-permute-start | bytes 331784 | tf_op jit(solution)/shard_map/ppermute | solution.py:412
  21.0 9.1 %collective-permute-done.1.received = bf16[144,384]{1,0:T(8,128)(2,1)S(1)} collective-permute-done((bf16[144,384]{1,0:T(8,128)(2,1)S(1)}, bf16[144,384]{1,0:T(8,128)(2,1)S(1)}, u32[]{:S(2)}, u32[]{:S(2)}) %collective-permute-start.1) | collective-permute-done | bytes 110624 | tf_op jit(solution)/shard_map/ppermute | solution.py:411
  30.2 0.0 copy-done
  30.2 2.2 %shard_map.165.earlier = bf16[2,144,192]{2,1,0:T(8,128)(2,1)S(1)} custom-call(bf16[144,384]{1,0:T(8,128)(2,1)S(1)} %collective-permute-done.1.received, bf16[144,384]{1,0:T(8,128)(2,1)S(1)} %get-tuple-element.22.own, bf16[288,288]{1,0:T(8,128)(2,1)S(1)} %copy-done, f32[4,192]{1,0:T(4,128)S(1)} %get-tuple-element.21.gains, ...), custom_call_target="tpu_custom_call" | custom-call | flops 297271296 | bytes 1048576 | tf_op jit(solution)/shard_map/pallas_call | solution.py:313
  32.4 0.0 collective-permute-done.2.received
  32.4 2.2 %shard_map.166 = bf16[2,2,144,192]{3,2,1,0:T(8,128)(2,1)S(1)} custom-call(bf16[2,144,192]{2,1,0:T(8,128)(2,1)S(1)} %shard_map.165.earlier, bf16[144,384]{1,0:T(8,128)(2,1)S(1)} %collective-permute-done.2.received, bf16[144,384]{1,0:T(8,128)(2,1)S(1)} %get-tuple-element.30.own, bf16[288,288]{1,0:T(8,128)(2,1)S(1)} %copy-done, ...), custom_call_target="tpu_custom_call" | custom-call | flops 297271296 | bytes 1048576 | tf_op jit(solution)/shard_map/pallas_call | solution.py:313
  34.6 5.0 %all-gather = bf16[4,2,144,192]{3,2,1,0:T(8,128)(2,1)S(1)} all-gather(bf16[2,2,144,192]{3,2,1,0:T(8,128)(2,1)S(1)} %shard_map.166), channel_id=2, replica_groups={{0,4},{8,12},{16,20},{24,28},{32,36},{40,44},{48,52},{56,60},{64,68},{7..., dimensions={0}, use_global_device_ids=true | all-gather | bytes 663552 | tf_op jit(solution)/shard_map/all_gather | solution.py:429
  39.7 0.7 %shard_map.167 = bf16[12,48,192]{2,1,0:T(8,128)(2,1)} custom-call(bf16[2,2,12,24,192]{4,3,2,1,0:T(8,128)(2,1)S(1)} %bitcast.8), custom_call_target="tpu_custom_call" | custom-call | tf_op jit(solution)/shard_map/pallas_call | solution.py:430
Async XLA Ops:
  1.6 16.2 %collective-permute-start = (bf16[576,256]{1,0:T(8,128)(2,1)S(1)}, bf16[576,256]{1,0:T(8,128)(2,1)S(1)}, u32[]{:S(2)}, u32[]{:S(2)}) collective-permute-start(bf16[576,256]{1,0:T(8,128)(2,1)S(1)} %get-tuple-element.19), channel_id=1, source_target_pairs={{0,4},{4,0},{8,12},{12,8},{16,20},{20,16},{24,28},{28,24},{32,36},... | collective-permute-start | bytes 884744 | tf_op jit(solution)/shard_map/ppermute | solution.py:392
  4.2 13.6 %copy-start.1 = (bf16[2,276,276]{2,1,0:T(8,128)(2,1)S(1)}, bf16[2,276,276]{2,1,0:T(8,128)(2,1)}, u32[]{:S(2)}) copy-start(bf16[2,276,276]{2,1,0:T(8,128)(2,1)} %constant.8.clone.turn) | copy-start | bytes 914116
  4.2 13.6 %copy-start.2 = (bf16[288,288]{1,0:T(8,128)(2,1)S(1)}, bf16[288,288]{1,0:T(8,128)(2,1)}, u32[]{:S(2)}) copy-start(bf16[288,288]{1,0:T(8,128)(2,1)} %constant.6.clone.pick) | copy-start | bytes 497668
  17.8 12.4 %copy-start = (bf16[288,288]{1,0:T(8,128)(2,1)S(1)}, bf16[288,288]{1,0:T(8,128)(2,1)}, u32[]{:S(2)}) copy-start(bf16[288,288]{1,0:T(8,128)(2,1)} %constant.7.clone.split) | copy-start | bytes 497668
  18.4 11.7 %collective-permute-start.1 = (bf16[144,384]{1,0:T(8,128)(2,1)S(1)}, bf16[144,384]{1,0:T(8,128)(2,1)S(1)}, u32[]{:S(2)}, u32[]{:S(2)}) collective-permute-start(bf16[144,384]{1,0:T(8,128)(2,1)S(1)} %get-tuple-element.22.own), channel_id=1, source_target_pairs={{0,256},{1,257},{2,258},{3,259},{4,260},{5,261},{6,262},{7,263},{8... | collective-permute-start | bytes 331784 | tf_op jit(solution)/shard_map/ppermute | solution.py:411
  19.7 12.6 %collective-permute-start.2 = (bf16[144,384]{1,0:T(8,128)(2,1)S(1)}, bf16[144,384]{1,0:T(8,128)(2,1)S(1)}, u32[]{:S(2)}, u32[]{:S(2)}) collective-permute-start(bf16[144,384]{1,0:T(8,128)(2,1)S(1)} %get-tuple-element.30.own), channel_id=1, source_target_pairs={{0,256},{1,257},{2,258},{3,259},{4,260},{5,261},{6,262},{7,263},{8... | collective-permute-start | bytes 331784 | tf_op jit(solution)/shard_map/ppermute | solution.py:412

commit v9 on v7

--- a/solution.py
+++ b/solution.py
@@ -72,7 +72,7 @@
     s1,
     g2,
     s2,
-    weights,
+    share,
     kept,
     sent,
     gains_out,
@@ -89,6 +89,7 @@
     table_v,
     gains_v,
     lines,
+    weights,
     sems,
 ):
     core = lax.rem(lax.axis_index("lat"), 2)
@@ -154,6 +155,14 @@
     weights[289:290, 0:48] = reduce_bv[...]
     for i in range(4):
         gains_out[i : i + 1, :] = gains_v[i].astype(F32)
+    share[...] = weights[pl.ds(pl.multiple_of(144 * core, 16), 160), :]
+
+
+def join_kernel(own, first, second, third, out):
+    me = lax.axis_index("tp")
+    out[me] = own[...]
+    for k, ref in ((1, first), (3, second), (2, third)):
+        out[me ^ k] = ref[...]
 
 
 def norm(x, gain, shift):
@@ -173,21 +182,23 @@
 
 def assemble(pack, wqkv, wproj, wexp, wred, bqkv, brow):
     for j in range(4):
-        wqkv[144 * j : 144 * (j + 1), :] = pack[j, 0:144, 0:192]
-        wproj[48 * j : 48 * (j + 1), :] = pack[j, 144:192, 0:192]
-        wexp[:, C * j : C * (j + 1)] = pack[j, 0:192, 192:384]
-        wred[C * j : C * j + 96, :] = pack[j, 192:288, 0:192]
-        wred[C * j + 96 : C * (j + 1), :] = pack[j, 192:288, 192:384]
-        brow[0:1, C * j : C * (j + 1)] = pack[j, 288:289, 192:384].astype(F32)
-        brow[1:2, 48 * j : 48 * (j + 1)] = pack[j, 288:289, 144:192].astype(F32)
-        brow[2:3, 48 * j : 48 * (j + 1)] = pack[j, 289:290, 0:48].astype(F32)
+        low, high = pack.at[0, j], pack.at[1, j]
+        wqkv[144 * j : 144 * (j + 1), :] = low[0:144, 0:C]
+        wproj[48 * j : 48 * (j + 1), :] = high[0:48, 0:C]
+        wexp[0:144, C * j : C * (j + 1)] = low[0:144, C : 2 * C]
+        wexp[144:192, C * j : C * (j + 1)] = high[0:48, C : 2 * C]
+        wred[C * j : C * j + 96, :] = high[48:144, 0:C]
+        wred[C * j + 96 : C * (j + 1), :] = high[48:144, C : 2 * C]
+        brow[0:1, C * j : C * (j + 1)] = high[144:145, C : 2 * C].astype(F32)
+        brow[1:2, 48 * j : 48 * (j + 1)] = high[144:145, 144:192].astype(F32)
+        brow[2:3, 48 * j : 48 * (j + 1)] = high[145:146, 0:48].astype(F32)
         at = 144 * j
         while at < 144 * (j + 1):
             part, inner = divmod(at, C)
             size = min(C - inner, 144 * (j + 1) - at)
             source = at - 144 * j
-            bqkv[part : part + 1, inner : inner + size] = pack[
-                j, 288:289, source : source + size
+            bqkv[part : part + 1, inner : inner + size] = high[
+                144:145, source : source + size
             ].astype(F32)
             at += size
 
@@ -360,10 +371,10 @@
     pick = jnp.asarray(pick_rows())
     split = jnp.asarray(pick_rows().T)
     turn = jnp.asarray(turn_columns())
-    weights, kept, sent, gains = pl.pallas_call(
+    share, kept, sent, gains = pl.pallas_call(
         load_kernel,
         out_shape=(
-            shape((304, 384), BF),
+            shape((160, 2 * C), BF),
             shape((576, 256), BF),
             shape((576, 256), BF),
             shape((4, C), F32),
@@ -384,13 +395,18 @@
             pltpu.VMEM((8, 1656), F32),
             pltpu.VMEM((4, 1, C), BF),
             pltpu.VMEM((4, 48, 128), F32),
+            pltpu.VMEM((304, 2 * C), BF),
             pltpu.SemaphoreType.DMA((20,)),
         ],
         compiler_params=PARAMS,
     )(*(pltpu.with_memory_space_constraint(x, pltpu.HBM) for x in operands))
+    shares = [
+        lax.ppermute(share, "tp", [(i, i ^ k) for i in range(lax.axis_size("tp"))]) for k in (1, 3, 2)
+    ]
     swap = [(i, i ^ 1) for i in range(lat_count)]
     other = lax.ppermute(sent, "lat", swap)
-    pack = lax.all_gather(weights, "tp")
+    joined = call(join_kernel, shape((4, 160, 2 * C), BF), (share, *shares))
+    pack = lax.all_gather(joined, "lat", axis_index_groups=pairs)
     mats = (
         shape((3 * C, C), BF),
         shape((C, C), BF),

time: 40.6 us -> 39.8 us (0.980)
  the two profiles are of different devices: /device:TPU:5 before, /device:TPU:13 now
where the time goes in v9:
time: 39.8 us; the launch traced here: 39.5 us
  starting transfers between devices  15.6 us (39%)
  waiting for transfers between devices  10 us (25%)
  Pallas kernels  7.47 us (19%)
  blocking collectives  6.28 us (16%)
    ppermute x1, waiting for transfers between devices, on_device(): received_0 = lax.ppermute(daily_0, 'section', [(0, 1)])  9.83 us
    ppermute x3, starting transfers between devices, on_device(): lax.ppermute(share, 'tp', [(i, i ^ k) for i in range(lax.axis_size('tp'))])  9.58 us
    pallas_call x4, Pallas kernels, call(): pl.pallas_call(kernel, out_shape=out_shape, in_specs=[VMEM] * len(args),...  5.14 us
    ppermute x1, starting transfers between devices, on_device(): other = lax.ppermute(sent, 'lat', swap)  3.42 us
    all_gather x1, blocking collectives, on_device(): pack = lax.all_gather(joined, 'lat', axis_index_groups=pairs)  3.16 us
    all_gather x1, blocking collectives, on_device(): both = lax.all_gather(states, 'lat', axis_index_groups=pairs)  3.13 us
    pallas_call x1, Pallas kernels, on_device(): pl.pallas_call(load_kernel, out_shape=(shape((160, 2 * C), BF), shape((57...  1.6 us
    ppermute x1, starting transfers between devices, on_device(): received_0 = lax.ppermute(daily_0, 'section', [(0, 1)])  1.29 us
  transfers between devices with their start and end apart: 6, of which 2 were waited for; matrix products, arithmetic and copies ran while one was open for 0% of the time, Pallas kernels for 6%

profile of v9, /device:TPU:13, one launch (start us, length us, event | category | flops | bytes accessed | tf_op | source)
XLA Modules:
  0.0 39.5 jit_solution(153438894019525692)
XLA Ops:
  0.0 1.6 %shard_map.163 = (bf16[160,384]{1,0:T(8,128)(2,1)S(1)}, bf16[576,256]{1,0:T(8,128)(2,1)S(1)}, bf16[576,256]{1,0:T(8,128)(2,1)S(1)}, f32[4,192]{1,0:T(4,128)S(1)}) custom-call(bf16[1,144,192]{2,1,0:T(8,128)(2,1)} %bitcast.10, bf16[1,48,192]{2,1,0:T(8,128)(2,1)} %bitcast.12, bf16[1,192,192]{2,1,0:T(8,128)(2,1)} %expand.1, bf16[1,192,192]{2,1,0:T(8,128)(2,1)} %reduce.1, ...), custom_call_target="tpu_custom_call" | custom-call | tf_op jit(solution)/shard_map/pallas_call | solution.py:374
  1.6 3.9 %collective-permute-start.3 = (bf16[160,384]{1,0:T(8,128)(2,1)S(1)}, bf16[160,384]{1,0:T(8,128)(2,1)S(1)}, u32[]{:S(2)}, u32[]{:S(2)}) collective-permute-start(bf16[160,384]{1,0:T(8,128)(2,1)S(1)} %get-tuple-element.20.own), channel_id=1, source_target_pairs={{0,2},{1,3},{2,0},{3,1},{4,6},{5,7},{6,4},{7,5},{8,10},{9,11},{10,... | collective-permute-start | bytes 368648 | tf_op jit(solution)/shard_map/ppermute | solution.py:404
  5.5 1.9 %collective-permute-start.2 = (bf16[160,384]{1,0:T(8,128)(2,1)S(1)}, bf16[160,384]{1,0:T(8,128)(2,1)S(1)}, u32[]{:S(2)}, u32[]{:S(2)}) collective-permute-start(bf16[160,384]{1,0:T(8,128)(2,1)S(1)} %get-tuple-element.20.own), channel_id=1, source_target_pairs={{0,3},{1,2},{2,1},{3,0},{4,7},{5,6},{6,5},{7,4},{8,11},{9,10},{10,... | collective-permute-start | bytes 368648 | tf_op jit(solution)/shard_map/ppermute | solution.py:404
  7.5 3.7 %collective-permute-start.1 = (bf16[160,384]{1,0:T(8,128)(2,1)S(1)}, bf16[160,384]{1,0:T(8,128)(2,1)S(1)}, u32[]{:S(2)}, u32[]{:S(2)}) collective-permute-start(bf16[160,384]{1,0:T(8,128)(2,1)S(1)} %get-tuple-element.20.own), channel_id=1, source_target_pairs={{0,1},{1,0},{2,3},{3,2},{4,5},{5,4},{6,7},{7,6},{8,9},{9,8},{10,11... | collective-permute-start | bytes 368648 | tf_op jit(solution)/shard_map/ppermute | solution.py:404
  11.2 3.4 %collective-permute-start = (bf16[576,256]{1,0:T(8,128)(2,1)S(1)}, bf16[576,256]{1,0:T(8,128)(2,1)S(1)}, u32[]{:S(2)}, u32[]{:S(2)}) collective-permute-start(bf16[576,256]{1,0:T(8,128)(2,1)S(1)} %get-tuple-element.19), channel_id=1, source_target_pairs={{0,4},{4,0},{8,12},{12,8},{16,20},{20,16},{24,28},{28,24},{32,36},... | collective-permute-start | bytes 884744 | tf_op jit(solution)/shard_map/ppermute | solution.py:407
  14.6 0.0 collective-permute-done.3.third
  14.6 0.0 collective-permute-done.2.second
  14.7 0.0 collective-permute-done.1.first
  14.7 0.1 shard_map.164
  14.7 0.0 copy-start.1
  14.7 0.0 copy-start.2
  14.8 3.2 %all-gather = bf16[8,160,384]{2,1,0:T(8,128)(2,1)S(1)} all-gather(bf16[4,160,384]{2,1,0:T(8,128)(2,1)S(1)} %shard_map.164), channel_id=2, replica_groups={{0,4},{8,12},{16,20},{24,28},{32,36},{40,44},{48,52},{56,60},{64,68},{7..., dimensions={0}, use_global_device_ids=true | all-gather | bytes 1474560 | tf_op jit(solution)/shard_map/all_gather | solution.py:409
  17.9 0.0 collective-permute-done.other
  17.9 0.0 copy-done.1
  17.9 0.0 copy-done.2
  17.9 0.7 %shard_map.165 = (bf16[144,384]{1,0:T(8,128)(2,1)S(1)}, bf16[144,384]{1,0:T(8,128)(2,1)S(1)}, f32[6,144,144]{2,1,0:T(8,128)S(1)}, bf16[576,192]{1,0:T(8,128)(2,1...) custom-call(bf16[576,256]{1,0:T(8,128)(2,1)S(1)} %get-tuple-element., ...), custom_call_target="tpu_custom_call" | custom-call | flops 594542592 | bytes 1048576 | tf_op jit(solution)/shard_map/pallas_call | solution.py:324
  18.6 1.3 %collective-permute-start.4 = (bf16[144,384]{1,0:T(8,128)(2,1)S(1)}, bf16[144,384]{1,0:T(8,128)(2,1)S(1)}, u32[]{:S(2)}, u32[]{:S(2)}) collective-permute-start(bf16[144,384]{1,0:T(8,128)(2,1)S(1)} %get-tuple-element.22.own), channel_id=1, source_target_pairs={{0,256},{1,257},{2,258},{3,259},{4,260},{5,261},{6,262},{7,263},{8... | collective-permute-start | bytes 331784 | tf_op jit(solution)/shard_map/ppermute | solution.py:426
  19.9 1.3 %collective-permute-start.5 = (bf16[144,384]{1,0:T(8,128)(2,1)S(1)}, bf16[144,384]{1,0:T(8,128)(2,1)S(1)}, u32[]{:S(2)}, u32[]{:S(2)}) collective-permute-start(bf16[144,384]{1,0:T(8,128)(2,1)S(1)} %get-tuple-element.30.own), channel_id=1, source_target_pairs={{0,256},{1,257},{2,258},{3,259},{4,260},{5,261},{6,262},{7,263},{8... | collective-permute-start | bytes 331784 | tf_op jit(solution)/shard_map/ppermute | solution.py:427
  21.2 9.8 %collective-permute-done.4.received = bf16[144,384]{1,0:T(8,128)(2,1)S(1)} collective-permute-done((bf16[144,384]{1,0:T(8,128)(2,1)S(1)}, bf16[144,384]{1,0:T(8,128)(2,1)S(1)}, u32[]{:S(2)}, u32[]{:S(2)}) %collective-permute-start.4) | collective-permute-done | bytes 110624 | tf_op jit(solution)/shard_map/ppermute | solution.py:426
  31.0 2.2 %shard_map.166.earlier = bf16[2,144,192]{2,1,0:T(8,128)(2,1)S(1)} custom-call(bf16[144,384]{1,0:T(8,128)(2,1)S(1)} %collective-permute-done.4.received, bf16[144,384]{1,0:T(8,128)(2,1)S(1)} %get-tuple-element.22.own, bf16[288,288]{1,0:T(8,128)(2,1)S(1)} %copy-done, f32[4,192]{1,0:T(4,128)S(1)} %get-tuple-element.21.gains, ...), custom_call_target="tpu_custom_call" | custom-call | flops 297271296 | bytes 1048576 | tf_op jit(solution)/shard_map/pallas_call | solution.py:324
  33.2 0.2 collective-permute-done.5.received
  33.4 2.2 %shard_map.167 = bf16[2,2,144,192]{3,2,1,0:T(8,128)(2,1)S(1)} custom-call(bf16[2,144,192]{2,1,0:T(8,128)(2,1)S(1)} %shard_map.166.earlier, bf16[144,384]{1,0:T(8,128)(2,1)S(1)} %collective-permute-done.5.received, bf16[144,384]{1,0:T(8,128)(2,1)S(1)} %get-tuple-element.30.own, bf16[288,288]{1,0:T(8,128)(2,1)S(1)} %copy-done, ...), custom_call_target="tpu_custom_call" | custom-call | flops 297271296 | bytes 1048576 | tf_op jit(solution)/shard_map/pallas_call | solution.py:324
  35.6 3.1 %all-gather.1 = bf16[4,2,144,192]{3,2,1,0:T(8,128)(2,1)S(1)} all-gather(bf16[2,2,144,192]{3,2,1,0:T(8,128)(2,1)S(1)} %shard_map.167), channel_id=3, replica_groups={{0,4},{8,12},{16,20},{24,28},{32,36},{40,44},{48,52},{56,60},{64,68},{7..., dimensions={0}, use_global_device_ids=true | all-gather | bytes 663552 | tf_op jit(solution)/shard_map/all_gather | solution.py:444
  38.8 0.7 %shard_map.168 = bf16[12,48,192]{2,1,0:T(8,128)(2,1)} custom-call(bf16[2,2,12,24,192]{4,3,2,1,0:T(8,128)(2,1)S(1)} %bitcast.8), custom_call_target="tpu_custom_call" | custom-call | tf_op jit(solution)/shard_map/pallas_call | solution.py:445
  (2 shorter events, 0.0 us)
Async XLA Ops:
  1.6 13.0 %collective-permute-start.3 = (bf16[160,384]{1,0:T(8,128)(2,1)S(1)}, bf16[160,384]{1,0:T(8,128)(2,1)S(1)}, u32[]{:S(2)}, u32[]{:S(2)}) collective-permute-start(bf16[160,384]{1,0:T(8,128)(2,1)S(1)} %get-tuple-element.20.own), channel_id=1, source_target_pairs={{0,2},{1,3},{2,0},{3,1},{4,6},{5,7},{6,4},{7,5},{8,10},{9,11},{10,... | collective-permute-start | bytes 368648 | tf_op jit(solution)/shard_map/ppermute | solution.py:404
  5.5 9.1 %collective-permute-start.2 = (bf16[160,384]{1,0:T(8,128)(2,1)S(1)}, bf16[160,384]{1,0:T(8,128)(2,1)S(1)}, u32[]{:S(2)}, u32[]{:S(2)}) collective-permute-start(bf16[160,384]{1,0:T(8,128)(2,1)S(1)} %get-tuple-element.20.own), channel_id=1, source_target_pairs={{0,3},{1,2},{2,1},{3,0},{4,7},{5,6},{6,5},{7,4},{8,11},{9,10},{10,... | collective-permute-start | bytes 368648 | tf_op jit(solution)/shard_map/ppermute | solution.py:404
  7.5 7.2 %collective-permute-start.1 = (bf16[160,384]{1,0:T(8,128)(2,1)S(1)}, bf16[160,384]{1,0:T(8,128)(2,1)S(1)}, u32[]{:S(2)}, u32[]{:S(2)}) collective-permute-start(bf16[160,384]{1,0:T(8,128)(2,1)S(1)} %get-tuple-element.20.own), channel_id=1, source_target_pairs={{0,1},{1,0},{2,3},{3,2},{4,5},{5,4},{6,7},{7,6},{8,9},{9,8},{10,11... | collective-permute-start | bytes 368648 | tf_op jit(solution)/shard_map/ppermute | solution.py:404
  11.2 6.7 %collective-permute-start = (bf16[576,256]{1,0:T(8,128)(2,1)S(1)}, bf16[576,256]{1,0:T(8,128)(2,1)S(1)}, u32[]{:S(2)}, u32[]{:S(2)}) collective-permute-start(bf16[576,256]{1,0:T(8,128)(2,1)S(1)} %get-tuple-element.19), channel_id=1, source_target_pairs={{0,4},{4,0},{8,12},{12,8},{16,20},{20,16},{24,28},{28,24},{32,36},... | collective-permute-start | bytes 884744 | tf_op jit(solution)/shard_map/ppermute | solution.py:407
  14.7 3.2 %copy-start.1 = (bf16[2,276,276]{2,1,0:T(8,128)(2,1)S(1)}, bf16[2,276,276]{2,1,0:T(8,128)(2,1)}, u32[]{:S(2)}) copy-start(bf16[2,276,276]{2,1,0:T(8,128)(2,1)} %constant.8.clone.turn) | copy-start | bytes 914116
  14.7 3.2 %copy-start.2 = (bf16[288,288]{1,0:T(8,128)(2,1)S(1)}, bf16[288,288]{1,0:T(8,128)(2,1)}, u32[]{:S(2)}) copy-start(bf16[288,288]{1,0:T(8,128)(2,1)} %constant.6.clone.pick) | copy-start | bytes 497668
  17.9 13.1 %copy-start = (bf16[288,288]{1,0:T(8,128)(2,1)S(1)}, bf16[288,288]{1,0:T(8,128)(2,1)}, u32[]{:S(2)}) copy-start(bf16[288,288]{1,0:T(8,128)(2,1)} %constant.7.clone.split) | copy-start | bytes 497668
  18.6 12.4 %collective-permute-start.4 = (bf16[144,384]{1,0:T(8,128)(2,1)S(1)}, bf16[144,384]{1,0:T(8,128)(2,1)S(1)}, u32[]{:S(2)}, u32[]{:S(2)}) collective-permute-start(bf16[144,384]{1,0:T(8,128)(2,1)S(1)} %get-tuple-element.22.own), channel_id=1, source_target_pairs={{0,256},{1,257},{2,258},{3,259},{4,260},{5,261},{6,262},{7,263},{8... | collective-permute-start | bytes 331784 | tf_op jit(solution)/shard_map/ppermute | solution.py:426
  19.9 13.5 %collective-permute-start.5 = (bf16[144,384]{1,0:T(8,128)(2,1)S(1)}, bf16[144,384]{1,0:T(8,128)(2,1)S(1)}, u32[]{:S(2)}, u32[]{:S(2)}) collective-permute-start(bf16[144,384]{1,0:T(8,128)(2,1)S(1)} %get-tuple-element.30.own), channel_id=1, source_target_pairs={{0,256},{1,257},{2,258},{3,259},{4,260},{5,261},{6,262},{7,263},{8... | collective-permute-start | bytes 331784 | tf_op jit(solution)/shard_map/ppermute | solution.py:427

commit v10 on v9

--- a/solution.py
+++ b/solution.py
@@ -161,8 +161,8 @@
 def join_kernel(own, first, second, third, out):
     me = lax.axis_index("tp")
     out[me] = own[...]
-    for k, ref in ((1, first), (3, second), (2, third)):
-        out[me ^ k] = ref[...]
+    for k, ref in ((3, first), (1, second), (2, third)):
+        out[lax.rem(me + 4 - k, 4)] = ref[...]
 
 
 def norm(x, gain, shift):
@@ -400,8 +400,9 @@
         ],
         compiler_params=PARAMS,
     )(*(pltpu.with_memory_space_constraint(x, pltpu.HBM) for x in operands))
+    tp_count = lax.axis_size("tp")
     shares = [
-        lax.ppermute(share, "tp", [(i, i ^ k) for i in range(lax.axis_size("tp"))]) for k in (1, 3, 2)
+        lax.ppermute(share, "tp", [(i, (i + k) % tp_count) for i in range(tp_count)]) for k in (3, 1, 2)
     ]
     swap = [(i, i ^ 1) for i in range(lat_count)]
     other = lax.ppermute(sent, "lat", swap)

time: 39.8 us -> 39.8 us (level)
  starting transfers between devices: 15.6 us -> 15.2 us
  waiting for transfers between devices: 10 us -> 10.4 us
where the time goes in v10:
time: 39.8 us; the launch traced here: 39.5 us
  starting transfers between devices  15.2 us (38%)
  waiting for transfers between devices  10.4 us (26%)
  Pallas kernels  7.46 us (19%)
  blocking collectives  6.28 us (16%)
    ppermute x1, waiting for transfers between devices, on_device(): received_0 = lax.ppermute(daily_0, 'section', [(0, 1)])  10.2 us
    ppermute x3, starting transfers between devices, on_device(): lax.ppermute(share, 'tp', [(i, (i + k) % tp_count) for i in range(tp_coun...  9.21 us
    pallas_call x4, Pallas kernels, call(): pl.pallas_call(kernel, out_shape=out_shape, in_specs=[VMEM] * len(args),...  5.14 us
    ppermute x1, starting transfers between devices, on_device(): other = lax.ppermute(sent, 'lat', swap)  3.42 us
    all_gather x1, blocking collectives, on_device(): pack = lax.all_gather(joined, 'lat', axis_index_groups=pairs)  3.16 us
    all_gather x1, blocking collectives, on_device(): both = lax.all_gather(states, 'lat', axis_index_groups=pairs)  3.13 us
    pallas_call x1, Pallas kernels, on_device(): pl.pallas_call(load_kernel, out_shape=(shape((160, 2 * C), BF), shape((57...  1.6 us
    ppermute x1, starting transfers between devices, on_device(): received_0 = lax.ppermute(daily_0, 'section', [(0, 1)])  1.29 us
  transfers between devices with their start and end apart: 6, of which 2 were waited for; matrix products, arithmetic and copies ran while one was open for 0% of the time, Pallas kernels for 6%

profile of v10, /device:TPU:13, one launch (start us, length us, event | category | flops | bytes accessed | tf_op | source)
XLA Modules:
  0.0 39.5 jit_solution(7979179445930454711)
XLA Ops:
  0.0 1.6 %shard_map.163 = (bf16[160,384]{1,0:T(8,128)(2,1)S(1)}, bf16[576,256]{1,0:T(8,128)(2,1)S(1)}, bf16[576,256]{1,0:T(8,128)(2,1)S(1)}, f32[4,192]{1,0:T(4,128)S(1)}) custom-call(bf16[1,144,192]{2,1,0:T(8,128)(2,1)} %bitcast.10, bf16[1,48,192]{2,1,0:T(8,128)(2,1)} %bitcast.12, bf16[1,192,192]{2,1,0:T(8,128)(2,1)} %expand.1, bf16[1,192,192]{2,1,0:T(8,128)(2,1)} %reduce.1, ...), custom_call_target="tpu_custom_call" | custom-call | tf_op jit(solution)/shard_map/pallas_call | solution.py:374
  1.6 3.9 %collective-permute-start.3 = (bf16[160,384]{1,0:T(8,128)(2,1)S(1)}, bf16[160,384]{1,0:T(8,128)(2,1)S(1)}, u32[]{:S(2)}, u32[]{:S(2)}) collective-permute-start(bf16[160,384]{1,0:T(8,128)(2,1)S(1)} %get-tuple-element.20.own), channel_id=1, source_target_pairs={{0,2},{1,3},{2,0},{3,1},{4,6},{5,7},{6,4},{7,5},{8,10},{9,11},{10,... | collective-permute-start | bytes 368648 | tf_op jit(solution)/shard_map/ppermute | solution.py:405
  5.5 1.9 %collective-permute-start.2 = (bf16[160,384]{1,0:T(8,128)(2,1)S(1)}, bf16[160,384]{1,0:T(8,128)(2,1)S(1)}, u32[]{:S(2)}, u32[]{:S(2)}) collective-permute-start(bf16[160,384]{1,0:T(8,128)(2,1)S(1)} %get-tuple-element.20.own), channel_id=1, source_target_pairs={{0,1},{1,2},{2,3},{3,0},{4,5},{5,6},{6,7},{7,4},{8,9},{9,10},{10,1... | collective-permute-start | bytes 368648 | tf_op jit(solution)/shard_map/ppermute | solution.py:405
  7.5 3.4 %collective-permute-start.1 = (bf16[160,384]{1,0:T(8,128)(2,1)S(1)}, bf16[160,384]{1,0:T(8,128)(2,1)S(1)}, u32[]{:S(2)}, u32[]{:S(2)}) collective-permute-start(bf16[160,384]{1,0:T(8,128)(2,1)S(1)} %get-tuple-element.20.own), channel_id=1, source_target_pairs={{0,3},{1,0},{2,1},{3,2},{4,7},{5,4},{6,5},{7,6},{8,11},{9,8},{10,9... | collective-permute-start | bytes 368648 | tf_op jit(solution)/shard_map/ppermute | solution.py:405
  10.8 3.4 %collective-permute-start = (bf16[576,256]{1,0:T(8,128)(2,1)S(1)}, bf16[576,256]{1,0:T(8,128)(2,1)S(1)}, u32[]{:S(2)}, u32[]{:S(2)}) collective-permute-start(bf16[576,256]{1,0:T(8,128)(2,1)S(1)} %get-tuple-element.19), channel_id=1, source_target_pairs={{0,4},{4,0},{8,12},{12,8},{16,20},{20,16},{24,28},{28,24},{32,36},... | collective-permute-start | bytes 884744 | tf_op jit(solution)/shard_map/ppermute | solution.py:408
  14.3 0.0 collective-permute-done.3.third
  14.3 0.0 collective-permute-done.2.second
  14.3 0.0 collective-permute-done.1.first
  14.3 0.1 shard_map.164
  14.4 0.0 copy-start.1
  14.4 0.0 copy-start.2
  14.4 3.2 %all-gather = bf16[8,160,384]{2,1,0:T(8,128)(2,1)S(1)} all-gather(bf16[4,160,384]{2,1,0:T(8,128)(2,1)S(1)} %shard_map.164), channel_id=2, replica_groups={{0,4},{8,12},{16,20},{24,28},{32,36},{40,44},{48,52},{56,60},{64,68},{7..., dimensions={0}, use_global_device_ids=true | all-gather | bytes 1474560 | tf_op jit(solution)/shard_map/all_gather | solution.py:410
  17.5 0.0 collective-permute-done.other
  17.5 0.0 copy-done.2
  17.6 0.7 %shard_map.165 = (bf16[144,384]{1,0:T(8,128)(2,1)S(1)}, bf16[144,384]{1,0:T(8,128)(2,1)S(1)}, f32[6,144,144]{2,1,0:T(8,128)S(1)}, bf16[576,192]{1,0:T(8,128)(2,1...) custom-call(bf16[576,256]{1,0:T(8,128)(2,1)S(1)} %get-tuple-element., ...), custom_call_target="tpu_custom_call" | custom-call | flops 594542592 | bytes 1048576 | tf_op jit(solution)/shard_map/pallas_call | solution.py:324
  18.2 1.3 %collective-permute-start.4 = (bf16[144,384]{1,0:T(8,128)(2,1)S(1)}, bf16[144,384]{1,0:T(8,128)(2,1)S(1)}, u32[]{:S(2)}, u32[]{:S(2)}) collective-permute-start(bf16[144,384]{1,0:T(8,128)(2,1)S(1)} %get-tuple-element.22.own), channel_id=1, source_target_pairs={{0,256},{1,257},{2,258},{3,259},{4,260},{5,261},{6,262},{7,263},{8... | collective-permute-start | bytes 331784 | tf_op jit(solution)/shard_map/ppermute | solution.py:427
  19.5 1.3 %collective-permute-start.5 = (bf16[144,384]{1,0:T(8,128)(2,1)S(1)}, bf16[144,384]{1,0:T(8,128)(2,1)S(1)}, u32[]{:S(2)}, u32[]{:S(2)}) collective-permute-start(bf16[144,384]{1,0:T(8,128)(2,1)S(1)} %get-tuple-element.30.own), channel_id=1, source_target_pairs={{0,256},{1,257},{2,258},{3,259},{4,260},{5,261},{6,262},{7,263},{8... | collective-permute-start | bytes 331784 | tf_op jit(solution)/shard_map/ppermute | solution.py:428
  20.8 10.2 %collective-permute-done.4.received = bf16[144,384]{1,0:T(8,128)(2,1)S(1)} collective-permute-done((bf16[144,384]{1,0:T(8,128)(2,1)S(1)}, bf16[144,384]{1,0:T(8,128)(2,1)S(1)}, u32[]{:S(2)}, u32[]{:S(2)}) %collective-permute-start.4) | collective-permute-done | bytes 110624 | tf_op jit(solution)/shard_map/ppermute | solution.py:427
  31.0 0.0 copy-done
  31.0 2.2 %shard_map.166.earlier = bf16[2,144,192]{2,1,0:T(8,128)(2,1)S(1)} custom-call(bf16[144,384]{1,0:T(8,128)(2,1)S(1)} %collective-permute-done.4.received, bf16[144,384]{1,0:T(8,128)(2,1)S(1)} %get-tuple-element.22.own, bf16[288,288]{1,0:T(8,128)(2,1)S(1)} %copy-done, f32[4,192]{1,0:T(4,128)S(1)} %get-tuple-element.21.gains, ...), custom_call_target="tpu_custom_call" | custom-call | flops 297271296 | bytes 1048576 | tf_op jit(solution)/shard_map/pallas_call | solution.py:324
  33.2 0.2 collective-permute-done.5.received
  33.4 2.2 %shard_map.167 = bf16[2,2,144,192]{3,2,1,0:T(8,128)(2,1)S(1)} custom-call(bf16[2,144,192]{2,1,0:T(8,128)(2,1)S(1)} %shard_map.166.earlier, bf16[144,384]{1,0:T(8,128)(2,1)S(1)} %collective-permute-done.5.received, bf16[144,384]{1,0:T(8,128)(2,1)S(1)} %get-tuple-element.30.own, bf16[288,288]{1,0:T(8,128)(2,1)S(1)} %copy-done, ...), custom_call_target="tpu_custom_call" | custom-call | flops 297271296 | bytes 1048576 | tf_op jit(solution)/shard_map/pallas_call | solution.py:324
  35.6 3.1 %all-gather.1 = bf16[4,2,144,192]{3,2,1,0:T(8,128)(2,1)S(1)} all-gather(bf16[2,2,144,192]{3,2,1,0:T(8,128)(2,1)S(1)} %shard_map.167), channel_id=3, replica_groups={{0,4},{8,12},{16,20},{24,28},{32,36},{40,44},{48,52},{56,60},{64,68},{7..., dimensions={0}, use_global_device_ids=true | all-gather | bytes 663552 | tf_op jit(solution)/shard_map/all_gather | solution.py:445
  38.8 0.7 %shard_map.168 = bf16[12,48,192]{2,1,0:T(8,128)(2,1)} custom-call(bf16[2,2,12,24,192]{4,3,2,1,0:T(8,128)(2,1)S(1)} %bitcast.8), custom_call_target="tpu_custom_call" | custom-call | tf_op jit(solution)/shard_map/pallas_call | solution.py:446
  (2 shorter events, 0.0 us)
Async XLA Ops:
  1.6 12.7 %collective-permute-start.3 = (bf16[160,384]{1,0:T(8,128)(2,1)S(1)}, bf16[160,384]{1,0:T(8,128)(2,1)S(1)}, u32[]{:S(2)}, u32[]{:S(2)}) collective-permute-start(bf16[160,384]{1,0:T(8,128)(2,1)S(1)} %get-tuple-element.20.own), channel_id=1, source_target_pairs={{0,2},{1,3},{2,0},{3,1},{4,6},{5,7},{6,4},{7,5},{8,10},{9,11},{10,... | collective-permute-start | bytes 368648 | tf_op jit(solution)/shard_map/ppermute | solution.py:405
  5.5 8.7 %collective-permute-start.2 = (bf16[160,384]{1,0:T(8,128)(2,1)S(1)}, bf16[160,384]{1,0:T(8,128)(2,1)S(1)}, u32[]{:S(2)}, u32[]{:S(2)}) collective-permute-start(bf16[160,384]{1,0:T(8,128)(2,1)S(1)} %get-tuple-element.20.own), channel_id=1, source_target_pairs={{0,1},{1,2},{2,3},{3,0},{4,5},{5,6},{6,7},{7,4},{8,9},{9,10},{10,1... | collective-permute-start | bytes 368648 | tf_op jit(solution)/shard_map/ppermute | solution.py:405
  7.5 6.8 %collective-permute-start.1 = (bf16[160,384]{1,0:T(8,128)(2,1)S(1)}, bf16[160,384]{1,0:T(8,128)(2,1)S(1)}, u32[]{:S(2)}, u32[]{:S(2)}) collective-permute-start(bf16[160,384]{1,0:T(8,128)(2,1)S(1)} %get-tuple-element.20.own), channel_id=1, source_target_pairs={{0,3},{1,0},{2,1},{3,2},{4,7},{5,4},{6,5},{7,6},{8,11},{9,8},{10,9... | collective-permute-start | bytes 368648 | tf_op jit(solution)/shard_map/ppermute | solution.py:405
  10.8 6.7 %collective-permute-start = (bf16[576,256]{1,0:T(8,128)(2,1)S(1)}, bf16[576,256]{1,0:T(8,128)(2,1)S(1)}, u32[]{:S(2)}, u32[]{:S(2)}) collective-permute-start(bf16[576,256]{1,0:T(8,128)(2,1)S(1)} %get-tuple-element.19), channel_id=1, source_target_pairs={{0,4},{4,0},{8,12},{12,8},{16,20},{20,16},{24,28},{28,24},{32,36},... | collective-permute-start | bytes 884744 | tf_op jit(solution)/shard_map/ppermute | solution.py:408
  14.4 3.2 %copy-start.1 = (bf16[2,276,276]{2,1,0:T(8,128)(2,1)S(1)}, bf16[2,276,276]{2,1,0:T(8,128)(2,1)}, u32[]{:S(2)}) copy-start(bf16[2,276,276]{2,1,0:T(8,128)(2,1)} %constant.8.clone.turn) | copy-start | bytes 914116
  14.4 3.2 %copy-start.2 = (bf16[288,288]{1,0:T(8,128)(2,1)S(1)}, bf16[288,288]{1,0:T(8,128)(2,1)}, u32[]{:S(2)}) copy-start(bf16[288,288]{1,0:T(8,128)(2,1)} %constant.6.clone.pick) | copy-start | bytes 497668
  17.5 13.5 %copy-start = (bf16[288,288]{1,0:T(8,128)(2,1)S(1)}, bf16[288,288]{1,0:T(8,128)(2,1)}, u32[]{:S(2)}) copy-start(bf16[288,288]{1,0:T(8,128)(2,1)} %constant.7.clone.split) | copy-start | bytes 497668
  18.2 12.8 %collective-permute-start.4 = (bf16[144,384]{1,0:T(8,128)(2,1)S(1)}, bf16[144,384]{1,0:T(8,128)(2,1)S(1)}, u32[]{:S(2)}, u32[]{:S(2)}) collective-permute-start(bf16[144,384]{1,0:T(8,128)(2,1)S(1)} %get-tuple-element.22.own), channel_id=1, source_target_pairs={{0,256},{1,257},{2,258},{3,259},{4,260},{5,261},{6,262},{7,263},{8... | collective-permute-start | bytes 331784 | tf_op jit(solution)/shard_map/ppermute | solution.py:427
  19.5 13.9 %collective-permute-start.5 = (bf16[144,384]{1,0:T(8,128)(2,1)S(1)}, bf16[144,384]{1,0:T(8,128)(2,1)S(1)}, u32[]{:S(2)}, u32[]{:S(2)}) collective-permute-start(bf16[144,384]{1,0:T(8,128)(2,1)S(1)} %get-tuple-element.30.own), channel_id=1, source_target_pairs={{0,256},{1,257},{2,258},{3,259},{4,260},{5,261},{6,262},{7,263},{8... | collective-permute-start | bytes 331784 | tf_op jit(solution)/shard_map/ppermute | solution.py:428

commit v11 on v10

--- a/solution.py
+++ b/solution.py
@@ -161,7 +161,7 @@
 def join_kernel(own, first, second, third, out):
     me = lax.axis_index("tp")
     out[me] = own[...]
-    for k, ref in ((3, first), (1, second), (2, third)):
+    for k, ref in ((2, first), (3, second), (1, third)):
         out[lax.rem(me + 4 - k, 4)] = ref[...]
 
 
@@ -402,7 +402,7 @@
     )(*(pltpu.with_memory_space_constraint(x, pltpu.HBM) for x in operands))
     tp_count = lax.axis_size("tp")
     shares = [
-        lax.ppermute(share, "tp", [(i, (i + k) % tp_count) for i in range(tp_count)]) for k in (3, 1, 2)
+        lax.ppermute(share, "tp", [(i, (i + k) % tp_count) for i in range(tp_count)]) for k in (2, 3, 1)
     ]
     swap = [(i, i ^ 1) for i in range(lat_count)]
     other = lax.ppermute(sent, "lat", swap)

time: 39.8 us -> 42.6 us (1.070)
  the two profiles are of different devices: /device:TPU:13 before, /device:TPU:5 now
where the time goes in v11:
time: 42.6 us; the launch traced here: 42.3 us
  starting transfers between devices  16.1 us (38%)
  waiting for transfers between devices  10.9 us (26%)
  blocking collectives  7.7 us (18%)
  Pallas kernels  7.46 us (18%)
    ppermute x1, waiting for transfers between devices, on_device(): received_0 = lax.ppermute(daily_0, 'section', [(0, 1)])  10.6 us
    ppermute x3, starting transfers between devices, on_device(): lax.ppermute(share, 'tp', [(i, (i + k) % tp_count) for i in range(tp_coun...  10.1 us
    pallas_call x4, Pallas kernels, call(): pl.pallas_call(kernel, out_shape=out_shape, in_specs=[VMEM] * len(args),...  5.14 us
    all_gather x1, blocking collectives, on_device(): pack = lax.all_gather(joined, 'lat', axis_index_groups=pairs)  4.58 us
    ppermute x1, starting transfers between devices, on_device(): other = lax.ppermute(sent, 'lat', swap)  3.42 us
    all_gather x1, blocking collectives, on_device(): both = lax.all_gather(states, 'lat', axis_index_groups=pairs)  3.13 us
    pallas_call x1, Pallas kernels, on_device(): pl.pallas_call(load_kernel, out_shape=(shape((160, 2 * C), BF), shape((57...  1.6 us
    ppermute x1, starting transfers between devices, on_device(): received_0 = lax.ppermute(daily_0, 'section', [(0, 1)])  1.29 us
  transfers between devices with their start and end apart: 6, of which 3 were waited for; matrix products, arithmetic and copies ran while one was open for 0% of the time, Pallas kernels for 5%

profile of v11, /device:TPU:5, one launch (start us, length us, event | category | flops | bytes accessed | tf_op | source)
XLA Modules:
  0.0 42.3 jit_solution(3412701078053781650)
XLA Ops:
  0.0 1.6 %shard_map.163 = (bf16[160,384]{1,0:T(8,128)(2,1)S(1)}, bf16[576,256]{1,0:T(8,128)(2,1)S(1)}, bf16[576,256]{1,0:T(8,128)(2,1)S(1)}, f32[4,192]{1,0:T(4,128)S(1)}) custom-call(bf16[1,144,192]{2,1,0:T(8,128)(2,1)} %bitcast.10, bf16[1,48,192]{2,1,0:T(8,128)(2,1)} %bitcast.12, bf16[1,192,192]{2,1,0:T(8,128)(2,1)} %expand.1, bf16[1,192,192]{2,1,0:T(8,128)(2,1)} %reduce.1, ...), custom_call_target="tpu_custom_call" | custom-call | tf_op jit(solution)/shard_map/pallas_call | solution.py:374
  1.6 3.2 %collective-permute-start.3 = (bf16[160,384]{1,0:T(8,128)(2,1)S(1)}, bf16[160,384]{1,0:T(8,128)(2,1)S(1)}, u32[]{:S(2)}, u32[]{:S(2)}) collective-permute-start(bf16[160,384]{1,0:T(8,128)(2,1)S(1)} %get-tuple-element.20.own), channel_id=1, source_target_pairs={{0,1},{1,2},{2,3},{3,0},{4,5},{5,6},{6,7},{7,4},{8,9},{9,10},{10,1... | collective-permute-start | bytes 368648 | tf_op jit(solution)/shard_map/ppermute | solution.py:405
  4.8 3.4 %collective-permute-start.2 = (bf16[160,384]{1,0:T(8,128)(2,1)S(1)}, bf16[160,384]{1,0:T(8,128)(2,1)S(1)}, u32[]{:S(2)}, u32[]{:S(2)}) collective-permute-start(bf16[160,384]{1,0:T(8,128)(2,1)S(1)} %get-tuple-element.20.own), channel_id=1, source_target_pairs={{0,3},{1,0},{2,1},{3,2},{4,7},{5,4},{6,5},{7,6},{8,11},{9,8},{10,9... | collective-permute-start | bytes 368648 | tf_op jit(solution)/shard_map/ppermute | solution.py:405
  8.2 3.5 %collective-permute-start.1 = (bf16[160,384]{1,0:T(8,128)(2,1)S(1)}, bf16[160,384]{1,0:T(8,128)(2,1)S(1)}, u32[]{:S(2)}, u32[]{:S(2)}) collective-permute-start(bf16[160,384]{1,0:T(8,128)(2,1)S(1)} %get-tuple-element.20.own), channel_id=1, source_target_pairs={{0,2},{1,3},{2,0},{3,1},{4,6},{5,7},{6,4},{7,5},{8,10},{9,11},{10,... | collective-permute-start | bytes 368648 | tf_op jit(solution)/shard_map/ppermute | solution.py:405
  11.7 3.4 %collective-permute-start = (bf16[576,256]{1,0:T(8,128)(2,1)S(1)}, bf16[576,256]{1,0:T(8,128)(2,1)S(1)}, u32[]{:S(2)}, u32[]{:S(2)}) collective-permute-start(bf16[576,256]{1,0:T(8,128)(2,1)S(1)} %get-tuple-element.19), channel_id=1, source_target_pairs={{0,4},{4,0},{8,12},{12,8},{16,20},{20,16},{24,28},{28,24},{32,36},... | collective-permute-start | bytes 884744 | tf_op jit(solution)/shard_map/ppermute | solution.py:408
  15.2 0.0 collective-permute-done.3.third
  15.2 0.0 collective-permute-done.2.second
  15.2 0.1 collective-permute-done.1.first
  15.3 0.1 shard_map.164
  15.4 0.0 copy-start.1
  15.4 0.0 copy-start.2
  15.4 4.6 %all-gather = bf16[8,160,384]{2,1,0:T(8,128)(2,1)S(1)} all-gather(bf16[4,160,384]{2,1,0:T(8,128)(2,1)S(1)} %shard_map.164), channel_id=2, replica_groups={{0,4},{8,12},{16,20},{24,28},{32,36},{40,44},{48,52},{56,60},{64,68},{7..., dimensions={0}, use_global_device_ids=true | all-gather | bytes 1474560 | tf_op jit(solution)/shard_map/all_gather | solution.py:410
  20.0 0.0 collective-permute-done.other
  20.0 0.0 copy-done.2
  20.0 0.7 %shard_map.165 = (bf16[144,384]{1,0:T(8,128)(2,1)S(1)}, bf16[144,384]{1,0:T(8,128)(2,1)S(1)}, f32[6,144,144]{2,1,0:T(8,128)S(1)}, bf16[576,192]{1,0:T(8,128)(2,1...) custom-call(bf16[576,256]{1,0:T(8,128)(2,1)S(1)} %get-tuple-element., ...), custom_call_target="tpu_custom_call" | custom-call | flops 594542592 | bytes 1048576 | tf_op jit(solution)/shard_map/pallas_call | solution.py:324
  20.7 1.3 %collective-permute-start.4 = (bf16[144,384]{1,0:T(8,128)(2,1)S(1)}, bf16[144,384]{1,0:T(8,128)(2,1)S(1)}, u32[]{:S(2)}, u32[]{:S(2)}) collective-permute-start(bf16[144,384]{1,0:T(8,128)(2,1)S(1)} %get-tuple-element.22.own), channel_id=1, source_target_pairs={{0,256},{1,257},{2,258},{3,259},{4,260},{5,261},{6,262},{7,263},{8... | collective-permute-start | bytes 331784 | tf_op jit(solution)/shard_map/ppermute | solution.py:427
  22.0 1.3 %collective-permute-start.5 = (bf16[144,384]{1,0:T(8,128)(2,1)S(1)}, bf16[144,384]{1,0:T(8,128)(2,1)S(1)}, u32[]{:S(2)}, u32[]{:S(2)}) collective-permute-start(bf16[144,384]{1,0:T(8,128)(2,1)S(1)} %get-tuple-element.30.own), channel_id=1, source_target_pairs={{0,256},{1,257},{2,258},{3,259},{4,260},{5,261},{6,262},{7,263},{8... | collective-permute-start | bytes 331784 | tf_op jit(solution)/shard_map/ppermute | solution.py:428
  23.3 10.6 %collective-permute-done.4.received = bf16[144,384]{1,0:T(8,128)(2,1)S(1)} collective-permute-done((bf16[144,384]{1,0:T(8,128)(2,1)S(1)}, bf16[144,384]{1,0:T(8,128)(2,1)S(1)}, u32[]{:S(2)}, u32[]{:S(2)}) %collective-permute-start.4) | collective-permute-done | bytes 110624 | tf_op jit(solution)/shard_map/ppermute | solution.py:427
  33.9 0.0 copy-done
  33.9 2.2 %shard_map.166.earlier = bf16[2,144,192]{2,1,0:T(8,128)(2,1)S(1)} custom-call(bf16[144,384]{1,0:T(8,128)(2,1)S(1)} %collective-permute-done.4.received, bf16[144,384]{1,0:T(8,128)(2,1)S(1)} %get-tuple-element.22.own, bf16[288,288]{1,0:T(8,128)(2,1)S(1)} %copy-done, f32[4,192]{1,0:T(4,128)S(1)} %get-tuple-element.21.gains, ...), custom_call_target="tpu_custom_call" | custom-call | flops 297271296 | bytes 1048576 | tf_op jit(solution)/shard_map/pallas_call | solution.py:324
  36.1 0.2 collective-permute-done.5.received
  36.2 2.2 %shard_map.167 = bf16[2,2,144,192]{3,2,1,0:T(8,128)(2,1)S(1)} custom-call(bf16[2,144,192]{2,1,0:T(8,128)(2,1)S(1)} %shard_map.166.earlier, bf16[144,384]{1,0:T(8,128)(2,1)S(1)} %collective-permute-done.5.received, bf16[144,384]{1,0:T(8,128)(2,1)S(1)} %get-tuple-element.30.own, bf16[288,288]{1,0:T(8,128)(2,1)S(1)} %copy-done, ...), custom_call_target="tpu_custom_call" | custom-call | flops 297271296 | bytes 1048576 | tf_op jit(solution)/shard_map/pallas_call | solution.py:324
  38.5 3.1 %all-gather.1 = bf16[4,2,144,192]{3,2,1,0:T(8,128)(2,1)S(1)} all-gather(bf16[2,2,144,192]{3,2,1,0:T(8,128)(2,1)S(1)} %shard_map.167), channel_id=3, replica_groups={{0,4},{8,12},{16,20},{24,28},{32,36},{40,44},{48,52},{56,60},{64,68},{7..., dimensions={0}, use_global_device_ids=true | all-gather | bytes 663552 | tf_op jit(solution)/shard_map/all_gather | solution.py:445
  41.6 0.7 %shard_map.168 = bf16[12,48,192]{2,1,0:T(8,128)(2,1)} custom-call(bf16[2,2,12,24,192]{4,3,2,1,0:T(8,128)(2,1)S(1)} %bitcast.8), custom_call_target="tpu_custom_call" | custom-call | tf_op jit(solution)/shard_map/pallas_call | solution.py:446
  (2 shorter events, 0.0 us)
Async XLA Ops:
  1.6 13.6 %collective-permute-start.3 = (bf16[160,384]{1,0:T(8,128)(2,1)S(1)}, bf16[160,384]{1,0:T(8,128)(2,1)S(1)}, u32[]{:S(2)}, u32[]{:S(2)}) collective-permute-start(bf16[160,384]{1,0:T(8,128)(2,1)S(1)} %get-tuple-element.20.own), channel_id=1, source_target_pairs={{0,1},{1,2},{2,3},{3,0},{4,5},{5,6},{6,7},{7,4},{8,9},{9,10},{10,1... | collective-permute-start | bytes 368648 | tf_op jit(solution)/shard_map/ppermute | solution.py:405
  4.8 10.4 %collective-permute-start.2 = (bf16[160,384]{1,0:T(8,128)(2,1)S(1)}, bf16[160,384]{1,0:T(8,128)(2,1)S(1)}, u32[]{:S(2)}, u32[]{:S(2)}) collective-permute-start(bf16[160,384]{1,0:T(8,128)(2,1)S(1)} %get-tuple-element.20.own), channel_id=1, source_target_pairs={{0,3},{1,0},{2,1},{3,2},{4,7},{5,4},{6,5},{7,6},{8,11},{9,8},{10,9... | collective-permute-start | bytes 368648 | tf_op jit(solution)/shard_map/ppermute | solution.py:405
  8.2 7.1 %collective-permute-start.1 = (bf16[160,384]{1,0:T(8,128)(2,1)S(1)}, bf16[160,384]{1,0:T(8,128)(2,1)S(1)}, u32[]{:S(2)}, u32[]{:S(2)}) collective-permute-start(bf16[160,384]{1,0:T(8,128)(2,1)S(1)} %get-tuple-element.20.own), channel_id=1, source_target_pairs={{0,2},{1,3},{2,0},{3,1},{4,6},{5,7},{6,4},{7,5},{8,10},{9,11},{10,... | collective-permute-start | bytes 368648 | tf_op jit(solution)/shard_map/ppermute | solution.py:405
  11.7 8.2 %collective-permute-start = (bf16[576,256]{1,0:T(8,128)(2,1)S(1)}, bf16[576,256]{1,0:T(8,128)(2,1)S(1)}, u32[]{:S(2)}, u32[]{:S(2)}) collective-permute-start(bf16[576,256]{1,0:T(8,128)(2,1)S(1)} %get-tuple-element.19), channel_id=1, source_target_pairs={{0,4},{4,0},{8,12},{12,8},{16,20},{20,16},{24,28},{28,24},{32,36},... | collective-permute-start | bytes 884744 | tf_op jit(solution)/shard_map/ppermute | solution.py:408
  15.4 4.6 %copy-start.1 = (bf16[2,276,276]{2,1,0:T(8,128)(2,1)S(1)}, bf16[2,276,276]{2,1,0:T(8,128)(2,1)}, u32[]{:S(2)}) copy-start(bf16[2,276,276]{2,1,0:T(8,128)(2,1)} %constant.8.clone.turn) | copy-start | bytes 914116
  15.4 4.6 %copy-start.2 = (bf16[288,288]{1,0:T(8,128)(2,1)S(1)}, bf16[288,288]{1,0:T(8,128)(2,1)}, u32[]{:S(2)}) copy-start(bf16[288,288]{1,0:T(8,128)(2,1)} %constant.6.clone.pick) | copy-start | bytes 497668
  20.0 13.9 %copy-start = (bf16[288,288]{1,0:T(8,128)(2,1)S(1)}, bf16[288,288]{1,0:T(8,128)(2,1)}, u32[]{:S(2)}) copy-start(bf16[288,288]{1,0:T(8,128)(2,1)} %constant.7.clone.split) | copy-start | bytes 497668
  20.7 13.2 %collective-permute-start.4 = (bf16[144,384]{1,0:T(8,128)(2,1)S(1)}, bf16[144,384]{1,0:T(8,128)(2,1)S(1)}, u32[]{:S(2)}, u32[]{:S(2)}) collective-permute-start(bf16[144,384]{1,0:T(8,128)(2,1)S(1)} %get-tuple-element.22.own), channel_id=1, source_target_pairs={{0,256},{1,257},{2,258},{3,259},{4,260},{5,261},{6,262},{7,263},{8... | collective-permute-start | bytes 331784 | tf_op jit(solution)/shard_map/ppermute | solution.py:427
  22.0 14.3 %collective-permute-start.5 = (bf16[144,384]{1,0:T(8,128)(2,1)S(1)}, bf16[144,384]{1,0:T(8,128)(2,1)S(1)}, u32[]{:S(2)}, u32[]{:S(2)}) collective-permute-start(bf16[144,384]{1,0:T(8,128)(2,1)S(1)} %get-tuple-element.30.own), channel_id=1, source_target_pairs={{0,256},{1,257},{2,258},{3,259},{4,260},{5,261},{6,262},{7,263},{8... | collective-permute-start | bytes 331784 | tf_op jit(solution)/shard_map/ppermute | solution.py:428
